TPU v7x, 512 devices: a whole 4x8x8 slice. The times are simulated.
512 devices in a mesh: leaf: 8 (over y), row: 8 (over z), col: 8 (over x, core).
Axes of the slice: x: 4, y: 8, z: 8, core: 2. Of those that a mesh axis runs over, the one named last changes fastest.
Arguments:
- child_front: float32 [8, 4096, 4096], P('leaf', 'row', 'col'), may hold values from -2 to 4, as said below
- parent_front: float32 [8192, 1, 64, 128], P('row', None, ('leaf', 'col')), may hold values from -2 to 4, as said below
- block_map: int32 [8, 30], replicated, may hold values from 0 to 63, as said below
Outputs:
- child_factor: float32 [8, 4096, 256], P('leaf', 'row')
- parent_out: float32 [8192, 1, 64, 128], P('row', None, ('leaf', 'col'))
Inputs may be any that keep to these rules, and one draw needn't show every extreme that they name: `child_front`: each child front is symmetric positive definite, with smallest eigenvalue above 0.1. `parent_front`: viewed as a 8192 x 8192 matrix, the parent front is symmetric positive definite, with smallest eigenvalue above 0.1. `block_map`: row c lists, in order, the parent block that receives each of the 30 trailing blocks of child front c; the entries of a row are distinct parent blocks. Put 2 empty blocks in front of a row and cut it into aligned groups of 4: in every group at most 1 entries share the value of entry // 8, and at most 1 share the value of entry modulo 8; both bounds are reached.
All inputs are finite; a program needn't handle non-finite values.
Results may differ from a plain program's by a relative error of at most 0.0001.
Values sent between devices are 32-bit elements; how exact they have to be, the bound alone decides.
No kernel may reach another device: no remote copies, remote signals or barrier semaphores. Data moves between devices by JAX's collectives and lax.ppermute only.
A program may use at most 64 MiB of HBM per device.

v0:
```python
import jax
import jax.numpy as jnp
from jax import lax
from jax.sharding import Mesh
from jax.sharding import PartitionSpec as P

FP = 8192
PANEL = 256
BLOCK = 128
COL = ("col_0", "col_1")
LEAF_COL = ("leaf", "col_0", "col_1")


def picked(value, axis, root):
    return lax.dynamic_index_in_dim(lax.all_gather(value, axis), root, 0, keepdims=False)


def broadcast_by_axis(value, axes, root):
    value = jnp.where(lax.axis_index(axes) == root, value, jnp.zeros_like(value))
    for axis in axes:
        value = lax.psum(value, axis)
    return value


def matmul(left, right):
    return jnp.dot(left, right, precision=lax.Precision.HIGHEST, preferred_element_type=jnp.float32)


def contract(form, left, right):
    return jnp.einsum(
        form, left, right, precision=lax.Precision.HIGHEST, preferred_element_type=jnp.float32
    )


def lower_inverse(corner):
    lower_factor = jnp.linalg.cholesky(corner)
    identity = jnp.eye(corner.shape[0], dtype=jnp.float32)
    return jax.scipy.linalg.solve_triangular(lower_factor, identity, lower=True)


def slot_ranks(targets, usable):
    count = targets.shape[-1]
    same = (
        (targets[..., :, None] == targets[..., None, :])
        & usable[..., :, None]
        & usable[..., None, :]
    )
    before = jnp.arange(count)[None, :] < jnp.arange(count)[:, None]
    return jnp.sum(same & before, axis=-1)


def pick_send(targets, ranks, usable, count, capacity):
    destination = jnp.arange(count)[:, None, None]
    slot_index = jnp.arange(capacity)[None, :, None]
    chosen = (
        (targets[None, None, :] == destination)
        & (ranks[None, None, :] == slot_index)
        & usable[None, None, :]
    )
    return chosen.astype(jnp.float32)


def column_regroup(
    col_target, col_rank, usable, maps, col_id, capacity, leaves, grid_cols, kblocks, period
):
    leaf_of = maps % period // grid_cols
    slot_of = maps // period
    arrived = (col_target == col_id) & usable
    chosen = arrived[None, None, :, None, :]
    chosen = chosen & (
        col_rank[None, None, :, None, :] == jnp.arange(capacity)[None, None, None, :, None]
    )
    chosen = chosen & (
        leaf_of[None, None, :, None, :] == jnp.arange(leaves)[:, None, None, None, None]
    )
    chosen = chosen & (
        slot_of[None, None, :, None, :] == jnp.arange(kblocks)[None, :, None, None, None]
    )
    return jnp.sum(chosen.astype(jnp.float32), axis=-1)


def per_device(child_front, parent_front, block_map):
    front_local = child_front[0]
    grid_rows = lax.axis_size("row")
    grid_cols = lax.axis_size(COL)
    leaves = lax.axis_size("leaf")
    row_id = lax.axis_index("row")
    col_id = lax.axis_index(COL)
    leaf_id = lax.axis_index("leaf")
    local_rows = front_local.shape[0]
    child_blocks = local_rows // BLOCK
    capacity = max(1, child_blocks // grid_rows)
    parent_blocks = FP // BLOCK
    per_row = parent_blocks // grid_rows
    period = leaves * grid_cols
    kblocks = parent_blocks // period
    parent_rows = per_row * BLOCK
    lead = PANEL // BLOCK
    top_rows = picked(front_local[:PANEL, :], "row", 0)
    panel_rows, corner = (
        picked(front_local[:, :PANEL], COL, 0),
        picked(top_rows[:, :PANEL], COL, 0),
    )
    inverse = lower_inverse(corner)
    factor = matmul(panel_rows, inverse.T)
    schur = front_local - matmul(factor, matmul(inverse, top_rows))
    padded = jnp.concatenate([jnp.full((leaves, lead), -1, jnp.int32), block_map], axis=1)
    all_maps = padded.reshape(leaves, grid_rows, child_blocks)
    all_usable = all_maps >= 0
    own_maps = lax.dynamic_index_in_dim(all_maps, leaf_id, 0, keepdims=False)
    own_usable = own_maps >= 0
    col_target = jnp.where(own_usable, own_maps % grid_cols, -1)
    col_rank = slot_ranks(col_target, own_usable)
    col_send = pick_send(
        lax.dynamic_index_in_dim(col_target, col_id, 0, keepdims=False),
        lax.dynamic_index_in_dim(col_rank, col_id, 0, keepdims=False),
        lax.dynamic_index_in_dim(own_usable, col_id, 0, keepdims=False),
        grid_cols,
        capacity,
    )
    regroup = column_regroup(
        col_target,
        col_rank,
        own_usable,
        own_maps,
        col_id,
        capacity,
        leaves,
        grid_cols,
        kblocks,
        period,
    )
    column_out = contract("dks,rsb->dkrb", col_send, schur.reshape(local_rows, child_blocks, BLOCK))
    column_in = lax.all_to_all(column_out, COL, split_axis=0, concat_axis=0, tiled=True)
    leaf_out = contract("lmnk,nkrb->lrmb", regroup, column_in)
    leaf_in = lax.all_to_all(leaf_out, "leaf", split_axis=0, concat_axis=0, tiled=True)
    all_target = jnp.where(all_usable, all_maps // per_row, -1)
    all_rank = slot_ranks(all_target, all_usable)
    mine_target = lax.dynamic_index_in_dim(all_target, row_id, 1, keepdims=False)
    mine_rank = lax.dynamic_index_in_dim(all_rank, row_id, 1, keepdims=False)
    mine_usable = lax.dynamic_index_in_dim(all_usable, row_id, 1, keepdims=False)
    row_pick = mine_target[None, :, None, :] == jnp.arange(grid_rows)[:, None, None, None]
    row_pick = row_pick & (mine_rank[None, :, None, :] == jnp.arange(capacity)[None, None, :, None])
    row_pick = (row_pick & mine_usable[None, :, None, :]).astype(jnp.float32)
    row_blocks = leaf_in.reshape(leaves, child_blocks, BLOCK, kblocks, BLOCK)
    row_out = contract("dcks,csbmt->dckbmt", row_pick, row_blocks)
    row_in = lax.all_to_all(row_out, "row", split_axis=0, concat_axis=0, tiled=True)
    placed = ((all_target == row_id) & all_usable)[None, :, :, None, :]
    placed = placed & (
        all_rank[None, :, :, None, :] == jnp.arange(capacity)[None, None, None, :, None]
    )
    placed = placed & (
        (all_maps % per_row)[None, :, :, None, :] == jnp.arange(per_row)[:, None, None, None, None]
    )
    placement = jnp.sum(placed.astype(jnp.float32), axis=-1)
    contribution = contract("pcnk,nckbmt->pbmt", placement, row_in).reshape(
        parent_rows, kblocks, BLOCK
    )
    assembled = parent_front[:, :, 0, :] + contribution
    top_parent = picked(assembled[:PANEL].reshape(PANEL, kblocks * BLOCK), "row", 0)
    top_blocks = top_parent.reshape(PANEL, kblocks, BLOCK)
    pieces = []
    corners = []
    for block_index in range(lead):
        slot_here = block_index // period
        piece, corner_piece = (
            broadcast_by_axis(assembled[:, slot_here, :], LEAF_COL, block_index % period),
            broadcast_by_axis(top_blocks[:, slot_here, :], LEAF_COL, block_index % period),
        )
        pieces.append(piece)
        corners.append(corner_piece)
    panel_parent = jnp.concatenate(pieces, axis=1)
    corner_parent = jnp.concatenate(corners, axis=1)
    inverse_parent = lower_inverse(corner_parent)
    parent_factor = matmul(panel_parent, inverse_parent.T)
    upper_parent = matmul(inverse_parent, top_parent)
    updated = assembled - matmul(parent_factor, upper_parent).reshape(parent_rows, kblocks, BLOCK)
    global_row = row_id * parent_rows + jnp.arange(parent_rows)
    device_column = leaf_id * grid_cols + col_id
    global_col = (jnp.arange(kblocks)[:, None] * period + device_column) * BLOCK + jnp.arange(
        BLOCK
    )[None, :]
    panel_values = jnp.take(parent_factor, jnp.minimum(global_col, PANEL - 1), axis=1)
    kept = jnp.where((global_row < PANEL)[:, None, None], assembled, updated)
    result = jnp.where((global_col < PANEL)[None, :, :], panel_values, kept)
    return (factor[None], result[:, :, None, :])


def solution(mesh):
    torus = Mesh(
        mesh.devices.reshape(mesh.shape["leaf"], mesh.shape["row"], 4, 2),
        ("leaf", "row", "col_0", "col_1"),
    )
    in_specs = (P("leaf", "row", COL), P("row", None, LEAF_COL, None), P())
    out_specs = (P("leaf", "row", None), P("row", None, LEAF_COL, None))
    return jax.shard_map(
        per_device, mesh=torus, in_specs=in_specs, out_specs=out_specs, check_vma=False
    )
```

profile of v0, /device:TPU:1, one launch (start us, length us, event | category | flops | bytes accessed | tf_op | source)
XLA Modules:
  0.0 686.8 jit_solution(12455523177208063199)
XLA Ops:
  9.2 64.9 %all-gather.8.cloned.1.call-done = f32[8,256,512]{2,1,0:T(8,128)} async-done(((f32[1,256,512]{2,1,0:T(8,128)}), f32[8,256,512]{2,1,0:T(8,128)}) %all-gather.8.cloned.1.call-update) | async-done | bytes 4194320 | tf_op jit(solution)/shard_map/all_gather | solution.py:15
  78.3 27.9 %all-gather.10.cloned.1.call-done = f32[2048,256]{0,1:T(8,128)} async-done(((f32[256,256]{0,1:T(8,128)}), f32[2048,256]{0,1:T(8,128)}) %all-gather.10.cloned.1.call-update) | async-done | bytes 2097168 | tf_op jit(solution)/shard_map/all_gather | solution.py:15
  108.3 11.7 %cholesky.130 = f32[128,128]{1,0:T(8,128)S(1)} custom-call(f32[128,128]{1,0:T(8,128)S(1)} %cholesky.194), custom_call_target="Cholesky" | custom-call | tf_op jit(solution)/shard_map/jit(cholesky)/cholesky | solution.py:36
  120.1 9.8 %custom-call.13 = f32[1,128,128]{1,2,0:T(8,128)S(1)} custom-call(f32[1,128,128]{2,1,0:T(8,128)S(1)} %get-tuple-element.79), custom_call_target="InvertDiagBlocksLowerTriangular" | custom-call | tf_op jit(solution)/shard_map/jit(cholesky)/cholesky | solution.py:36
  130.4 11.7 %cholesky.147 = f32[128,128]{1,0:T(8,128)S(1)} custom-call(f32[128,128]{1,0:T(8,128)S(1)} %convolution_subtract_fusion.5), custom_call_target="Cholesky" | custom-call | tf_op jit(solution)/shard_map/jit(cholesky)/cholesky | solution.py:36
  144.1 4.3 while.4
  148.4 19.7 %custom-call.14 = f32[2,128,128]{1,2,0:T(8,128)S(1)} custom-call(f32[2,128,128]{2,1,0:T(8,128)S(1)} %get-tuple-element.18), custom_call_target="InvertDiagBlocksLowerTriangular" | custom-call | tf_op jit(solution)/shard_map/jit(_solve_triangular)/triangular_solve | solution.py:38
  178.7 3.8 all-to-all-start
  182.5 26.2 %all-to-all-done = f32[8,1,512,128]{3,2,1,0:T(8,128)S(1)} async-done(((f32[8,1,512,128]{3,2,1,0:T(8,128)}), f32[8,1,512,128]{3,2,1,0:T(8,128)S(1)}, u32[]{:S(2)}, u32[]{:S(2)}) %all-to-all-start) | async-done | bytes 2097184 | tf_op jit(solution)/shard_map/all_to_all | solution.py:134
  213.6 6.6 all-to-all-start.1
  221.0 50.8 %all-to-all-done.1 = f32[8,512,1,128]{3,1,2,0:T(8,128)S(1)} async-done(((f32[8,512,1,128]{3,1,2,0:T(8,128)}), f32[8,512,1,128]{3,1,2,0:T(8,128)S(1)}, u32[]{:S(2)}, u32[]{:S(2)}) %all-to-all-start.1) | async-done | bytes 2097184 | tf_op jit(solution)/shard_map/all_to_all | solution.py:136
  271.8 3.3 convolution_bitcast_fusion
  277.8 7.2 %all-to-all-start.2 = ((f32[8,8,1,128,1,128]{5,3,1,2,4,0:T(8,128)}), f32[8,8,1,128,1,128]{5,3,1,2,4,0:T(8,128)}, u32[]{:S(2)}, u32[]{:S(2)}) async-start(f32[8,8,1,128,1,128]{5,3,1,2,4,0:T(8,128)} %copy.190), calls=%async_computation.2 | async-start | bytes 8388608 | tf_op jit(solution)/shard_map/all_to_all | solution.py:147
  285.5 96.4 %all-to-all-done.2 = f32[8,8,1,128,1,128]{5,3,1,2,4,0:T(8,128)} async-done(((f32[8,8,1,128,1,128]{5,3,1,2,4,0:T(8,128)}), f32[8,8,1,128,1,128]{5,3,1,2,4,0:T(8,128)}, u32[]{:S(2)}, u32[]{:S(2)}) %all-to-all-start.2) | async-done | bytes 4194336 | tf_op jit(solution)/shard_map/all_to_all | solution.py:147
  381.9 11.3 %fusion.11 = f32[8,128,128]{2,0,1:T(8,128)S(1)} fusion(f32[8,8,1,128,1,128]{5,3,1,2,4,0:T(8,128)} %all-to-all-done.2, f32[8,8,8]{2,1,0:T(8,128)S(1)} %convert_reduce_fusion), kind=kOutput, calls=%fused_computation.18 | convolution fusion | flops 100663296 | bytes 4720640 | tf_op jit(solution)/shard_map/pcnk,nckbmt->pbmt/dot_general | solution.py:30
  396.1 24.4 %all-gather.14.cloned.1.call-done = f32[2048,1,128]{0,2,1:T(8,128)} async-done(((f32[256,1,128]{0,2,1:T(8,128)}), f32[2048,1,128]{0,2,1:T(8,128)}) %all-gather.14.cloned.1.call-update) | async-done | bytes 1048592 | tf_op jit(solution)/shard_map/all_gather | solution.py:15
  422.3 83.0 %all-reduce.9.cloned.1.call-done = (f32[1024,128]{1,0:T(8,128)}, f32[1024,128]{1,0:T(8,128)}, f32[256,128]{0,1:T(8,128)}, f32[256,128]{0,1:T(8,128)}) async-done(((f32[1024,128]{1,0:T(8,128)}, f32[1024,128]{1,0:T(8,128)}, f32[256,128]{0,1:T(8,128)}, f32[256,128]{0,1:T(8,128)}), (f32[1024,128]{1,0:T(8,128)}, f32[1024,128]{1,0:T(8,128)}, f32[256,128]{0,1:T(8,128)}, ...) | async-done | bytes 1310736 | tf_op jit(solution)/shard_map/psum | solution.py:21
  505.6 62.5 %all-reduce.11.cloned.1.call-done = (f32[1024,128]{1,0:T(8,128)}, f32[1024,128]{1,0:T(8,128)}, f32[256,128]{0,1:T(8,128)}, f32[256,128]{0,1:T(8,128)}) async-done(((f32[1024,128]{1,0:T(8,128)}, f32[1024,128]{1,0:T(8,128)}, f32[256,128]{0,1:T(8,128)}, f32[256,128]{0,1:T(8,128)}), (f32[1024,128]{1,0:T(8,128)}, f32[1024,128]{1,0:T(8,128)}, f32[256,128]{0,1:T(8,128)}, ...) | async-done | bytes 1310736 | tf_op jit(solution)/shard_map/psum | solution.py:21
  569.1 41.6 %all-reduce.13.cloned.1.call-done = (f32[1024,128]{1,0:T(8,128)}, f32[1024,128]{1,0:T(8,128)}, f32[256,128]{0,1:T(8,128)}, f32[256,128]{0,1:T(8,128)}) async-done(((f32[1024,128]{1,0:T(8,128)}, f32[1024,128]{1,0:T(8,128)}, f32[256,128]{0,1:T(8,128)}, f32[256,128]{0,1:T(8,128)}), (f32[1024,128]{1,0:T(8,128)}, f32[1024,128]{1,0:T(8,128)}, f32[256,128]{0,1:T(8,128)}, ...) | async-done | bytes 1310736 | tf_op jit(solution)/shard_map/psum | solution.py:21
  612.8 11.7 %cholesky.164 = f32[128,128]{1,0:T(8,128)S(1)} custom-call(f32[128,128]{1,0:T(8,128)S(1)} %cholesky.197), custom_call_target="Cholesky" | custom-call | tf_op jit(solution)/shard_map/jit(cholesky)/cholesky | solution.py:36
  624.6 9.8 %custom-call.15 = f32[1,128,128]{1,2,0:T(8,128)S(1)} custom-call(f32[1,128,128]{2,1,0:T(8,128)S(1)} %get-tuple-element.75), custom_call_target="InvertDiagBlocksLowerTriangular" | custom-call | tf_op jit(solution)/shard_map/jit(cholesky)/cholesky | solution.py:36
  634.9 11.7 %cholesky.181 = f32[128,128]{1,0:T(8,128)S(1)} custom-call(f32[128,128]{1,0:T(8,128)S(1)} %convolution_subtract_fusion.4), custom_call_target="Cholesky" | custom-call | tf_op jit(solution)/shard_map/jit(cholesky)/cholesky | solution.py:36
  649.3 4.2 while.5
  653.5 19.7 %custom-call.16 = f32[2,128,128]{1,2,0:T(8,128)S(1)} custom-call(f32[2,128,128]{2,1,0:T(8,128)S(1)} %get-tuple-element.19), custom_call_target="InvertDiagBlocksLowerTriangular" | custom-call | tf_op jit(solution)/shard_map/jit(_solve_triangular)/triangular_solve | solution.py:38
  (127 shorter events, 52.7 us)
Async XLA Ops:
  7.2 69.1 %copy-start = (f32[1,512,512]{2,1,0:T(8,128)S(1)}, f32[1,512,512]{2,1,0:T(8,128)}, u32[]{:S(2)}) copy-start(f32[1,512,512]{2,1,0:T(8,128)} %param.6) | copy-start | bytes 3145732
  7.2 67.0 %all-gather.8.cloned.1.call-start = ((), (), s32[]{:S(2)}) async-start(), calls=%async_computation.3 | async-start | bytes 4718592 | tf_op jit(solution)/shard_map/all_gather | solution.py:15
  9.2 97.0 %all-gather.10.cloned.1.call-start = ((), (), s32[]{:S(2)}) async-start(), calls=%async_computation.4 | async-start | bytes 2359296 | tf_op jit(solution)/shard_map/all_gather | solution.py:15
  76.2 1.3 copy-start.4
  76.2 95.2 %all-gather.12.cloned.1.call-start = ((), (), s32[]{:S(2)}) async-start(), calls=%async_computation.5 | async-start | bytes 4718592 | tf_op jit(solution)/shard_map/all_gather | solution.py:15
  178.7 30.0 %all-to-all-start = ((f32[8,1,512,128]{3,2,1,0:T(8,128)}), f32[8,1,512,128]{3,2,1,0:T(8,128)S(1)}, u32[]{:S(2)}, u32[]{:S(2)}) async-start(f32[8,1,512,128]{3,2,1,0:T(8,128)} %copy.183), calls=%async_computation | async-start | bytes 4194304 | tf_op jit(solution)/shard_map/all_to_all | solution.py:134
  213.6 58.3 %all-to-all-start.1 = ((f32[8,512,1,128]{3,1,2,0:T(8,128)}), f32[8,512,1,128]{3,1,2,0:T(8,128)S(1)}, u32[]{:S(2)}, u32[]{:S(2)}) async-start(f32[8,512,1,128]{3,1,2,0:T(8,128)} %copy.185), calls=%async_computation.1 | async-start | bytes 4194304 | tf_op jit(solution)/shard_map/all_to_all | solution.py:136
  277.8 7.3 %copy-start.1 = (f32[1024,1,1,128]{3,2,1,0:T(1,128)S(1)}, f32[1024,1,1,128]{3,2,1,0:T(1,128)}, u32[]{:S(2)}) copy-start(f32[1024,1,1,128]{3,2,1,0:T(1,128)} %param.7) | copy-start | bytes 1572868
  277.8 104.1 %all-to-all-start.2 = ((f32[8,8,1,128,1,128]{5,3,1,2,4,0:T(8,128)}), f32[8,8,1,128,1,128]{5,3,1,2,4,0:T(8,128)}, u32[]{:S(2)}, u32[]{:S(2)}) async-start(f32[8,8,1,128,1,128]{5,3,1,2,4,0:T(8,128)} %copy.190), calls=%async_computation.2 | async-start | bytes 8388608 | tf_op jit(solution)/shard_map/all_to_all | solution.py:147
  285.0 135.5 %all-gather.14.cloned.1.call-start = ((), (), s32[]{:S(2)}) async-start(), calls=%async_computation.6 | async-start | bytes 1179648 | tf_op jit(solution)/shard_map/all_gather | solution.py:15
  394.3 111.0 %all-reduce.9.cloned.1.call-start = ((), (), s32[]{:S(2)}) async-start(), calls=%async_computation.7 | async-start | bytes 2621440 | tf_op jit(solution)/shard_map/psum | solution.py:21
  422.2 145.8 %all-reduce.11.cloned.1.call-start = ((), (), s32[]{:S(2)}) async-start(), calls=%async_computation.8 | async-start | bytes 2621440 | tf_op jit(solution)/shard_map/psum | solution.py:21
  505.3 105.4 %all-reduce.13.cloned.1.call-start = ((), (), s32[]{:S(2)}) async-start(), calls=%async_computation.9 | async-start | bytes 2621440 | tf_op jit(solution)/shard_map/psum | solution.py:21
  612.8 61.3 %copy-start.2 = (f32[1024,128]{1,0:T(8,128)S(1)}, f32[1024,128]{1,0:T(8,128)}, u32[]{:S(2)}) copy-start(f32[1024,128]{1,0:T(8,128)} %get-tuple-element.56) | copy-start | bytes 1572868
  612.8 61.3 %copy-start.3 = (f32[1024,128]{1,0:T(8,128)S(1)}, f32[1024,128]{1,0:T(8,128)}, u32[]{:S(2)}) copy-start(f32[1024,128]{1,0:T(8,128)} %get-tuple-element.57) | copy-start | bytes 1572868
Sparse Core Ops, SparseCore 0:
  10.6 63.4 all-gather.7
  76.9 29.2 all-gather.9
  108.9 37.9 all-gather.11
  394.4 26.1 all-gather.13
  423.5 81.7 all-reduce.8
  507.7 60.2 all-reduce.10
  571.1 39.5 all-reduce.12
where the time goes:
time: 695 us; the launch traced here: 687 us
  waiting for transfers between devices  478 us (69%)
  other arithmetic  114 us (16%)
  matrix products  32.1 us (5%)
  local copies, waits for them, and re-layouts  26.7 us (4%)
  starting transfers between devices  18.2 us (3%)
  between operations  17.6 us (3%)
    psum x3, waiting for transfers between devices, broadcast_by_axis(): value = lax.psum(value, axis)  187 us
    all_gather x4, waiting for transfers between devices, picked(): lax.all_gather(value, axis)  117 us
    all_to_all x1, waiting for transfers between devices, per_device(): lax.all_to_all(row_out, 'row', split_axis=0, concat_axis=0, tiled=True)  96.4 us
    another operation x13, other arithmetic, lower_inverse(): lower_factor = jnp.linalg.cholesky(corner)  68.6 us
    all_to_all x1, waiting for transfers between devices, per_device(): lax.all_to_all(leaf_out, 'leaf', split_axis=0, concat_axis=0, tiled=True)  50.8 us
    another operation x5, other arithmetic, lower_inverse(): return jax.scipy.linalg.solve_triangular(lower_factor, identity, lower=True)  39.4 us
    all_to_all x1, waiting for transfers between devices, per_device(): lax.all_to_all(column_out, COL, split_axis=0, concat_axis=0, tiled=True)  26.2 us
    dot_general x4, matrix products, contract(): jnp.einsum(form, left, right, precision=lax.Precision.HIGHEST, preferred_...  19.1 us
  transfers between devices with their start and end apart: 10, of which 9 were waited for; matrix products, arithmetic and copies ran while one was open for 10% of the time, Pallas kernels for 0%

commit v1 on v0

v1 whole, which is shorter than its diff:
```python
import jax
import jax.numpy as jnp
from jax import lax
from jax.experimental import pallas as pl
from jax.experimental.pallas import tpu as pltpu
from jax.sharding import Mesh
from jax.sharding import PartitionSpec as P

FP = 8192
PANEL = 256
BLOCK = 128
COL = ("col_0", "col_1")
ROW_COL = ("row", "col_0", "col_1")
LEAF_COL = ("leaf", "col_0", "col_1")
LEAF_ROW = ("leaf", "row")
HIGHEST = lax.Precision.HIGHEST
STEP = 64
GROUP = 8


def matmul(left, right):
    return jnp.dot(left, right, precision=HIGHEST, preferred_element_type=jnp.float32)


def matmul_nt(left, right):
    return lax.dot_general(
        left,
        right,
        (((1,), (1,)), ((), ())),
        precision=HIGHEST,
        preferred_element_type=jnp.float32,
    )


def matmul_tn(left, right):
    return lax.dot_general(
        left,
        right,
        (((0,), (0,)), ((), ())),
        precision=HIGHEST,
        preferred_element_type=jnp.float32,
    )


def exchange(value, axes):
    return lax.all_to_all(value, axes, split_axis=0, concat_axis=0, tiled=True)


def spread(value, axes, count):
    return exchange(jnp.broadcast_to(value[None], (count, *value.shape)), axes)


def eliminate(tile, eye, step):
    width = 2 * step
    row = lax.broadcasted_iota(jnp.int32, (step, width), 0)
    work = jnp.concatenate([tile, eye], axis=1)
    pivots = jnp.ones((step, width), jnp.float32)

    def tall(value):
        return jnp.concatenate([value] * (step // 8), axis=0)

    for first in range(0, step, GROUP):
        span = range(GROUP)
        cols = [
            jnp.broadcast_to(work[:, first + i : first + i + 1], (step, width)) for i in span
        ]
        rows = [jnp.broadcast_to(work[first + i : first + i + 1, :], (8, width)) for i in span]
        small = {}
        for i in span:
            for j in range(i, GROUP):
                small[i, j] = jnp.broadcast_to(cols[i][first + j : first + j + 1, :], (8, width))
        ratio = {}
        recip = []
        for i in span:
            recip.append(1.0 / small[i, i])
            for j in range(i + 1, GROUP):
                ratio[i, j] = small[i, j] * recip[i]
            for j in range(i + 1, GROUP):
                for k in range(j, GROUP):
                    small[j, k] = small[j, k] - ratio[i, j] * small[i, k]
        update = None
        for i in span:
            scaled = jnp.where(row > first + i, cols[i] * tall(recip[i]), 0.0)
            pivots = jnp.where(row == first + i, tall(small[i, i]), pivots)
            for j in range(i + 1, GROUP):
                cols[j] = cols[j] - cols[i] * tall(ratio[i, j])
                rows[j] = rows[j] - ratio[i, j] * rows[i]
            term = scaled * tall(rows[i])
            update = term if update is None else update + term
        work = work - update
    return work[:, step:width] * lax.rsqrt(pivots)[:, :step]


def inverse_kernel(corner_ref, out_ref, work_ref):
    size = corner_ref.shape[0]
    step = STEP
    row = lax.broadcasted_iota(jnp.int32, (size, size), 0)
    col = lax.broadcasted_iota(jnp.int32, (size, size), 1)
    work_ref[:, :size] = corner_ref[...]
    work_ref[:, size:] = (row == col).astype(jnp.float32)
    small_row = lax.broadcasted_iota(jnp.int32, (step, step), 0)
    small_col = lax.broadcasted_iota(jnp.int32, (step, step), 1)
    eye = (small_row == small_col).astype(jnp.float32)
    for start in range(0, size, step):
        stop = start + step
        lead = eliminate(work_ref[start:stop, start:stop], eye, step)
        upper = matmul(lead, work_ref[start:stop, :])
        out_ref[start:stop, :] = upper[:, size:]
        if stop < size:
            work_ref[stop:, :] = work_ref[stop:, :] - matmul_tn(upper[:, stop:size], upper)


def lower_inverse(corner):
    size = corner.shape[0]
    return pl.pallas_call(
        inverse_kernel,
        out_shape=jax.ShapeDtypeStruct((size, size), jnp.float32),
        scratch_shapes=[pltpu.VMEM((size, 2 * size), jnp.float32)],
        name="lower_inverse",
    )(corner)


def pick_kernel(index_ref, valid_ref, front_ref, out_ref):
    keep = valid_ref[pl.program_id(0)] > 0
    out_ref[0] = jnp.where(keep, front_ref[...], 0.0)


def pick_columns(index, valid, front):
    rows = front.shape[0]
    count = index.shape[0]
    return pl.pallas_call(
        pick_kernel,
        out_shape=jax.ShapeDtypeStruct((count, rows, BLOCK), jnp.float32),
        grid_spec=pltpu.PrefetchScalarGridSpec(
            num_scalar_prefetch=2,
            grid=(count,),
            in_specs=[pl.BlockSpec((rows, BLOCK), lambda i, index, valid: (0, index[i]))],
            out_specs=pl.BlockSpec((1, rows, BLOCK), lambda i, index, valid: (i, 0, 0)),
        ),
        name="pick_columns",
    )(index, valid, front)


def schur_kernel(
    slot_ref, slot_valid_ref, piece_ref, piece_valid_ref, cols_ref, factor_ref, block_ref, out_ref, tmp
):
    target = pl.program_id(0)
    live = slot_valid_ref[target] > 0

    @pl.when(live)
    def _():
        tmp[...] = cols_ref[0] - matmul_nt(factor_ref[...], block_ref[0])
        for dest in range(out_ref.shape[0]):
            start = pl.multiple_of(piece_ref[dest] * BLOCK, BLOCK)
            piece = tmp[pl.ds(start, BLOCK), :]
            out_ref[dest] = jnp.where(piece_valid_ref[dest] > 0, piece, 0.0)

    @pl.when(jnp.logical_not(live))
    def _():
        out_ref[...] = jnp.zeros_like(out_ref)


def schur_pieces(slot, slot_valid, piece, piece_valid, cols, factor, blocks):
    leaves = slot.shape[0]
    bands = piece.shape[0]
    rows = factor.shape[0]
    panel = factor.shape[1]
    return pl.pallas_call(
        schur_kernel,
        out_shape=jax.ShapeDtypeStruct((leaves * bands, BLOCK, BLOCK), jnp.float32),
        grid_spec=pltpu.PrefetchScalarGridSpec(
            num_scalar_prefetch=4,
            grid=(leaves,),
            in_specs=[
                pl.BlockSpec((1, rows, BLOCK), lambda i, s, sv, p, pv: (s[i], 0, 0)),
                pl.BlockSpec((rows, panel), lambda i, s, sv, p, pv: (0, 0)),
                pl.BlockSpec((1, BLOCK, panel), lambda i, s, sv, p, pv: (s[i], 0, 0)),
            ],
            out_specs=pl.BlockSpec((bands, BLOCK, BLOCK), lambda i, s, sv, p, pv: (i, 0, 0)),
            scratch_shapes=[pltpu.VMEM((rows, BLOCK), jnp.float32)],
        ),
        name="schur_pieces",
    )(slot, slot_valid, piece, piece_valid, cols, factor, blocks)


def place_kernel(slot_ref, parent_ref, blocks_ref, out_ref):
    step = pl.program_id(0)

    @pl.when(step == 0)
    def _():
        out_ref[...] = parent_ref[...]

    count = blocks_ref.shape[0]
    for item in range(count):
        slot = slot_ref[step * count + item]

        @pl.when(slot >= 0)
        def _(item=item, slot=slot):
            start = pl.multiple_of(slot * BLOCK, BLOCK)
            out_ref[pl.ds(start, BLOCK), :] += blocks_ref[item]


def place_blocks(slots, parent, blocks):
    total = blocks.shape[0]
    batch = 8
    rows = parent.shape[0]
    return pl.pallas_call(
        place_kernel,
        out_shape=jax.ShapeDtypeStruct(parent.shape, jnp.float32),
        grid_spec=pltpu.PrefetchScalarGridSpec(
            num_scalar_prefetch=1,
            grid=(total // batch,),
            in_specs=[
                pl.BlockSpec((rows, BLOCK), lambda i, slots: (0, 0)),
                pl.BlockSpec((batch, BLOCK, BLOCK), lambda i, slots: (i, 0, 0)),
            ],
            out_specs=pl.BlockSpec((rows, BLOCK), lambda i, slots: (0, 0)),
        ),
        name="place_blocks",
    )(slots, parent, blocks)


def locate(values, usable, count):
    hit = (values[..., None, :] == jnp.arange(count)[:, None]) & usable[..., None, :]
    index = jnp.sum(jnp.where(hit, jnp.arange(values.shape[-1]), 0), axis=-1)
    return index.astype(jnp.int32), jnp.any(hit, axis=-1)


def at(value, index, axis=0):
    return lax.dynamic_index_in_dim(value, index, axis, keepdims=False)


def per_device(child_front, parent_front, block_map):
    front = child_front[0]
    parent = parent_front[:, 0, 0, :]
    grid_rows = lax.axis_size("row")
    grid_cols = lax.axis_size(COL)
    leaves = lax.axis_size("leaf")
    row_id = lax.axis_index("row")
    col_id = lax.axis_index(COL)
    leaf_id = lax.axis_index("leaf")
    rows = front.shape[0]
    child_blocks = rows // BLOCK
    lead = PANEL // BLOCK
    plane = grid_rows * grid_cols
    parent_rows = parent.shape[0]

    padded = jnp.concatenate([jnp.full((leaves, lead), -1, jnp.int32), block_map], axis=1)
    maps = padded.reshape(leaves, grid_rows, child_blocks)
    usable = maps >= 0
    band = maps // grid_cols
    residue = maps % grid_cols
    lo_index, lo_valid = locate(residue, usable, grid_cols)
    hi_index, hi_valid = locate(band, usable, grid_rows)

    own_lo_index, own_lo_valid = at(lo_index, leaf_id), at(lo_valid, leaf_id)
    send_index, send_valid = at(own_lo_index, col_id), at(own_lo_valid, col_id)
    cols = exchange(
        pick_columns(send_index, send_valid.astype(jnp.int32), front), COL
    )

    corner = jnp.concatenate([front[:PANEL, :BLOCK], front[:PANEL, BLOCK:PANEL]], axis=0)
    corner = exchange(corner.reshape(plane, -1, BLOCK), ROW_COL)[0]
    corner = spread(corner, ROW_COL, plane).reshape(lead, PANEL, BLOCK)
    corner = jnp.concatenate([corner[i] for i in range(lead)], axis=1)
    inverse = lower_inverse(corner)
    piece = exchange(front[:, :PANEL].reshape(grid_cols, -1, PANEL), COL)[0]
    factor = spread(matmul_nt(piece, inverse), COL, grid_cols).reshape(rows, PANEL)

    column_index = at(own_lo_index, col_id, 1)
    column_valid = at(own_lo_valid, col_id, 1)
    mine = lax.dynamic_slice_in_dim(factor, at(column_index, row_id) * BLOCK, BLOCK, 0)
    blocks = spread(mine, "row", grid_rows)
    column_band = jnp.sum(
        jnp.where(
            jnp.arange(child_blocks) == column_index[:, None],
            at(band, leaf_id),
            0,
        ),
        axis=-1,
    )
    slot, slot_valid = locate(column_band, column_valid, leaves)
    pieces = schur_pieces(
        slot,
        slot_valid.astype(jnp.int32),
        at(at(hi_index, leaf_id), row_id),
        at(at(hi_valid, leaf_id), row_id).astype(jnp.int32),
        cols,
        factor,
        blocks,
    )
    arrived = exchange(pieces, LEAF_ROW)

    own_column = leaf_id * grid_cols + col_id
    present = jnp.any((maps == own_column) & usable, axis=(1, 2))
    row_index = at(hi_index, row_id, 2)
    row_valid = at(hi_valid, row_id, 2)
    row_slot = jnp.sum(
        jnp.where(jnp.arange(child_blocks) == row_index[..., None], residue, 0), axis=-1
    )
    slots = jnp.where(row_valid & present[:, None], row_slot, -1).astype(jnp.int32).reshape(-1)
    assembled = place_blocks(slots, parent, arrived)

    top = exchange(assembled[:PANEL].reshape(grid_rows, -1, BLOCK), "row")[0]
    top = spread(top, "row", grid_rows).reshape(PANEL, BLOCK)
    both = jnp.concatenate([assembled, top], axis=0)
    both = exchange(both.reshape(leaves * grid_cols, -1, BLOCK), LEAF_COL)[:lead]
    both = spread(both, LEAF_COL, leaves * grid_cols)
    both = jnp.concatenate(
        [both[:, i].reshape(parent_rows + PANEL, BLOCK) for i in range(lead)], axis=1
    )
    panel = both[:parent_rows]
    inverse_parent = lower_inverse(both[parent_rows:])
    parent_factor = matmul_nt(panel, inverse_parent)
    upper = matmul(inverse_parent, top)
    updated = assembled - matmul(parent_factor, upper)
    global_row = row_id * parent_rows + jnp.arange(parent_rows)
    kept = jnp.where((global_row < PANEL)[:, None], assembled, updated)
    result = kept
    for i in range(lead):
        result = jnp.where(
            own_column == i, parent_factor[:, i * BLOCK : (i + 1) * BLOCK], result
        )
    return (factor[None], result[:, None, None, :])


def solution(mesh):
    torus = Mesh(
        mesh.devices.reshape(mesh.shape["leaf"], mesh.shape["row"], 4, 2),
        ("leaf", "row", "col_0", "col_1"),
    )
    in_specs = (P("leaf", "row", COL), P("row", None, LEAF_COL, None), P())
    out_specs = (P("leaf", "row", None), P("row", None, LEAF_COL, None))
    return jax.shard_map(
        per_device, mesh=torus, in_specs=in_specs, out_specs=out_specs, check_vma=False
    )
```

time: 695 us -> 436 us (0.63); the launches traced: 687 us -> 437 us
  waiting for transfers between devices: 478 us -> 216 us
  blocking collectives: 0 us -> 116 us
  other arithmetic: 114 us -> 4.88 us
  Pallas kernels: 0 us -> 44.7 us
  matrix products: 32.1 us -> 5.52 us
  starting transfers between devices: 18.2 us -> 35.7 us
  between operations: 17.6 us -> 1.53 us
  local copies, waits for them, and re-layouts: 26.7 us -> 12.9 us
    psum x3 -> x0, waiting for transfers between devices: 187 us -> none  [broadcast_by_axis(): value = lax.psum(value, axis)]
    all_gather x4 -> x0, waiting for transfers between devices: 117 us -> none  [picked(): lax.all_gather(value, axis)]
    all_to_all x0 -> x4, blocking collectives: none -> 116 us  [exchange(): return lax.all_to_all(value, axes, split_axis=0, concat_axis=0, tiled=True)]
    another operation x18 -> x0, other arithmetic: 108 us -> none  [the longest x13 68.6 us: lower_inverse(): lower_factor = jnp.linalg.cholesky(corner)]
    pallas_call x0 -> x5, Pallas kernels: none -> 44.7 us  [the longest x2 24.7 us: lower_inverse(): pl.pallas_call(inverse_kernel, out_shape=jax.ShapeDtypeStruct((size, size...]
    all_to_all x3 -> x7, waiting for transfers between devices: 173 us -> 216 us  [exchange(): return lax.all_to_all(value, axes, split_axis=0, concat_axis=0, tiled=True)]
    dot_general x10 -> x4, matrix products: 29.4 us -> 5.52 us  [the longest x2 3.36 us: matmul_nt(): lax.dot_general(left, right, (((1,), (1,)), ((), ())), precision=HIGHEST,...]
    all_to_all x3 -> x7, starting transfers between devices: 17.7 us -> 35.7 us  [exchange(): return lax.all_to_all(value, axes, split_axis=0, concat_axis=0, tiled=True)]
  transfers between devices with their start and end apart: 10 -> 7, of which waited for: 9 -> 6; matrix products, arithmetic and copies ran while one was open for 10% -> 2% of each run, Pallas kernels for 0% -> 4%
where the time goes in v1:
time: 436 us; the launch traced here: 437 us
  waiting for transfers between devices  216 us (50%)
  blocking collectives  116 us (27%)
  Pallas kernels  44.7 us (10%)
  starting transfers between devices  35.7 us (8%)
  local copies, waits for them, and re-layouts  12.9 us (3%)
  matrix products  5.52 us (1%)
  other arithmetic  4.88 us (1%)
    all_to_all x7, waiting for transfers between devices, exchange(): return lax.all_to_all(value, axes, split_axis=0, concat_axis=0, tiled=True)  216 us
    all_to_all x4, blocking collectives, exchange(): return lax.all_to_all(value, axes, split_axis=0, concat_axis=0, tiled=True)  116 us
    all_to_all x7, starting transfers between devices, exchange(): return lax.all_to_all(value, axes, split_axis=0, concat_axis=0, tiled=True)  35.7 us
    pallas_call x2, Pallas kernels, lower_inverse(): pl.pallas_call(inverse_kernel, out_shape=jax.ShapeDtypeStruct((size, size...  24.7 us
  transfers between devices with their start and end apart: 7, of which 6 were waited for; matrix products, arithmetic and copies ran while one was open for 2% of the time, Pallas kernels for 4%

profile of v1, /device:TPU:1, one launch (start us, length us, event | category | flops | bytes accessed | tf_op | source)
XLA Modules:
  0.0 437.1 jit_solution(15214046777218618797)
XLA Ops:
  1.8 27.7 %all_to_all.55 = f32[64,8,128]{2,1,0:T(8,128)S(1)} all-to-all(f32[64,8,128]{2,1,0:T(8,128)S(1)} %maximum_bitcast_fusion), channel_id=1, replica_groups=mesh['leaf'=8,'row'=8,'col_0'=4,'col_1'=2] {'row','col_0','col_1'}, dimensions={0} | all-to-all | bytes 524288 | tf_op jit(solution)/shard_map/all_to_all | solution.py:46
  30.2 4.8 %all-to-all-start.1 = ((f32[64,8,128]{2,1,0:T(8,128)}), f32[64,8,128]{2,1,0:T(8,128)S(1)}, u32[]{:S(2)}, u32[]{:S(2)}) async-start(f32[64,8,128]{2,1,0:T(8,128)} %broadcast_in_dim.87), calls=%async_computation.1 | async-start | bytes 524288 | tf_op jit(solution)/shard_map/all_to_all | solution.py:46
  35.9 12.1 %all-to-all-done.1 = f32[64,8,128]{2,1,0:T(8,128)S(1)} async-done(((f32[64,8,128]{2,1,0:T(8,128)}), f32[64,8,128]{2,1,0:T(8,128)S(1)}, u32[]{:S(2)}, u32[]{:S(2)}) %all-to-all-start.1) | async-done | bytes 262176 | tf_op jit(solution)/shard_map/all_to_all | solution.py:46
  48.0 3.7 all-to-all-start.2
  52.7 12.3 %lower_inverse.2 = f32[256,256]{1,0:T(8,128)} custom-call(f32[256,256]{1,0:T(8,128)} %pad_maximum_fusion.2.corner_ref), custom_call_target="tpu_custom_call" | custom-call | tf_op jit(solution)/shard_map/lower_inverse/pallas_call | solution.py:115
  67.2 4.8 %all-to-all-start.3 = ((f32[8,64,256]{2,1,0:T(8,128)}), f32[8,64,256]{2,1,0:T(8,128)S(1)}, u32[]{:S(2)}, u32[]{:S(2)}) async-start(f32[8,64,256]{2,1,0:T(8,128)} %broadcast_in_dim.88), calls=%async_computation.3 | async-start | bytes 1048576 | tf_op jit(solution)/shard_map/all_to_all | solution.py:46
  73.4 5.6 %pick_columns.1 = f32[8,512,128]{2,1,0:T(8,128)} custom-call(s32[8]{0:T(128)} %fusion.19.index_ref, s32[8]{0:T(128)} %fusion.16.valid_ref, f32[512,512]{1,0:T(8,128)} %bitcast.56), custom_call_target="tpu_custom_call" | custom-call | tf_op jit(solution)/shard_map/pick_columns/pallas_call | solution.py:131
  79.0 2.4 all-to-all-done.3
  81.4 4.5 %all-to-all-start.4 = ((f32[8,512,128]{2,1,0:T(8,128)}), f32[8,512,128]{2,1,0:T(8,128)S(1)}, u32[]{:S(2)}, u32[]{:S(2)}) async-start(f32[8,512,128]{2,1,0:T(8,128)} %pick_columns.1), calls=%async_computation.4 | async-start | bytes 4194304 | tf_op jit(solution)/shard_map/all_to_all | solution.py:46
  87.2 25.0 %all-to-all-done.4.cols_ref = f32[8,512,128]{2,1,0:T(8,128)S(1)} async-done(((f32[8,512,128]{2,1,0:T(8,128)}), f32[8,512,128]{2,1,0:T(8,128)S(1)}, u32[]{:S(2)}, u32[]{:S(2)}) %all-to-all-start.4) | async-done | bytes 2097184 | tf_op jit(solution)/shard_map/all_to_all | solution.py:46
  113.8 4.2 all-to-all-start.5
  121.0 26.2 %all-to-all-done.5.block_ref = f32[8,128,256]{2,1,0:T(8,128)} async-done(((f32[8,128,256]{2,1,0:T(8,128)}), f32[8,128,256]{2,1,0:T(8,128)}, u32[]{:S(2)}, u32[]{:S(2)}) %all-to-all-start.5) | async-done | bytes 1048608 | tf_op jit(solution)/shard_map/all_to_all | solution.py:46
  147.2 8.1 %schur_pieces.1 = f32[64,128,128]{2,1,0:T(8,128)} custom-call(s32[8]{0:T(128)} %select_reduce_fusion.3.slot_ref, s32[8]{0:T(128)} %convert_element_type.13.slot_valid_ref, s32[8]{0:T(128)} %fusion.18.piece_ref, s32[8]{0:T(128)} %fusion.17.piece_valid_ref, f32[8,512,128]{2,1,0:T(8,128)} %copy-done, f32[512,256]{1,0:T(8,128)} %bitcast.53, ...), custom_call_target="tpu_custom_call" | custom-call | tf_op jit(solution)/shard_map/schur_pieces/pallas_call | solution.py:168
  155.3 7.8 %all-to-all-start.6 = ((f32[64,128,128]{2,1,0:T(8,128)}), f32[64,128,128]{2,1,0:T(8,128)}, u32[]{:S(2)}, u32[]{:S(2)}) async-start(f32[64,128,128]{2,1,0:T(8,128)} %schur_pieces.1), calls=%async_computation.6 | async-start | bytes 8388608 | tf_op jit(solution)/shard_map/all_to_all | solution.py:46
  164.6 116.3 %all-to-all-done.6.blocks_ref = f32[64,128,128]{2,1,0:T(8,128)} async-done(((f32[64,128,128]{2,1,0:T(8,128)}), f32[64,128,128]{2,1,0:T(8,128)}, u32[]{:S(2)}, u32[]{:S(2)}) %all-to-all-start.6) | async-done | bytes 4194336 | tf_op jit(solution)/shard_map/all_to_all | solution.py:46
  280.9 6.3 %place_blocks.1 = f32[1024,128]{1,0:T(8,128)} custom-call(s32[64]{0:T(128)} %and_select_fusion.slot_ref, f32[1024,128]{1,0:T(8,128)} %bitcast.62, f32[64,128,128]{2,1,0:T(8,128)} %all-to-all-done.6.blocks_ref), custom_call_target="tpu_custom_call" | custom-call | tf_op jit(solution)/shard_map/place_blocks/pallas_call | solution.py:207
  288.2 23.5 %all_to_all.56 = f32[8,32,128]{2,1,0:T(8,128)S(1)} all-to-all(f32[8,32,128]{2,1,0:T(8,128)S(1)} %bitcast.61), channel_id=1, replica_groups=mesh['leaf'=8,'row'=8,'col_0'=4,'col_1'=2] {'row'}, dimensions={0} | all-to-all | bytes 262144 | tf_op jit(solution)/shard_map/all_to_all | solution.py:46
  311.7 10.4 %all_to_all.57 = f32[8,32,128]{2,1,0:T(8,128)S(1)} all-to-all(f32[8,32,128]{2,1,0:T(8,128)S(1)} %broadcast_in_dim.98), channel_id=1, replica_groups=mesh['leaf'=8,'row'=8,'col_0'=4,'col_1'=2] {'row'}, dimensions={0} | all-to-all | bytes 262144 | tf_op jit(solution)/shard_map/all_to_all | solution.py:46
  322.3 54.7 %all_to_all.58 = f32[64,20,128]{2,1,0:T(8,128)S(1)} all-to-all(f32[64,20,128]{2,1,0:T(8,128)S(1)} %reshape.127), channel_id=1, replica_groups=mesh['leaf'=8,'row'=8,'col_0'=4,'col_1'=2] {'leaf','col_0','col_1'}, dimensions={0} | all-to-all | bytes 1310720 | tf_op jit(solution)/shard_map/all_to_all | solution.py:46
  378.4 5.9 %all-to-all-start.10 = ((f32[64,2,20,128]{3,1,2,0:T(2,128)}), f32[64,2,20,128]{3,1,2,0:T(2,128)S(1)}, u32[]{:S(2)}, u32[]{:S(2)}) async-start(f32[64,2,20,128]{3,1,2,0:T(2,128)} %broadcast_in_dim.99), calls=%async_computation.10 | async-start | bytes 2621440 | tf_op jit(solution)/shard_map/all_to_all | solution.py:46
  384.3 33.6 %all-to-all-done.10 = f32[64,2,20,128]{3,1,2,0:T(2,128)S(1)} async-done(((f32[64,2,20,128]{3,1,2,0:T(2,128)}), f32[64,2,20,128]{3,1,2,0:T(2,128)S(1)}, u32[]{:S(2)}, u32[]{:S(2)}) %all-to-all-start.10) | async-done | bytes 1310752 | tf_op jit(solution)/shard_map/all_to_all | solution.py:46
  419.7 12.3 %lower_inverse.3 = f32[256,256]{1,0:T(8,128)} custom-call(f32[256,256]{1,0:T(8,128)} %pad_maximum_fusion.1.corner_ref), custom_call_target="tpu_custom_call" | custom-call | tf_op jit(solution)/shard_map/lower_inverse/pallas_call | solution.py:115
  432.0 2.0 fusion.4
  434.5 1.8 fusion.2
  (72 shorter events, 19.5 us)
Async XLA Ops:
  0.6 34.3 %copy-start.4 = (f32[1,512,512]{2,1,0:T(8,128)S(1)}, f32[1,512,512]{2,1,0:T(8,128)}, u32[]{:S(2)}) copy-start(f32[1,512,512]{2,1,0:T(8,128)} %param.3) | copy-start | bytes 3145732
  1.7 34.1 %copy-start.6 = (s32[8,30]{1,0:T(8,128)S(1)}, s32[8,30]{1,0:T(8,128)}, u32[]{:S(2)}) copy-start(s32[8,30]{1,0:T(8,128)} %param.5) | copy-start | bytes 2884
  30.2 17.9 %all-to-all-start.1 = ((f32[64,8,128]{2,1,0:T(8,128)}), f32[64,8,128]{2,1,0:T(8,128)S(1)}, u32[]{:S(2)}, u32[]{:S(2)}) async-start(f32[64,8,128]{2,1,0:T(8,128)} %broadcast_in_dim.87), calls=%async_computation.1 | async-start | bytes 524288 | tf_op jit(solution)/shard_map/all_to_all | solution.py:46
  48.0 17.0 %all-to-all-start.2 = ((f32[8,64,256]{2,1,0:T(8,128)}), f32[8,64,256]{2,1,0:T(8,128)S(1)}, u32[]{:S(2)}, u32[]{:S(2)}) async-start(f32[8,64,256]{2,1,0:T(8,128)} %bitcast.5), calls=%async_computation.2 | async-start | bytes 1048576 | tf_op jit(solution)/shard_map/all_to_all | solution.py:46
  67.2 14.2 %all-to-all-start.3 = ((f32[8,64,256]{2,1,0:T(8,128)}), f32[8,64,256]{2,1,0:T(8,128)S(1)}, u32[]{:S(2)}, u32[]{:S(2)}) async-start(f32[8,64,256]{2,1,0:T(8,128)} %broadcast_in_dim.88), calls=%async_computation.3 | async-start | bytes 1048576 | tf_op jit(solution)/shard_map/all_to_all | solution.py:46
  81.4 5.7 %copy-start.1 = (f32[8,64,256]{2,1,0:T(8,128)}, f32[8,64,256]{2,1,0:T(8,128)S(1)}, u32[]{:S(2)}) copy-start(f32[8,64,256]{2,1,0:T(8,128)S(1)} %all-to-all-done.3) | copy-start | bytes 1572868
  81.4 30.7 %all-to-all-start.4 = ((f32[8,512,128]{2,1,0:T(8,128)}), f32[8,512,128]{2,1,0:T(8,128)S(1)}, u32[]{:S(2)}, u32[]{:S(2)}) async-start(f32[8,512,128]{2,1,0:T(8,128)} %pick_columns.1), calls=%async_computation.4 | async-start | bytes 4194304 | tf_op jit(solution)/shard_map/all_to_all | solution.py:46
  112.1 1.6 copy-start
  113.8 33.4 %all-to-all-start.5 = ((f32[8,128,256]{2,1,0:T(8,128)}), f32[8,128,256]{2,1,0:T(8,128)}, u32[]{:S(2)}, u32[]{:S(2)}) async-start(f32[8,128,256]{2,1,0:T(8,128)} %broadcast_in_dim.96), calls=%async_computation.5 | async-start | bytes 2097152 | tf_op jit(solution)/shard_map/all_to_all | solution.py:46
  155.3 125.6 %all-to-all-start.6 = ((f32[64,128,128]{2,1,0:T(8,128)}), f32[64,128,128]{2,1,0:T(8,128)}, u32[]{:S(2)}, u32[]{:S(2)}) async-start(f32[64,128,128]{2,1,0:T(8,128)} %schur_pieces.1), calls=%async_computation.6 | async-start | bytes 8388608 | tf_op jit(solution)/shard_map/all_to_all | solution.py:46
  287.2 34.9 %copy-start.3 = (f32[1024,128]{1,0:T(8,128)S(1)}, f32[1024,128]{1,0:T(8,128)}, u32[]{:S(2)}) copy-start(f32[1024,128]{1,0:T(8,128)} %place_blocks.1) | copy-start | bytes 1572868
  378.4 39.5 %all-to-all-start.10 = ((f32[64,2,20,128]{3,1,2,0:T(2,128)}), f32[64,2,20,128]{3,1,2,0:T(2,128)S(1)}, u32[]{:S(2)}, u32[]{:S(2)}) async-start(f32[64,2,20,128]{3,1,2,0:T(2,128)} %broadcast_in_dim.99), calls=%async_computation.10 | async-start | bytes 2621440 | tf_op jit(solution)/shard_map/all_to_all | solution.py:46
  432.0 2.0 copy-start.5
  434.1 2.2 copy-start.2

commit v2 on v1

--- a/solution.py
+++ b/solution.py
@@ -10,7 +10,6 @@
 PANEL = 256
 BLOCK = 128
 COL = ("col_0", "col_1")
-ROW_COL = ("row", "col_0", "col_1")
 LEAF_COL = ("leaf", "col_0", "col_1")
 LEAF_ROW = ("leaf", "row")
 HIGHEST = lax.Precision.HIGHEST
@@ -120,67 +119,57 @@
     )(corner)
 
 
-def pick_kernel(index_ref, valid_ref, front_ref, out_ref):
-    keep = valid_ref[pl.program_id(0)] > 0
-    out_ref[0] = jnp.where(keep, front_ref[...], 0.0)
-
-
-def pick_columns(index, valid, front):
+def pick_kernel(index_ref, front_ref, out_ref):
+    out_ref[0] = front_ref[...]
+
+
+def pick_columns(index, front):
     rows = front.shape[0]
     count = index.shape[0]
     return pl.pallas_call(
         pick_kernel,
         out_shape=jax.ShapeDtypeStruct((count, rows, BLOCK), jnp.float32),
         grid_spec=pltpu.PrefetchScalarGridSpec(
-            num_scalar_prefetch=2,
+            num_scalar_prefetch=1,
             grid=(count,),
-            in_specs=[pl.BlockSpec((rows, BLOCK), lambda i, index, valid: (0, index[i]))],
-            out_specs=pl.BlockSpec((1, rows, BLOCK), lambda i, index, valid: (i, 0, 0)),
+            in_specs=[pl.BlockSpec((rows, BLOCK), lambda i, index: (0, index[i]))],
+            out_specs=pl.BlockSpec((1, rows, BLOCK), lambda i, index: (i, 0, 0)),
         ),
         name="pick_columns",
-    )(index, valid, front)
-
-
-def schur_kernel(
-    slot_ref, slot_valid_ref, piece_ref, piece_valid_ref, cols_ref, factor_ref, block_ref, out_ref, tmp
-):
-    target = pl.program_id(0)
-    live = slot_valid_ref[target] > 0
-
-    @pl.when(live)
+    )(index, front)
+
+
+def schur_kernel(slot_ref, live_ref, piece_ref, cols_ref, factor_ref, inverse_ref, block_ref, out_ref, tmp):
+    @pl.when(live_ref[pl.program_id(0)] > 0)
     def _():
-        tmp[...] = cols_ref[0] - matmul_nt(factor_ref[...], block_ref[0])
+        block = matmul_nt(block_ref[0], inverse_ref[...])
+        tmp[...] = cols_ref[0] - matmul_nt(factor_ref[...], block)
         for dest in range(out_ref.shape[0]):
             start = pl.multiple_of(piece_ref[dest] * BLOCK, BLOCK)
-            piece = tmp[pl.ds(start, BLOCK), :]
-            out_ref[dest] = jnp.where(piece_valid_ref[dest] > 0, piece, 0.0)
-
-    @pl.when(jnp.logical_not(live))
-    def _():
-        out_ref[...] = jnp.zeros_like(out_ref)
-
-
-def schur_pieces(slot, slot_valid, piece, piece_valid, cols, factor, blocks):
+            out_ref[dest] = tmp[pl.ds(start, BLOCK), :]
+
+
+def schur_pieces(slot, live, piece, cols, factor, inverse, blocks):
     leaves = slot.shape[0]
     bands = piece.shape[0]
-    rows = factor.shape[0]
-    panel = factor.shape[1]
+    rows, panel = factor.shape
     return pl.pallas_call(
         schur_kernel,
         out_shape=jax.ShapeDtypeStruct((leaves * bands, BLOCK, BLOCK), jnp.float32),
         grid_spec=pltpu.PrefetchScalarGridSpec(
-            num_scalar_prefetch=4,
+            num_scalar_prefetch=3,
             grid=(leaves,),
             in_specs=[
-                pl.BlockSpec((1, rows, BLOCK), lambda i, s, sv, p, pv: (s[i], 0, 0)),
-                pl.BlockSpec((rows, panel), lambda i, s, sv, p, pv: (0, 0)),
-                pl.BlockSpec((1, BLOCK, panel), lambda i, s, sv, p, pv: (s[i], 0, 0)),
+                pl.BlockSpec((1, rows, BLOCK), lambda i, s, v, p: (s[i], 0, 0)),
+                pl.BlockSpec((rows, panel), lambda i, s, v, p: (0, 0)),
+                pl.BlockSpec((panel, panel), lambda i, s, v, p: (0, 0)),
+                pl.BlockSpec((1, BLOCK, panel), lambda i, s, v, p: (s[i], 0, 0)),
             ],
-            out_specs=pl.BlockSpec((bands, BLOCK, BLOCK), lambda i, s, sv, p, pv: (i, 0, 0)),
+            out_specs=pl.BlockSpec((bands, BLOCK, BLOCK), lambda i, s, v, p: (i, 0, 0)),
             scratch_shapes=[pltpu.VMEM((rows, BLOCK), jnp.float32)],
         ),
         name="schur_pieces",
-    )(slot, slot_valid, piece, piece_valid, cols, factor, blocks)
+    )(slot, live, piece, cols, factor, inverse, blocks)
 
 
 def place_kernel(slot_ref, parent_ref, blocks_ref, out_ref):
@@ -230,6 +219,18 @@
     return lax.dynamic_index_in_dim(value, index, axis, keepdims=False)
 
 
+def gather_col(value):
+    along = spread(value, "col_0", lax.axis_size("col_0"))
+    other = lax.ppermute(along, "col_1", [(0, 1), (1, 0)])
+    first = lax.axis_index("col_1") == 0
+    both = jnp.stack([jnp.where(first, along, other), jnp.where(first, other, along)], axis=1)
+    return both.reshape(-1, *value.shape)
+
+
+def side_by_side(blocks):
+    return jnp.concatenate([blocks[i] for i in range(blocks.shape[0])], axis=1)
+
+
 def per_device(child_front, parent_front, block_map):
     front = child_front[0]
     parent = parent_front[:, 0, 0, :]
@@ -242,7 +243,6 @@
     rows = front.shape[0]
     child_blocks = rows // BLOCK
     lead = PANEL // BLOCK
-    plane = grid_rows * grid_cols
     parent_rows = parent.shape[0]
 
     padded = jnp.concatenate([jnp.full((leaves, lead), -1, jnp.int32), block_map], axis=1)
@@ -252,75 +252,72 @@
     residue = maps % grid_cols
     lo_index, lo_valid = locate(residue, usable, grid_cols)
     hi_index, hi_valid = locate(band, usable, grid_rows)
-
     own_lo_index, own_lo_valid = at(lo_index, leaf_id), at(lo_valid, leaf_id)
-    send_index, send_valid = at(own_lo_index, col_id), at(own_lo_valid, col_id)
-    cols = exchange(
-        pick_columns(send_index, send_valid.astype(jnp.int32), front), COL
-    )
-
-    corner = jnp.concatenate([front[:PANEL, :BLOCK], front[:PANEL, BLOCK:PANEL]], axis=0)
-    corner = exchange(corner.reshape(plane, -1, BLOCK), ROW_COL)[0]
-    corner = spread(corner, ROW_COL, plane).reshape(lead, PANEL, BLOCK)
-    corner = jnp.concatenate([corner[i] for i in range(lead)], axis=1)
-    inverse = lower_inverse(corner)
-    piece = exchange(front[:, :PANEL].reshape(grid_cols, -1, PANEL), COL)[0]
-    factor = spread(matmul_nt(piece, inverse), COL, grid_cols).reshape(rows, PANEL)
-
     column_index = at(own_lo_index, col_id, 1)
     column_valid = at(own_lo_valid, col_id, 1)
-    mine = lax.dynamic_slice_in_dim(factor, at(column_index, row_id) * BLOCK, BLOCK, 0)
-    blocks = spread(mine, "row", grid_rows)
+
+    share = PANEL // grid_cols
+    deals = front[:, :PANEL].reshape(-1, grid_cols, share, PANEL).transpose(1, 0, 2, 3)
+    deal = exchange(deals.reshape(grid_cols, -1, PANEL), COL)[0]
+    corner = gather_col(spread(deal[:share], "row", grid_rows)[0]).reshape(PANEL, PANEL)
+    raw = gather_col(deal).reshape(grid_cols, -1, share, PANEL)
+    raw = raw.transpose(1, 0, 2, 3).reshape(rows, PANEL)
+    mine = lax.dynamic_slice_in_dim(raw, at(column_index, row_id) * BLOCK, BLOCK, 0)
+    blocks = lax.all_gather(mine, "row")
+    cols = exchange(pick_columns(at(own_lo_index, col_id), front), COL)
+    inverse = lower_inverse(corner)
+    factor = matmul_nt(raw, inverse)
+
     column_band = jnp.sum(
-        jnp.where(
-            jnp.arange(child_blocks) == column_index[:, None],
-            at(band, leaf_id),
-            0,
-        ),
-        axis=-1,
+        jnp.where(jnp.arange(child_blocks) == column_index[:, None], at(band, leaf_id), 0), axis=-1
     )
     slot, slot_valid = locate(column_band, column_valid, leaves)
     pieces = schur_pieces(
         slot,
         slot_valid.astype(jnp.int32),
         at(at(hi_index, leaf_id), row_id),
-        at(at(hi_valid, leaf_id), row_id).astype(jnp.int32),
         cols,
         factor,
+        inverse,
         blocks,
     )
-    arrived = exchange(pieces, LEAF_ROW)
 
     own_column = leaf_id * grid_cols + col_id
     present = jnp.any((maps == own_column) & usable, axis=(1, 2))
-    row_index = at(hi_index, row_id, 2)
-    row_valid = at(hi_valid, row_id, 2)
     row_slot = jnp.sum(
-        jnp.where(jnp.arange(child_blocks) == row_index[..., None], residue, 0), axis=-1
-    )
-    slots = jnp.where(row_valid & present[:, None], row_slot, -1).astype(jnp.int32).reshape(-1)
-    assembled = place_blocks(slots, parent, arrived)
-
-    top = exchange(assembled[:PANEL].reshape(grid_rows, -1, BLOCK), "row")[0]
+        jnp.where(jnp.arange(child_blocks) == hi_index[..., None], residue[:, :, None, :], 0),
+        axis=-1,
+    )
+    row_slot = jnp.where(hi_valid & present[:, None, None], row_slot, -1).astype(jnp.int32)
+
+    tops = exchange(pieces.reshape(leaves, grid_rows, BLOCK, BLOCK)[:, 0], "leaf")
+    top_slot = at(row_slot, row_id, 1)[:, 0]
+    top = jnp.where(row_id == 0, parent[:PANEL], 0.0).reshape(lead, BLOCK, BLOCK)
+    top = top + jnp.stack(
+        [
+            sum(jnp.where(top_slot[c] == i, tops[c], 0.0) for c in range(leaves))
+            for i in range(lead)
+        ]
+    )
+    top = jnp.sum(exchange(top.reshape(grid_rows, -1, BLOCK), "row"), axis=0)
     top = spread(top, "row", grid_rows).reshape(PANEL, BLOCK)
-    both = jnp.concatenate([assembled, top], axis=0)
-    both = exchange(both.reshape(leaves * grid_cols, -1, BLOCK), LEAF_COL)[:lead]
-    both = spread(both, LEAF_COL, leaves * grid_cols)
-    both = jnp.concatenate(
-        [both[:, i].reshape(parent_rows + PANEL, BLOCK) for i in range(lead)], axis=1
-    )
-    panel = both[:parent_rows]
-    inverse_parent = lower_inverse(both[parent_rows:])
-    parent_factor = matmul_nt(panel, inverse_parent)
+    arrived = exchange(pieces, LEAF_ROW)
+
+    every_leaf = lax.all_gather(top, "leaf")
+    pair = jnp.stack([at(every_leaf, row_id), every_leaf[0]])
+    every_col = lax.all_gather(pair, COL)
+    band_top = side_by_side(every_col[:, 0])
+    inverse_parent = lower_inverse(side_by_side(every_col[:lead, 1]))
+    band_upper = matmul(inverse_parent, band_top)
     upper = matmul(inverse_parent, top)
-    updated = assembled - matmul(parent_factor, upper)
     global_row = row_id * parent_rows + jnp.arange(parent_rows)
-    kept = jnp.where((global_row < PANEL)[:, None], assembled, updated)
-    result = kept
-    for i in range(lead):
-        result = jnp.where(
-            own_column == i, parent_factor[:, i * BLOCK : (i + 1) * BLOCK], result
-        )
+    update = jnp.where((global_row < PANEL)[:, None], 0.0, matmul_tn(band_upper, upper))
+    in_panel = own_column < lead
+    start = jnp.minimum(own_column, lead - 1) * BLOCK
+    panel = lax.dynamic_slice_in_dim(band_upper, start, BLOCK, 0).T
+    base = jnp.where(in_panel, panel, parent - update)
+    slots = jnp.where(in_panel, -1, at(row_slot, row_id, 2)).reshape(-1)
+    result = place_blocks(slots, base, arrived)
     return (factor[None], result[:, None, None, :])
 
 

time: 436 us -> 298 us (0.68)
  waiting for transfers between devices: 216 us -> 122 us
  blocking collectives: 116 us -> 22.4 us
  between operations: 1.53 us -> 24.4 us
  starting transfers between devices: 35.7 us -> 45.4 us
  local copies, waits for them, and re-layouts: 12.9 us -> 20.1 us
  Pallas kernels: 44.7 us -> 49.5 us
    all_to_all x7, waiting for transfers between devices: 216 us -> 29.3 us  [exchange(): return lax.all_to_all(value, axes, split_axis=0, concat_axis=0, tiled=True)]
    all_to_all x4 -> x2, blocking collectives: 116 us -> 22.4 us  [exchange(): return lax.all_to_all(value, axes, split_axis=0, concat_axis=0, tiled=True)]
    all_gather x0 -> x3, waiting for transfers between devices: none -> 92.3 us  [the longest x1 51.9 us: per_device(): every_leaf = lax.all_gather(top, 'leaf')]
    ppermute x0 -> x2, starting transfers between devices: none -> 6.01 us  [gather_col(): other = lax.ppermute(along, 'col_1', [(0, 1), (1, 0)])]
    unnamed x16 -> x19, local copies, waits for them, and re-layouts: 1.4 us -> 6.76 us
  transfers between devices with their start and end apart: 7 -> 12, of which waited for: 6 -> 9; matrix products, arithmetic and copies ran while one was open for 2% -> 9% of each run, Pallas kernels for 4% -> 11%
where the time goes in v2:
time: 298 us; the launch traced here: 296 us
  waiting for transfers between devices  122 us (41%)
  Pallas kernels  49.5 us (17%)
  starting transfers between devices  45.4 us (15%)
  between operations  24.4 us (8%)
  blocking collectives  22.4 us (8%)
  local copies, waits for them, and re-layouts  20.1 us (7%)
  matrix products  6.48 us (2%)
  other arithmetic  4.78 us (2%)
    all_gather x1, waiting for transfers between devices, per_device(): every_leaf = lax.all_gather(top, 'leaf')  51.9 us
    all_to_all x7, starting transfers between devices, exchange(): return lax.all_to_all(value, axes, split_axis=0, concat_axis=0, tiled=True)  39.3 us
    all_gather x1, waiting for transfers between devices, per_device(): every_col = lax.all_gather(pair, COL)  29.7 us
    all_to_all x7, waiting for transfers between devices, exchange(): return lax.all_to_all(value, axes, split_axis=0, concat_axis=0, tiled=True)  29.3 us
    pallas_call x2, Pallas kernels, lower_inverse(): pl.pallas_call(inverse_kernel, out_shape=jax.ShapeDtypeStruct((size, size...  24.7 us
    all_to_all x2, blocking collectives, exchange(): return lax.all_to_all(value, axes, split_axis=0, concat_axis=0, tiled=True)  22.4 us
    pallas_call x1, Pallas kernels, schur_pieces(): pl.pallas_call(schur_kernel, out_shape=jax.ShapeDtypeStruct((leaves * ban...  12.1 us
    all_gather x1, waiting for transfers between devices, per_device(): blocks = lax.all_gather(mine, 'row')  10.7 us
  transfers between devices with their start and end apart: 12, of which 9 were waited for; matrix products, arithmetic and copies ran while one was open for 9% of the time, Pallas kernels for 11%

profile of v2, /device:TPU:1, one launch (start us, length us, event | category | flops | bytes accessed | tf_op | source)
XLA Modules:
  0.0 295.5 jit_solution(6351867212912484993)
XLA Ops:
  9.1 10.2 %all-to-all-start = ((f32[8,64,256]{2,1,0:T(8,128)}), f32[8,64,256]{2,1,0:T(8,128)S(1)}, u32[]{:S(2)}, u32[]{:S(2)}) async-start(f32[8,64,256]{2,1,0:T(8,128)} %bitcast.3), calls=%async_computation | async-start | bytes 1048576 | tf_op jit(solution)/shard_map/all_to_all | solution.py:45
  19.7 9.0 %all-to-all-done = f32[8,64,256]{2,1,0:T(8,128)S(1)} async-done(((f32[8,64,256]{2,1,0:T(8,128)}), f32[8,64,256]{2,1,0:T(8,128)S(1)}, u32[]{:S(2)}, u32[]{:S(2)}) %all-to-all-start) | async-done | bytes 524320 | tf_op jit(solution)/shard_map/all_to_all | solution.py:45
  29.4 3.4 %all-to-all-start.1 = ((f32[4,64,256]{2,1,0:T(8,128)}), f32[4,64,256]{2,1,0:T(8,128)S(1)}, u32[]{:S(2)}, u32[]{:S(2)}) async-start(f32[4,64,256]{2,1,0:T(8,128)} %broadcast_in_dim.126), calls=%async_computation.1 | async-start | bytes 524288 | tf_op jit(solution)/shard_map/all_to_all | solution.py:45
  33.2 5.2 %all-to-all-done.1 = f32[4,64,256]{2,1,0:T(8,128)S(1)} async-done(((f32[4,64,256]{2,1,0:T(8,128)}), f32[4,64,256]{2,1,0:T(8,128)S(1)}, u32[]{:S(2)}, u32[]{:S(2)}) %all-to-all-start.1) | async-done | bytes 262176 | tf_op jit(solution)/shard_map/all_to_all | solution.py:45
  38.4 4.0 %collective-permute-start = (f32[4,64,256]{2,1,0:T(8,128)S(1)}, f32[4,64,256]{2,1,0:T(8,128)S(1)}, u32[]{:S(2)}, u32[]{:S(2)}) collective-permute-start(f32[4,64,256]{2,1,0:T(8,128)S(1)} %all-to-all-done.1), channel_id=1, source_target_pairs={{0,1},{1,0},{2,3},{3,2},{4,5},{5,4},{6,7},{7,6},{8,9},{9,8},{10,11... | collective-permute-start | bytes 786440 | tf_op jit(solution)/shard_map/ppermute | solution.py:224
  43.1 5.6 %all-to-all-start.2 = ((f32[8,32,256]{2,1,0:T(8,128)}), f32[8,32,256]{2,1,0:T(8,128)S(1)}, u32[]{:S(2)}, u32[]{:S(2)}) async-start(f32[8,32,256]{2,1,0:T(8,128)} %broadcast_in_dim.128), calls=%async_computation.2 | async-start | bytes 524288 | tf_op jit(solution)/shard_map/all_to_all | solution.py:45
  49.2 6.5 %pick_columns.1 = f32[8,512,128]{2,1,0:T(8,128)} custom-call(s32[8]{0:T(128)} %fusion.19.index_ref, f32[512,512]{1,0:T(8,128)} %bitcast.119), custom_call_target="tpu_custom_call" | custom-call | tf_op jit(solution)/shard_map/pick_columns/pallas_call | solution.py:129
  57.1 4.0 %all-to-all-done.2 = f32[8,32,256]{2,1,0:T(8,128)S(1)} async-done(((f32[8,32,256]{2,1,0:T(8,128)}), f32[8,32,256]{2,1,0:T(8,128)S(1)}, u32[]{:S(2)}, u32[]{:S(2)}) %all-to-all-start.2) | async-done | bytes 262176 | tf_op jit(solution)/shard_map/all_to_all | solution.py:45
  61.7 3.3 %all-to-all-start.3 = ((f32[4,32,256]{2,1,0:T(8,128)}), f32[4,32,256]{2,1,0:T(8,128)S(1)}, u32[]{:S(2)}, u32[]{:S(2)}) async-start(f32[4,32,256]{2,1,0:T(8,128)} %broadcast_in_dim.130), calls=%async_computation.3 | async-start | bytes 262144 | tf_op jit(solution)/shard_map/all_to_all | solution.py:45
  65.7 4.1 %all-to-all-done.3 = f32[4,32,256]{2,1,0:T(8,128)S(1)} async-done(((f32[4,32,256]{2,1,0:T(8,128)}), f32[4,32,256]{2,1,0:T(8,128)S(1)}, u32[]{:S(2)}, u32[]{:S(2)}) %all-to-all-start.3) | async-done | bytes 131104 | tf_op jit(solution)/shard_map/all_to_all | solution.py:45
  69.8 5.1 %all-to-all-start.4 = ((f32[8,512,128]{2,1,0:T(8,128)}), f32[8,512,128]{2,1,0:T(8,128)S(1)}, u32[]{:S(2)}, u32[]{:S(2)}) async-start(f32[8,512,128]{2,1,0:T(8,128)} %pick_columns.1), calls=%async_computation.4 | async-start | bytes 4194304 | tf_op jit(solution)/shard_map/all_to_all | solution.py:45
  81.2 12.3 %lower_inverse.2.inverse_ref = f32[256,256]{1,0:T(8,128)} custom-call(f32[256,256]{1,0:T(8,128)} %bitcast.126), custom_call_target="tpu_custom_call" | custom-call | tf_op jit(solution)/shard_map/lower_inverse/pallas_call | solution.py:114
  95.9 5.3 %all-to-all-done.4.cols_ref = f32[8,512,128]{2,1,0:T(8,128)S(1)} async-done(((f32[8,512,128]{2,1,0:T(8,128)}), f32[8,512,128]{2,1,0:T(8,128)S(1)}, u32[]{:S(2)}, u32[]{:S(2)}) %all-to-all-start.4) | async-done | bytes 2097184 | tf_op jit(solution)/shard_map/all_to_all | solution.py:45
  101.2 10.7 %all-gather.8.cloned.1.call-done = f32[1024,256]{1,0:T(8,128)} async-done(((f32[128,256]{1,0:T(8,128)}), f32[1024,256]{1,0:T(8,128)}) %all-gather.8.cloned.1.call-update) | async-done | bytes 1048592 | tf_op jit(solution)/shard_map/all_gather | solution.py:266
  111.9 12.1 %schur_pieces.1 = f32[64,128,128]{2,1,0:T(8,128)} custom-call(s32[8]{0:T(128)} %select_reduce_fusion.4.slot_ref, s32[8]{0:T(128)} %convert_element_type.3.live_ref, s32[8]{0:T(128)} %fusion.18.piece_ref, f32[8,512,128]{2,1,0:T(8,128)} %copy-done, f32[512,256]{1,0:T(8,128)} %fusion.21.factor_ref, f32[256,256]{1,0:T(8,128)} %lower_inverse.2.inverse_ref, ...), custom_call_target="tpu_custom_call" | custom-call | tf_op jit(solution)/shard_map/schur_pieces/pallas_call | solution.py:156
  126.0 5.3 %all-to-all-start.5 = ((f32[8,128,128]{2,1,0:T(8,128)}), f32[8,128,128]{2,1,0:T(8,128)S(1)}, u32[]{:S(2)}, u32[]{:S(2)}) async-start(f32[8,128,128]{2,1,0:T(8,128)} %slice_bitcast_fusion), calls=%async_computation.5 | async-start | bytes 1048576 | tf_op jit(solution)/shard_map/all_to_all | solution.py:45
  143.8 11.5 %all_to_all.45 = f32[8,32,128]{2,1,0:T(8,128)S(1)} all-to-all(f32[8,32,128]{2,1,0:T(8,128)S(1)} %add.163), channel_id=1, replica_groups=mesh['leaf'=8,'row'=8,'col_0'=4,'col_1'=2] {'row'}, dimensions={0} | all-to-all | bytes 262144 | tf_op jit(solution)/shard_map/all_to_all | solution.py:45
  155.3 11.0 %all_to_all.46 = f32[8,32,128]{2,1,0:T(8,128)} all-to-all(f32[8,32,128]{2,1,0:T(8,128)S(1)} %broadcast_in_dim.143), channel_id=1, replica_groups=mesh['leaf'=8,'row'=8,'col_0'=4,'col_1'=2] {'row'}, dimensions={0} | all-to-all | bytes 262144 | tf_op jit(solution)/shard_map/all_to_all | solution.py:45
  166.3 6.4 %all-to-all-start.8 = ((f32[64,128,128]{2,1,0:T(8,128)}), f32[64,128,128]{2,1,0:T(8,128)}, u32[]{:S(2)}, u32[]{:S(2)}) async-start(f32[64,128,128]{2,1,0:T(8,128)} %schur_pieces.1), calls=%async_computation.8 | async-start | bytes 8388608 | tf_op jit(solution)/shard_map/all_to_all | solution.py:45
  172.7 51.9 %all-gather.6.cloned.1.call-done = f32[8,256,128]{2,1,0:T(8,128)} async-done(((f32[1,256,128]{2,1,0:T(8,128)}), f32[8,256,128]{2,1,0:T(8,128)}) %all-gather.6.cloned.1.call-update) | async-done | bytes 1048592 | tf_op jit(solution)/shard_map/all_gather | solution.py:306
  227.3 29.7 %all-gather.10.cloned.1.call-done = f32[16,256,128]{2,1,0:T(8,128)} async-done(((f32[2,256,128]{2,1,0:T(8,128)}), f32[16,256,128]{2,1,0:T(8,128)}) %all-gather.10.cloned.1.call-update) | async-done | bytes 2097168 | tf_op jit(solution)/shard_map/all_gather | solution.py:308
  258.7 12.4 %lower_inverse.3 = f32[256,256]{1,0:T(8,128)} custom-call(f32[256,256]{1,0:T(8,128)} %pad_maximum_fusion.3.corner_ref), custom_call_target="tpu_custom_call" | custom-call | tf_op jit(solution)/shard_map/lower_inverse/pallas_call | solution.py:114
  280.2 2.7 fusion.1.parent_ref
  282.9 6.2 %place_blocks.1 = f32[1024,128]{1,0:T(8,128)} custom-call(s32[64]{0:T(128)} %select_n.272.slot_ref, f32[1024,128]{1,0:T(8,128)} %fusion.1.parent_ref, f32[64,128,128]{2,1,0:T(8,128)} %all-to-all-done.8.blocks_ref), custom_call_target="tpu_custom_call" | custom-call | tf_op jit(solution)/shard_map/place_blocks/pallas_call | solution.py:196
  (88 shorter events, 33.2 us)
Async XLA Ops:
  7.2 12.2 %copy-start.4 = (s32[8,30]{1,0:T(8,128)S(1)}, s32[8,30]{1,0:T(8,128)}, u32[]{:S(2)}) copy-start(s32[8,30]{1,0:T(8,128)} %param.5) | copy-start | bytes 2884
  9.1 19.6 %all-to-all-start = ((f32[8,64,256]{2,1,0:T(8,128)}), f32[8,64,256]{2,1,0:T(8,128)S(1)}, u32[]{:S(2)}, u32[]{:S(2)}) async-start(f32[8,64,256]{2,1,0:T(8,128)} %bitcast.3), calls=%async_computation | async-start | bytes 1048576 | tf_op jit(solution)/shard_map/all_to_all | solution.py:45
  29.4 8.9 %all-to-all-start.1 = ((f32[4,64,256]{2,1,0:T(8,128)}), f32[4,64,256]{2,1,0:T(8,128)S(1)}, u32[]{:S(2)}, u32[]{:S(2)}) async-start(f32[4,64,256]{2,1,0:T(8,128)} %broadcast_in_dim.126), calls=%async_computation.1 | async-start | bytes 524288 | tf_op jit(solution)/shard_map/all_to_all | solution.py:45
  38.4 18.5 %collective-permute-start = (f32[4,64,256]{2,1,0:T(8,128)S(1)}, f32[4,64,256]{2,1,0:T(8,128)S(1)}, u32[]{:S(2)}, u32[]{:S(2)}) collective-permute-start(f32[4,64,256]{2,1,0:T(8,128)S(1)} %all-to-all-done.1), channel_id=1, source_target_pairs={{0,1},{1,0},{2,3},{3,2},{4,5},{5,4},{6,7},{7,6},{8,9},{9,8},{10,11... | collective-permute-start | bytes 786440 | tf_op jit(solution)/shard_map/ppermute | solution.py:224
  43.1 17.9 %all-to-all-start.2 = ((f32[8,32,256]{2,1,0:T(8,128)}), f32[8,32,256]{2,1,0:T(8,128)S(1)}, u32[]{:S(2)}, u32[]{:S(2)}) async-start(f32[8,32,256]{2,1,0:T(8,128)} %broadcast_in_dim.128), calls=%async_computation.2 | async-start | bytes 524288 | tf_op jit(solution)/shard_map/all_to_all | solution.py:45
  61.7 8.1 %all-to-all-start.3 = ((f32[4,32,256]{2,1,0:T(8,128)}), f32[4,32,256]{2,1,0:T(8,128)S(1)}, u32[]{:S(2)}, u32[]{:S(2)}) async-start(f32[4,32,256]{2,1,0:T(8,128)} %broadcast_in_dim.130), calls=%async_computation.3 | async-start | bytes 262144 | tf_op jit(solution)/shard_map/all_to_all | solution.py:45
  69.8 31.3 %all-to-all-start.4 = ((f32[8,512,128]{2,1,0:T(8,128)}), f32[8,512,128]{2,1,0:T(8,128)S(1)}, u32[]{:S(2)}, u32[]{:S(2)}) async-start(f32[8,512,128]{2,1,0:T(8,128)} %pick_columns.1), calls=%async_computation.4 | async-start | bytes 4194304 | tf_op jit(solution)/shard_map/all_to_all | solution.py:45
  75.0 37.0 %all-gather.8.cloned.1.call-start = ((), (), s32[]{:S(2)}) async-start(), calls=%async_computation.10 | async-start | bytes 1179648 | tf_op jit(solution)/shard_map/all_gather | solution.py:266
  76.6 3.8 %collective-permute-start.1 = (f32[4,32,256]{2,1,0:T(8,128)S(1)}, f32[4,32,256]{2,1,0:T(8,128)S(1)}, u32[]{:S(2)}, u32[]{:S(2)}) collective-permute-start(f32[4,32,256]{2,1,0:T(8,128)S(1)} %all-to-all-done.3), channel_id=1, source_target_pairs={{0,1},{1,0},{2,3},{3,2},{4,5},{5,4},{6,7},{7,6},{8,9},{9,8},{10,11... | collective-permute-start | bytes 393224 | tf_op jit(solution)/shard_map/ppermute | solution.py:224
  101.2 10.7 %copy-start = (f32[8,512,128]{2,1,0:T(8,128)}, f32[8,512,128]{2,1,0:T(8,128)S(1)}, u32[]{:S(2)}) copy-start(f32[8,512,128]{2,1,0:T(8,128)S(1)} %all-to-all-done.4.cols_ref) | copy-start | bytes 6291460
  124.1 17.7 %copy-start.3 = (f32[1024,1,1,128]{3,2,1,0:T(1,128)S(1)}, f32[1024,1,1,128]{3,2,1,0:T(1,128)}, u32[]{:S(2)}) copy-start(f32[1024,1,1,128]{3,2,1,0:T(1,128)} %param.4) | copy-start | bytes 1572868
  126.0 17.6 %all-to-all-start.5 = ((f32[8,128,128]{2,1,0:T(8,128)}), f32[8,128,128]{2,1,0:T(8,128)S(1)}, u32[]{:S(2)}, u32[]{:S(2)}) async-start(f32[8,128,128]{2,1,0:T(8,128)} %slice_bitcast_fusion), calls=%async_computation.5 | async-start | bytes 1048576 | tf_op jit(solution)/shard_map/all_to_all | solution.py:45
  131.3 93.3 %all-gather.6.cloned.1.call-start = ((), (), s32[]{:S(2)}) async-start(), calls=%async_computation.9 | async-start | bytes 1179648 | tf_op jit(solution)/shard_map/all_gather | solution.py:306
  166.3 116.6 %all-to-all-start.8 = ((f32[64,128,128]{2,1,0:T(8,128)}), f32[64,128,128]{2,1,0:T(8,128)}, u32[]{:S(2)}, u32[]{:S(2)}) async-start(f32[64,128,128]{2,1,0:T(8,128)} %schur_pieces.1), calls=%async_computation.8 | async-start | bytes 8388608 | tf_op jit(solution)/shard_map/all_to_all | solution.py:45
  172.7 84.3 %all-gather.10.cloned.1.call-start = ((), (), s32[]{:S(2)}) async-start(), calls=%async_computation.11 | async-start | bytes 2359296 | tf_op jit(solution)/shard_map/all_gather | solution.py:308
  271.0 7.4 %copy-start.1 = (f32[256,256]{1,0:T(8,128)S(1)}, f32[256,256]{1,0:T(8,128)}, u32[]{:S(2)}) copy-start(f32[256,256]{1,0:T(8,128)} %lower_inverse.3) | copy-start | bytes 786436
  278.5 1.3 copy-start.2
Sparse Core Ops, SparseCore 0:
  77.8 34.0 all-gather.7
  166.4 58.1 all-gather.5
  227.3 29.5 all-gather.9

commit v3 on v2

--- a/solution.py
+++ b/solution.py
@@ -90,12 +90,12 @@
     return work[:, step:width] * lax.rsqrt(pivots)[:, :step]
 
 
-def inverse_kernel(corner_ref, out_ref, work_ref):
-    size = corner_ref.shape[0]
+def invert(corner, out_ref, work_ref):
+    size = corner.shape[0]
     step = STEP
     row = lax.broadcasted_iota(jnp.int32, (size, size), 0)
     col = lax.broadcasted_iota(jnp.int32, (size, size), 1)
-    work_ref[:, :size] = corner_ref[...]
+    work_ref[:, :size] = corner
     work_ref[:, size:] = (row == col).astype(jnp.float32)
     small_row = lax.broadcasted_iota(jnp.int32, (step, step), 0)
     small_col = lax.broadcasted_iota(jnp.int32, (step, step), 1)
@@ -109,6 +109,10 @@
             work_ref[stop:, :] = work_ref[stop:, :] - matmul_tn(upper[:, stop:size], upper)
 
 
+def inverse_kernel(corner_ref, out_ref, work_ref):
+    invert(corner_ref[...], out_ref, work_ref)
+
+
 def lower_inverse(corner):
     size = corner.shape[0]
     return pl.pallas_call(
@@ -117,6 +121,54 @@
         scratch_shapes=[pltpu.VMEM((size, 2 * size), jnp.float32)],
         name="lower_inverse",
     )(corner)
+
+
+def parent_kernel(where_ref, tops_ref, top_ref, parent_ref, out_ref, inverse_ref, work_ref):
+    row_id, own_column = where_ref[0], where_ref[1]
+    lead = PANEL // BLOCK
+    blocks = tops_ref.shape[0]
+    corner = jnp.concatenate([tops_ref[i, 1] for i in range(lead)], axis=1)
+    invert(corner, inverse_ref, work_ref)
+
+    @pl.when(own_column >= lead)
+    def _():
+        upper = matmul(inverse_ref[...], top_ref[...])
+
+        def body(block, carry):
+            part = pl.ds(pl.multiple_of(block * BLOCK, BLOCK), BLOCK)
+            change = matmul_tn(matmul(inverse_ref[...], tops_ref[block, 0]), upper)
+            first = (row_id == 0) & (block < lead)
+            out_ref[part, :] = parent_ref[part, :] - jnp.where(first, 0.0, change)
+            return carry
+
+        lax.fori_loop(0, blocks, body, 0)
+
+    @pl.when(own_column < lead)
+    def _():
+        start = pl.multiple_of(jnp.minimum(own_column, lead - 1) * BLOCK, BLOCK)
+        rows = inverse_ref[pl.ds(start, BLOCK), :]
+
+        def body(block, carry):
+            part = pl.ds(pl.multiple_of(block * BLOCK, BLOCK), BLOCK)
+            out_ref[part, :] = matmul(rows, tops_ref[block, 0]).T
+            return carry
+
+        lax.fori_loop(0, blocks, body, 0)
+
+
+def parent_base(where, tops, top, parent):
+    vmem = pl.BlockSpec(memory_space=pltpu.VMEM)
+    return pl.pallas_call(
+        parent_kernel,
+        out_shape=jax.ShapeDtypeStruct(parent.shape, jnp.float32),
+        in_specs=[pl.BlockSpec(memory_space=pltpu.SMEM), vmem, vmem, vmem],
+        out_specs=vmem,
+        scratch_shapes=[
+            pltpu.VMEM((PANEL, PANEL), jnp.float32),
+            pltpu.VMEM((PANEL, 2 * PANEL), jnp.float32),
+        ],
+        name="parent_base",
+    )(where, tops, top, parent)
 
 
 def pick_kernel(index_ref, front_ref, out_ref):
@@ -139,74 +191,99 @@
     )(index, front)
 
 
-def schur_kernel(slot_ref, live_ref, piece_ref, cols_ref, factor_ref, inverse_ref, block_ref, out_ref, tmp):
-    @pl.when(live_ref[pl.program_id(0)] > 0)
-    def _():
-        block = matmul_nt(block_ref[0], inverse_ref[...])
-        tmp[...] = cols_ref[0] - matmul_nt(factor_ref[...], block)
-        for dest in range(out_ref.shape[0]):
-            start = pl.multiple_of(piece_ref[dest] * BLOCK, BLOCK)
-            out_ref[dest] = tmp[pl.ds(start, BLOCK), :]
-
-
-def schur_pieces(slot, live, piece, cols, factor, inverse, blocks):
+def schur_kernel(
+    slot_ref, live_ref, piece_ref, valid_ref, cols_ref, factor_ref, inverse_ref, block_ref,
+    out_ref, top_ref, tmp_ref, sems, top_sems,
+):
+    leaves = live_ref.shape[0]
+    bands = valid_ref.shape[0]
+
+    def copies(leaf, dest):
+        start = pl.multiple_of(piece_ref[dest] * BLOCK, BLOCK)
+        piece = tmp_ref.at[leaf, pl.ds(start, BLOCK), :]
+        item = leaf * bands + dest
+        yield pltpu.make_async_copy(piece, out_ref.at[item], sems.at[item])
+        if dest == 0:
+            yield pltpu.make_async_copy(piece, top_ref.at[leaf], top_sems.at[leaf])
+
+    def each(leaf, act):
+        for dest in range(bands):
+
+            @pl.when(valid_ref[dest] > 0)
+            def _(dest=dest):
+                for copy in copies(leaf, dest):
+                    act(copy)
+
+    def start(leaf, carry):
+        @pl.when(live_ref[leaf] > 0)
+        def _():
+            slot = slot_ref[leaf]
+            block = matmul_nt(block_ref[slot], inverse_ref[...])
+            tmp_ref[leaf] = cols_ref[slot] - matmul_nt(factor_ref[...], block)
+            each(leaf, lambda copy: copy.start())
+
+        return carry
+
+    def finish(leaf, carry):
+        @pl.when(live_ref[leaf] > 0)
+        def _():
+            each(leaf, lambda copy: copy.wait())
+
+        return carry
+
+    lax.fori_loop(0, leaves, start, 0)
+    lax.fori_loop(0, leaves, finish, 0)
+
+
+def schur_pieces(slot, live, piece, valid, cols, factor, inverse, blocks):
     leaves = slot.shape[0]
     bands = piece.shape[0]
-    rows, panel = factor.shape
+    rows = factor.shape[0]
+    smem = pl.BlockSpec(memory_space=pltpu.SMEM)
+    vmem = pl.BlockSpec(memory_space=pltpu.VMEM)
+    anywhere = pl.BlockSpec(memory_space=pl.ANY)
     return pl.pallas_call(
         schur_kernel,
-        out_shape=jax.ShapeDtypeStruct((leaves * bands, BLOCK, BLOCK), jnp.float32),
-        grid_spec=pltpu.PrefetchScalarGridSpec(
-            num_scalar_prefetch=3,
-            grid=(leaves,),
-            in_specs=[
-                pl.BlockSpec((1, rows, BLOCK), lambda i, s, v, p: (s[i], 0, 0)),
-                pl.BlockSpec((rows, panel), lambda i, s, v, p: (0, 0)),
-                pl.BlockSpec((panel, panel), lambda i, s, v, p: (0, 0)),
-                pl.BlockSpec((1, BLOCK, panel), lambda i, s, v, p: (s[i], 0, 0)),
-            ],
-            out_specs=pl.BlockSpec((bands, BLOCK, BLOCK), lambda i, s, v, p: (i, 0, 0)),
-            scratch_shapes=[pltpu.VMEM((rows, BLOCK), jnp.float32)],
+        out_shape=(
+            jax.ShapeDtypeStruct((leaves * bands, BLOCK, BLOCK), jnp.float32),
+            jax.ShapeDtypeStruct((leaves, BLOCK, BLOCK), jnp.float32),
         ),
+        in_specs=[smem] * 4 + [vmem] * 4,
+        out_specs=(anywhere, anywhere),
+        scratch_shapes=[
+            pltpu.VMEM((leaves, rows, BLOCK), jnp.float32),
+            pltpu.SemaphoreType.DMA((leaves * bands,)),
+            pltpu.SemaphoreType.DMA((leaves,)),
+        ],
         name="schur_pieces",
-    )(slot, live, piece, cols, factor, inverse, blocks)
-
-
-def place_kernel(slot_ref, parent_ref, blocks_ref, out_ref):
-    step = pl.program_id(0)
-
-    @pl.when(step == 0)
-    def _():
-        out_ref[...] = parent_ref[...]
-
-    count = blocks_ref.shape[0]
-    for item in range(count):
-        slot = slot_ref[step * count + item]
+    )(slot, live, piece, valid, cols, factor, inverse, blocks)
+
+
+def place_kernel(slot_ref, base_ref, blocks_ref, out_ref):
+    out_ref[...] = base_ref[...]
+
+    def body(item, carry):
+        slot = slot_ref[item]
 
         @pl.when(slot >= 0)
-        def _(item=item, slot=slot):
+        def _():
             start = pl.multiple_of(slot * BLOCK, BLOCK)
             out_ref[pl.ds(start, BLOCK), :] += blocks_ref[item]
 
-
-def place_blocks(slots, parent, blocks):
-    total = blocks.shape[0]
-    batch = 8
-    rows = parent.shape[0]
+        return carry
+
+    lax.fori_loop(0, blocks_ref.shape[0], body, 0)
+
+
+def place_blocks(slots, base, blocks):
+    vmem = pl.BlockSpec(memory_space=pltpu.VMEM)
     return pl.pallas_call(
         place_kernel,
-        out_shape=jax.ShapeDtypeStruct(parent.shape, jnp.float32),
-        grid_spec=pltpu.PrefetchScalarGridSpec(
-            num_scalar_prefetch=1,
-            grid=(total // batch,),
-            in_specs=[
-                pl.BlockSpec((rows, BLOCK), lambda i, slots: (0, 0)),
-                pl.BlockSpec((batch, BLOCK, BLOCK), lambda i, slots: (i, 0, 0)),
-            ],
-            out_specs=pl.BlockSpec((rows, BLOCK), lambda i, slots: (0, 0)),
-        ),
+        out_shape=jax.ShapeDtypeStruct(base.shape, jnp.float32),
+        in_specs=[pl.BlockSpec(memory_space=pltpu.SMEM), vmem, vmem],
+        out_specs=vmem,
         name="place_blocks",
-    )(slots, parent, blocks)
+    )(slots, base, blocks)
 
 
 def locate(values, usable, count):
@@ -219,16 +296,35 @@
     return lax.dynamic_index_in_dim(value, index, axis, keepdims=False)
 
 
-def gather_col(value):
-    along = spread(value, "col_0", lax.axis_size("col_0"))
+def ordered(value, other, first):
+    return jnp.concatenate([jnp.where(first, value, other), jnp.where(first, other, value)])
+
+
+def swapped_core(along):
     other = lax.ppermute(along, "col_1", [(0, 1), (1, 0)])
     first = lax.axis_index("col_1") == 0
     both = jnp.stack([jnp.where(first, along, other), jnp.where(first, other, along)], axis=1)
-    return both.reshape(-1, *value.shape)
-
-
-def side_by_side(blocks):
-    return jnp.concatenate([blocks[i] for i in range(blocks.shape[0])], axis=1)
+    return both.reshape(-1, *along.shape[1:])
+
+
+def gather_col_permuted(value):
+    index = lax.axis_index("col_0")
+    along = value[None]
+    for bit in range(2):
+        other = lax.ppermute(along, "col_0", [(i, i ^ (1 << bit)) for i in range(4)])
+        along = ordered(along, other, (index >> bit) % 2 == 0)
+    return swapped_core(along)
+
+
+def from_first_row(value):
+    index = lax.axis_index("row")
+    stride = lax.axis_size("row") // 2
+    while stride:
+        pairs = [(i, i + stride) for i in range(0, lax.axis_size("row"), 2 * stride)]
+        other = lax.ppermute(value, "row", pairs)
+        value = jnp.where(index % (2 * stride) == stride, other, value)
+        stride //= 2
+    return value
 
 
 def per_device(child_front, parent_front, block_map):
@@ -259,12 +355,15 @@
     share = PANEL // grid_cols
     deals = front[:, :PANEL].reshape(-1, grid_cols, share, PANEL).transpose(1, 0, 2, 3)
     deal = exchange(deals.reshape(grid_cols, -1, PANEL), COL)[0]
-    corner = gather_col(spread(deal[:share], "row", grid_rows)[0]).reshape(PANEL, PANEL)
-    raw = gather_col(deal).reshape(grid_cols, -1, share, PANEL)
+    corner = gather_col_permuted(from_first_row(deal[:share])).reshape(PANEL, PANEL)
+    along = spread(deal, "col_0", lax.axis_size("col_0"))
+    picked = pick_columns(at(own_lo_index, col_id), front)
+    picked, along = lax.optimization_barrier((picked, along))
+    raw = swapped_core(along).reshape(grid_cols, -1, share, PANEL)
     raw = raw.transpose(1, 0, 2, 3).reshape(rows, PANEL)
     mine = lax.dynamic_slice_in_dim(raw, at(column_index, row_id) * BLOCK, BLOCK, 0)
     blocks = lax.all_gather(mine, "row")
-    cols = exchange(pick_columns(at(own_lo_index, col_id), front), COL)
+    cols = exchange(picked, COL)
     inverse = lower_inverse(corner)
     factor = matmul_nt(raw, inverse)
 
@@ -272,10 +371,11 @@
         jnp.where(jnp.arange(child_blocks) == column_index[:, None], at(band, leaf_id), 0), axis=-1
     )
     slot, slot_valid = locate(column_band, column_valid, leaves)
-    pieces = schur_pieces(
+    pieces, tops = schur_pieces(
         slot,
         slot_valid.astype(jnp.int32),
         at(at(hi_index, leaf_id), row_id),
+        at(at(hi_valid, leaf_id), row_id).astype(jnp.int32),
         cols,
         factor,
         inverse,
@@ -290,7 +390,7 @@
     )
     row_slot = jnp.where(hi_valid & present[:, None, None], row_slot, -1).astype(jnp.int32)
 
-    tops = exchange(pieces.reshape(leaves, grid_rows, BLOCK, BLOCK)[:, 0], "leaf")
+    tops = exchange(tops, "leaf")
     top_slot = at(row_slot, row_id, 1)[:, 0]
     top = jnp.where(row_id == 0, parent[:PANEL], 0.0).reshape(lead, BLOCK, BLOCK)
     top = top + jnp.stack(
@@ -306,17 +406,8 @@
     every_leaf = lax.all_gather(top, "leaf")
     pair = jnp.stack([at(every_leaf, row_id), every_leaf[0]])
     every_col = lax.all_gather(pair, COL)
-    band_top = side_by_side(every_col[:, 0])
-    inverse_parent = lower_inverse(side_by_side(every_col[:lead, 1]))
-    band_upper = matmul(inverse_parent, band_top)
-    upper = matmul(inverse_parent, top)
-    global_row = row_id * parent_rows + jnp.arange(parent_rows)
-    update = jnp.where((global_row < PANEL)[:, None], 0.0, matmul_tn(band_upper, upper))
-    in_panel = own_column < lead
-    start = jnp.minimum(own_column, lead - 1) * BLOCK
-    panel = lax.dynamic_slice_in_dim(band_upper, start, BLOCK, 0).T
-    base = jnp.where(in_panel, panel, parent - update)
-    slots = jnp.where(in_panel, -1, at(row_slot, row_id, 2)).reshape(-1)
+    base = parent_base(jnp.stack([row_id, own_column]).astype(jnp.int32), every_col, top, parent)
+    slots = jnp.where(own_column < lead, -1, at(row_slot, row_id, 2)).reshape(-1)
     result = place_blocks(slots, base, arrived)
     return (factor[None], result[:, None, None, :])
 

time: 298 us -> 307 us (1.030)
  waiting for transfers between devices: 122 us -> 137 us
  local copies, waits for them, and re-layouts: 20.1 us -> 9.52 us
  starting transfers between devices: 45.4 us -> 54.2 us
  matrix products: 6.48 us -> 2.36 us
    ppermute x2 -> x7, waiting for transfers between devices: 0.01 us -> 22.9 us  [the longest x2 22.9 us: gather_col_permuted(): other = lax.ppermute(along, 'col_0', [(i, i ^ 1 << bit) for i in range(4)])]
    ppermute x2 -> x7, starting transfers between devices: 6.01 us -> 24.5 us  [the longest x3 8.73 us: from_first_row(): other = lax.ppermute(value, 'row', pairs)]
    all_to_all x7 -> x5, waiting for transfers between devices: 29.3 us -> 12.4 us  [exchange(): return lax.all_to_all(value, axes, split_axis=0, concat_axis=0, tiled=True)]
    pallas_call x2 -> x1, Pallas kernels: 24.7 us -> 12.3 us  [lower_inverse(): pl.pallas_call(inverse_kernel, out_shape=jax.ShapeDtypeStruct((size, size...]
    all_gather x1, waiting for transfers between devices: 10.7 us -> 0.01 us  [per_device(): blocks = lax.all_gather(mine, 'row')]
    pallas_call x2 -> x3, Pallas kernels: 18.3 us -> 28.8 us  [the longest x1 16 us: parent_base(): pl.pallas_call(parent_kernel, out_shape=jax.ShapeDtypeStruct(parent.shape...]
    all_gather x1, waiting for transfers between devices: 51.9 us -> 62.1 us  [per_device(): every_leaf = lax.all_gather(top, 'leaf')]
    all_to_all x7 -> x5, starting transfers between devices: 39.3 us -> 29.7 us  [exchange(): return lax.all_to_all(value, axes, split_axis=0, concat_axis=0, tiled=True)]
  transfers between devices with their start and end apart: 12 -> 15, of which waited for: 9 -> 7; matrix products, arithmetic and copies ran while one was open for 9% -> 5% of each run, Pallas kernels for 11% -> 11%
where the time goes in v3:
time: 307 us; the launch traced here: 302 us
  waiting for transfers between devices  137 us (45%)
  starting transfers between devices  54.2 us (18%)
  Pallas kernels  47.1 us (15%)
  between operations  24.4 us (8%)
  blocking collectives  21.7 us (7%)
  local copies, waits for them, and re-layouts  9.52 us (3%)
  other arithmetic  6.18 us (2%)
    all_gather x1, waiting for transfers between devices, per_device(): every_leaf = lax.all_gather(top, 'leaf')  62.1 us
    all_gather x1, waiting for transfers between devices, per_device(): every_col = lax.all_gather(pair, COL)  38.4 us
    all_to_all x5, starting transfers between devices, exchange(): return lax.all_to_all(value, axes, split_axis=0, concat_axis=0, tiled=True)  29.7 us
    ppermute x2, waiting for transfers between devices, gather_col_permuted(): other = lax.ppermute(along, 'col_0', [(i, i ^ 1 << bit) for i in range(4)])  22.9 us
    all_to_all x2, blocking collectives, exchange(): return lax.all_to_all(value, axes, split_axis=0, concat_axis=0, tiled=True)  21.7 us
    pallas_call x1, Pallas kernels, parent_base(): pl.pallas_call(parent_kernel, out_shape=jax.ShapeDtypeStruct(parent.shape...  16 us
    all_to_all x5, waiting for transfers between devices, exchange(): return lax.all_to_all(value, axes, split_axis=0, concat_axis=0, tiled=True)  12.4 us
    pallas_call x1, Pallas kernels, lower_inverse(): pl.pallas_call(inverse_kernel, out_shape=jax.ShapeDtypeStruct((size, size...  12.3 us
  transfers between devices with their start and end apart: 15, of which 7 were waited for; matrix products, arithmetic and copies ran while one was open for 5% of the time, Pallas kernels for 11%

profile of v3, /device:TPU:1, one launch (start us, length us, event | category | flops | bytes accessed | tf_op | source)
XLA Modules:
  0.0 302.2 jit_solution(3854709641653226888)
XLA Ops:
  9.1 10.2 %all-to-all-start = ((f32[8,64,256]{2,1,0:T(8,128)}), f32[8,64,256]{2,1,0:T(8,128)S(1)}, u32[]{:S(2)}, u32[]{:S(2)}) async-start(f32[8,64,256]{2,1,0:T(8,128)} %bitcast.5), calls=%async_computation | async-start | bytes 1048576 | tf_op jit(solution)/shard_map/all_to_all | solution.py:45
  20.7 5.9 %pick_columns.1 = f32[8,512,128]{2,1,0:T(8,128)} custom-call(s32[8]{0:T(128)} %fusion.10.index_ref, f32[512,512]{1,0:T(8,128)} %bitcast.77), custom_call_target="tpu_custom_call" | custom-call | tf_op jit(solution)/shard_map/pick_columns/pallas_call | solution.py:181
  27.0 1.7 all-to-all-done
  28.7 6.1 %collective-permute-start.1 = (f32[32,256]{1,0:T(8,128)S(1)}, f32[32,256]{1,0:T(8,128)S(1)}, u32[]{:S(2)}, u32[]{:S(2)}) collective-permute-start(f32[32,256]{1,0:T(8,128)S(1)} %slice_bitcast_fusion.1), channel_id=1, source_target_pairs={{0,32},{1,33},{2,34},{3,35},{4,36},{5,37},{6,38},{7,39},{64,96},{6... | collective-permute-start | bytes 98312 | tf_op jit(solution)/shard_map/ppermute | solution.py:324
  35.6 3.4 %all-to-all-start.1 = ((f32[4,64,256]{2,1,0:T(8,128)}), f32[4,64,256]{2,1,0:T(8,128)S(1)}, u32[]{:S(2)}, u32[]{:S(2)}) async-start(f32[4,64,256]{2,1,0:T(8,128)} %broadcast_in_dim.101), calls=%async_computation.1 | async-start | bytes 524288 | tf_op jit(solution)/shard_map/all_to_all | solution.py:45
  40.3 4.2 %all-to-all-done.1 = f32[4,64,256]{2,1,0:T(8,128)S(1)} async-done(((f32[4,64,256]{2,1,0:T(8,128)}), f32[4,64,256]{2,1,0:T(8,128)S(1)}, u32[]{:S(2)}, u32[]{:S(2)}) %all-to-all-start.1) | async-done | bytes 262176 | tf_op jit(solution)/shard_map/all_to_all | solution.py:45
  44.5 4.3 %collective-permute-start = (f32[4,64,256]{2,1,0:T(8,128)S(1)}, f32[4,64,256]{2,1,0:T(8,128)S(1)}, u32[]{:S(2)}, u32[]{:S(2)}) collective-permute-start(f32[4,64,256]{2,1,0:T(8,128)S(1)} %all-to-all-done.1), channel_id=1, source_target_pairs={{0,1},{1,0},{2,3},{3,2},{4,5},{5,4},{6,7},{7,6},{8,9},{9,8},{10,11... | collective-permute-start | bytes 786440 | tf_op jit(solution)/shard_map/ppermute | solution.py:304
  51.6 3.6 %all-to-all-start.2 = ((f32[8,512,128]{2,1,0:T(8,128)}), f32[8,512,128]{2,1,0:T(8,128)S(1)}, u32[]{:S(2)}, u32[]{:S(2)}) async-start(f32[8,512,128]{2,1,0:T(8,128)} %pick_columns.1), calls=%async_computation.2 | async-start | bytes 4194304 | tf_op jit(solution)/shard_map/all_to_all | solution.py:45
  56.1 3.2 %collective-permute-start.4 = (f32[1,32,256]{2,1,0:T(8,128)S(1)}, f32[1,32,256]{2,1,0:T(8,128)S(1)}, u32[]{:S(2)}, u32[]{:S(2)}) collective-permute-start(f32[1,32,256]{2,1,0:T(8,128)S(1)} %select_bitcast_fusion.4), channel_id=1, source_target_pairs={{0,2},{2,0},{4,6},{6,4},{1,3},{3,1},{5,7},{7,5},{8,10},{10,8},{12,... | collective-permute-start | bytes 98312 | tf_op jit(solution)/shard_map/ppermute | solution.py:314
  59.4 21.2 %collective-permute-done.4 = f32[1,32,256]{2,1,0:T(8,128)S(1)} collective-permute-done((f32[1,32,256]{2,1,0:T(8,128)S(1)}, f32[1,32,256]{2,1,0:T(8,128)S(1)}, u32[]{:S(2)}, u32[]{:S(2)}) %collective-permute-start.4) | collective-permute-done | bytes 32800 | tf_op jit(solution)/shard_map/ppermute | solution.py:314
  80.7 4.3 %collective-permute-start.5 = (f32[2,32,256]{2,1,0:T(8,128)S(1)}, f32[2,32,256]{2,1,0:T(8,128)S(1)}, u32[]{:S(2)}, u32[]{:S(2)}) collective-permute-start(f32[2,32,256]{2,1,0:T(8,128)S(1)} %pad_maximum_fusion.5), channel_id=1, source_target_pairs={{0,4},{2,6},{4,0},{6,2},{1,5},{3,7},{5,1},{7,3},{8,12},{10,14},{12... | collective-permute-start | bytes 196616 | tf_op jit(solution)/shard_map/ppermute | solution.py:314
  87.2 3.9 %collective-permute-start.6 = (f32[4,32,256]{2,1,0:T(8,128)S(1)}, f32[4,32,256]{2,1,0:T(8,128)S(1)}, u32[]{:S(2)}, u32[]{:S(2)}) collective-permute-start(f32[4,32,256]{2,1,0:T(8,128)S(1)} %pad_maximum_fusion.3), channel_id=1, source_target_pairs={{0,1},{1,0},{2,3},{3,2},{4,5},{5,4},{6,7},{7,6},{8,9},{9,8},{10,11... | collective-permute-start | bytes 393224 | tf_op jit(solution)/shard_map/ppermute | solution.py:304
  93.7 12.3 %lower_inverse.1.inverse_ref = f32[256,256]{1,0:T(8,128)} custom-call(f32[256,256]{1,0:T(8,128)} %bitcast.85), custom_call_target="tpu_custom_call" | custom-call | tf_op jit(solution)/shard_map/lower_inverse/pallas_call | solution.py:118
  106.1 2.4 fusion.13.factor_ref
  109.8 8.7 %schur_pieces.1 = (f32[64,128,128]{2,1,0:T(8,128)}, f32[8,128,128]{2,1,0:T(8,128)}) custom-call(s32[8]{0:T(128)} %select_reduce_fusion.4.slot_ref, s32[8]{0:T(128)} %convert_element_type.8.live_ref, s32[8]{0:T(128)} %fusion.11.piece_ref, s32[8]{0:T(128)} %fusion.9.valid_ref, f32[8,512,128]{2,1,0:T(8,128)} %copy-done, f32[512,256]{1,0:T(8,128)} %fusion.13.factor_ref, ...), custom_call_target="tpu_custom_call" | custom-call | tf_op jit(solution)/shard_map/schur_pieces/pallas_call | solution.py:245
  118.5 6.8 %all-to-all-start.3 = ((f32[8,128,128]{2,1,0:T(8,128)}), f32[8,128,128]{2,1,0:T(8,128)S(1)}, u32[]{:S(2)}, u32[]{:S(2)}) async-start(f32[8,128,128]{2,1,0:T(8,128)} %get-tuple-element.8), calls=%async_computation.3 | async-start | bytes 1048576 | tf_op jit(solution)/shard_map/all_to_all | solution.py:45
  136.7 6.6 %all-to-all-done.3 = f32[8,128,128]{2,1,0:T(8,128)S(1)} async-done(((f32[8,128,128]{2,1,0:T(8,128)}), f32[8,128,128]{2,1,0:T(8,128)S(1)}, u32[]{:S(2)}, u32[]{:S(2)}) %all-to-all-start.3) | async-done | bytes 524320 | tf_op jit(solution)/shard_map/all_to_all | solution.py:45
  143.4 10.6 %all_to_all.35 = f32[8,32,128]{2,1,0:T(8,128)S(1)} all-to-all(f32[8,32,128]{2,1,0:T(8,128)S(1)} %add.177), channel_id=1, replica_groups=mesh['leaf'=8,'row'=8,'col_0'=4,'col_1'=2] {'row'}, dimensions={0} | all-to-all | bytes 262144 | tf_op jit(solution)/shard_map/all_to_all | solution.py:45
  154.0 11.2 %all_to_all.36 = f32[8,32,128]{2,1,0:T(8,128)} all-to-all(f32[8,32,128]{2,1,0:T(8,128)S(1)} %broadcast_in_dim.112), channel_id=1, replica_groups=mesh['leaf'=8,'row'=8,'col_0'=4,'col_1'=2] {'row'}, dimensions={0} | all-to-all | bytes 262144 | tf_op jit(solution)/shard_map/all_to_all | solution.py:45
  165.2 5.7 %all-to-all-start.6 = ((f32[64,128,128]{2,1,0:T(8,128)}), f32[64,128,128]{2,1,0:T(8,128)}, u32[]{:S(2)}, u32[]{:S(2)}) async-start(f32[64,128,128]{2,1,0:T(8,128)} %get-tuple-element.9), calls=%async_computation.6 | async-start | bytes 8388608 | tf_op jit(solution)/shard_map/all_to_all | solution.py:45
  171.7 62.1 %all-gather.6.cloned.1.call-done = f32[8,256,128]{2,1,0:T(8,128)} async-done(((f32[1,256,128]{2,1,0:T(8,128)}), f32[8,256,128]{2,1,0:T(8,128)}) %all-gather.6.cloned.1.call-update) | async-done | bytes 1048592 | tf_op jit(solution)/shard_map/all_gather | solution.py:406
  237.1 38.4 %all-gather.10.cloned.1.call-done = f32[16,256,128]{2,1,0:T(8,128)} async-done(((f32[2,256,128]{2,1,0:T(8,128)}), f32[16,256,128]{2,1,0:T(8,128)}) %all-gather.10.cloned.1.call-update) | async-done | bytes 2097168 | tf_op jit(solution)/shard_map/all_gather | solution.py:408
  275.5 16.0 %parent_base.1.base_ref = f32[1024,128]{1,0:T(8,128)} custom-call(s32[2]{0:T(128)} %pad_add_fusion.where_ref, f32[8,2,256,128]{3,2,1,0:T(8,128)} %bitcast.79, f32[256,128]{1,0:T(8,128)} %bitcast.83, f32[1024,128]{1,0:T(8,128)} %bitcast.86), custom_call_target="tpu_custom_call" | custom-call | tf_op jit(solution)/shard_map/parent_base/pallas_call | solution.py:161
  291.5 4.1 %place_blocks.1 = f32[1024,128]{1,0:T(8,128)} custom-call(s32[64]{0:T(128)} %select_n.348.slot_ref, f32[1024,128]{1,0:T(8,128)} %parent_base.1.base_ref, f32[64,128,128]{2,1,0:T(8,128)} %all-to-all-done.6.blocks_ref), custom_call_target="tpu_custom_call" | custom-call | tf_op jit(solution)/shard_map/place_blocks/pallas_call | solution.py:280
  (77 shorter events, 20.8 us)
Async XLA Ops:
  7.2 12.2 %copy-start.1 = (s32[8,30]{1,0:T(8,128)S(1)}, s32[8,30]{1,0:T(8,128)}, u32[]{:S(2)}) copy-start(s32[8,30]{1,0:T(8,128)} %param.5) | copy-start | bytes 2884
  9.1 19.6 %all-to-all-start = ((f32[8,64,256]{2,1,0:T(8,128)}), f32[8,64,256]{2,1,0:T(8,128)S(1)}, u32[]{:S(2)}, u32[]{:S(2)}) async-start(f32[8,64,256]{2,1,0:T(8,128)} %bitcast.5), calls=%async_computation | async-start | bytes 1048576 | tf_op jit(solution)/shard_map/all_to_all | solution.py:45
  28.7 10.3 %collective-permute-start.1 = (f32[32,256]{1,0:T(8,128)S(1)}, f32[32,256]{1,0:T(8,128)S(1)}, u32[]{:S(2)}, u32[]{:S(2)}) collective-permute-start(f32[32,256]{1,0:T(8,128)S(1)} %slice_bitcast_fusion.1), channel_id=1, source_target_pairs={{0,32},{1,33},{2,34},{3,35},{4,36},{5,37},{6,38},{7,39},{64,96},{6... | collective-permute-start | bytes 98312 | tf_op jit(solution)/shard_map/ppermute | solution.py:324
  35.6 8.9 %all-to-all-start.1 = ((f32[4,64,256]{2,1,0:T(8,128)}), f32[4,64,256]{2,1,0:T(8,128)S(1)}, u32[]{:S(2)}, u32[]{:S(2)}) async-start(f32[4,64,256]{2,1,0:T(8,128)} %broadcast_in_dim.101), calls=%async_computation.1 | async-start | bytes 524288 | tf_op jit(solution)/shard_map/all_to_all | solution.py:45
  39.0 11.3 %collective-permute-start.2 = (f32[32,256]{1,0:T(8,128)S(1)}, f32[32,256]{1,0:T(8,128)S(1)}, u32[]{:S(2)}, u32[]{:S(2)}) collective-permute-start(f32[32,256]{1,0:T(8,128)S(1)} %broadcast_select_fusion.3), channel_id=1, source_target_pairs={{0,16},{32,48},{1,17},{33,49},{2,18},{34,50},{3,19},{35,51},{4,20}... | collective-permute-start | bytes 98312 | tf_op jit(solution)/shard_map/ppermute | solution.py:324
  44.5 10.7 %collective-permute-start = (f32[4,64,256]{2,1,0:T(8,128)S(1)}, f32[4,64,256]{2,1,0:T(8,128)S(1)}, u32[]{:S(2)}, u32[]{:S(2)}) collective-permute-start(f32[4,64,256]{2,1,0:T(8,128)S(1)} %all-to-all-done.1), channel_id=1, source_target_pairs={{0,1},{1,0},{2,3},{3,2},{4,5},{5,4},{6,7},{7,6},{8,9},{9,8},{10,11... | collective-permute-start | bytes 786440 | tf_op jit(solution)/shard_map/ppermute | solution.py:304
  50.3 5.8 %collective-permute-start.3 = (f32[32,256]{1,0:T(8,128)S(1)}, f32[32,256]{1,0:T(8,128)S(1)}, u32[]{:S(2)}, u32[]{:S(2)}) collective-permute-start(f32[32,256]{1,0:T(8,128)S(1)} %broadcast_select_fusion.4), channel_id=1, source_target_pairs={{0,8},{16,24},{32,40},{48,56},{1,9},{17,25},{33,41},{49,57},{2,10}... | collective-permute-start | bytes 98312 | tf_op jit(solution)/shard_map/ppermute | solution.py:324
  51.6 56.8 %all-to-all-start.2 = ((f32[8,512,128]{2,1,0:T(8,128)}), f32[8,512,128]{2,1,0:T(8,128)S(1)}, u32[]{:S(2)}, u32[]{:S(2)}) async-start(f32[8,512,128]{2,1,0:T(8,128)} %pick_columns.1), calls=%async_computation.2 | async-start | bytes 4194304 | tf_op jit(solution)/shard_map/all_to_all | solution.py:45
  55.2 53.2 %all-gather.8.cloned.1.call-start = ((), (), s32[]{:S(2)}) async-start(), calls=%async_computation.8 | async-start | bytes 1179648 | tf_op jit(solution)/shard_map/all_gather | solution.py:365
  56.1 24.6 %collective-permute-start.4 = (f32[1,32,256]{2,1,0:T(8,128)S(1)}, f32[1,32,256]{2,1,0:T(8,128)S(1)}, u32[]{:S(2)}, u32[]{:S(2)}) collective-permute-start(f32[1,32,256]{2,1,0:T(8,128)S(1)} %select_bitcast_fusion.4), channel_id=1, source_target_pairs={{0,2},{2,0},{4,6},{6,4},{1,3},{3,1},{5,7},{7,5},{8,10},{10,8},{12,... | collective-permute-start | bytes 98312 | tf_op jit(solution)/shard_map/ppermute | solution.py:314
  80.7 6.5 %collective-permute-start.5 = (f32[2,32,256]{2,1,0:T(8,128)S(1)}, f32[2,32,256]{2,1,0:T(8,128)S(1)}, u32[]{:S(2)}, u32[]{:S(2)}) collective-permute-start(f32[2,32,256]{2,1,0:T(8,128)S(1)} %pad_maximum_fusion.5), channel_id=1, source_target_pairs={{0,4},{2,6},{4,0},{6,2},{1,5},{3,7},{5,1},{7,3},{8,12},{10,14},{12... | collective-permute-start | bytes 196616 | tf_op jit(solution)/shard_map/ppermute | solution.py:314
  87.2 5.7 %collective-permute-start.6 = (f32[4,32,256]{2,1,0:T(8,128)S(1)}, f32[4,32,256]{2,1,0:T(8,128)S(1)}, u32[]{:S(2)}, u32[]{:S(2)}) collective-permute-start(f32[4,32,256]{2,1,0:T(8,128)S(1)} %pad_maximum_fusion.3), channel_id=1, source_target_pairs={{0,1},{1,0},{2,3},{3,2},{4,5},{5,4},{6,7},{7,6},{8,9},{9,8},{10,11... | collective-permute-start | bytes 393224 | tf_op jit(solution)/shard_map/ppermute | solution.py:304
  108.4 1.3 copy-start
  118.5 24.8 %all-to-all-start.3 = ((f32[8,128,128]{2,1,0:T(8,128)}), f32[8,128,128]{2,1,0:T(8,128)S(1)}, u32[]{:S(2)}, u32[]{:S(2)}) async-start(f32[8,128,128]{2,1,0:T(8,128)} %get-tuple-element.8), calls=%async_computation.3 | async-start | bytes 1048576 | tf_op jit(solution)/shard_map/all_to_all | solution.py:45
  165.2 126.4 %all-to-all-start.6 = ((f32[64,128,128]{2,1,0:T(8,128)}), f32[64,128,128]{2,1,0:T(8,128)}, u32[]{:S(2)}, u32[]{:S(2)}) async-start(f32[64,128,128]{2,1,0:T(8,128)} %get-tuple-element.9), calls=%async_computation.6 | async-start | bytes 8388608 | tf_op jit(solution)/shard_map/all_to_all | solution.py:45
  170.9 62.9 %all-gather.6.cloned.1.call-start = ((), (), s32[]{:S(2)}) async-start(), calls=%async_computation.7 | async-start | bytes 1179648 | tf_op jit(solution)/shard_map/all_gather | solution.py:406
  171.6 103.9 %all-gather.10.cloned.1.call-start = ((), (), s32[]{:S(2)}) async-start(), calls=%async_computation.9 | async-start | bytes 2359296 | tf_op jit(solution)/shard_map/all_gather | solution.py:408
Sparse Core Ops, SparseCore 0:
  58.1 33.6 all-gather.7
  173.8 60.0 all-gather.5
  236.5 38.9 all-gather.9

commit v4 on v3

--- a/solution.py
+++ b/solution.py
@@ -296,24 +296,11 @@
     return lax.dynamic_index_in_dim(value, index, axis, keepdims=False)
 
 
-def ordered(value, other, first):
-    return jnp.concatenate([jnp.where(first, value, other), jnp.where(first, other, value)])
-
-
 def swapped_core(along):
     other = lax.ppermute(along, "col_1", [(0, 1), (1, 0)])
     first = lax.axis_index("col_1") == 0
     both = jnp.stack([jnp.where(first, along, other), jnp.where(first, other, along)], axis=1)
     return both.reshape(-1, *along.shape[1:])
-
-
-def gather_col_permuted(value):
-    index = lax.axis_index("col_0")
-    along = value[None]
-    for bit in range(2):
-        other = lax.ppermute(along, "col_0", [(i, i ^ (1 << bit)) for i in range(4)])
-        along = ordered(along, other, (index >> bit) % 2 == 0)
-    return swapped_core(along)
 
 
 def from_first_row(value):
@@ -352,17 +339,20 @@
     column_index = at(own_lo_index, col_id, 1)
     column_valid = at(own_lo_valid, col_id, 1)
 
+    parent_top = lax.all_gather(parent[:PANEL], "row")[0]
     share = PANEL // grid_cols
     deals = front[:, :PANEL].reshape(-1, grid_cols, share, PANEL).transpose(1, 0, 2, 3)
     deal = exchange(deals.reshape(grid_cols, -1, PANEL), COL)[0]
-    corner = gather_col_permuted(from_first_row(deal[:share])).reshape(PANEL, PANEL)
     along = spread(deal, "col_0", lax.axis_size("col_0"))
+    corner = spread(from_first_row(deal[:share]), "col_0", lax.axis_size("col_0"))
     picked = pick_columns(at(own_lo_index, col_id), front)
-    picked, along = lax.optimization_barrier((picked, along))
     raw = swapped_core(along).reshape(grid_cols, -1, share, PANEL)
     raw = raw.transpose(1, 0, 2, 3).reshape(rows, PANEL)
     mine = lax.dynamic_slice_in_dim(raw, at(column_index, row_id) * BLOCK, BLOCK, 0)
+    mine, parent_top = lax.optimization_barrier((mine, parent_top))
     blocks = lax.all_gather(mine, "row")
+    picked, corner, mine = lax.optimization_barrier((picked, corner, mine))
+    corner = swapped_core(corner).reshape(PANEL, PANEL)
     cols = exchange(picked, COL)
     inverse = lower_inverse(corner)
     factor = matmul_nt(raw, inverse)
@@ -390,17 +380,10 @@
     )
     row_slot = jnp.where(hi_valid & present[:, None, None], row_slot, -1).astype(jnp.int32)
 
-    tops = exchange(tops, "leaf")
-    top_slot = at(row_slot, row_id, 1)[:, 0]
-    top = jnp.where(row_id == 0, parent[:PANEL], 0.0).reshape(lead, BLOCK, BLOCK)
-    top = top + jnp.stack(
-        [
-            sum(jnp.where(top_slot[c] == i, tops[c], 0.0) for c in range(leaves))
-            for i in range(lead)
-        ]
-    )
-    top = jnp.sum(exchange(top.reshape(grid_rows, -1, BLOCK), "row"), axis=0)
-    top = spread(top, "row", grid_rows).reshape(PANEL, BLOCK)
+    tops = exchange(tops.reshape(leaves * grid_rows, -1, BLOCK), LEAF_ROW)
+    chosen = row_slot[:, :, 0].reshape(-1) == jnp.arange(lead)[:, None]
+    top = jnp.sum(jnp.where(chosen[:, :, None, None], tops, 0.0), axis=1)
+    top = spread(top, "row", grid_rows).transpose(1, 0, 2, 3).reshape(PANEL, BLOCK) + parent_top
     arrived = exchange(pieces, LEAF_ROW)
 
     every_leaf = lax.all_gather(top, "leaf")

time: 307 us -> 291 us (0.948)
  blocking collectives: 21.7 us -> 11.5 us
  between operations: 24.4 us -> 14.6 us
  local copies, waits for them, and re-layouts: 9.52 us -> 12.9 us
    ppermute x2 -> x0, waiting for transfers between devices: 22.9 us -> none  [gather_col_permuted(): other = lax.ppermute(along, 'col_0', [(i, i ^ 1 << bit) for i in range(4)])]
    all_to_all x5 -> x6, waiting for transfers between devices: 12.4 us -> 30 us  [exchange(): return lax.all_to_all(value, axes, split_axis=0, concat_axis=0, tiled=True)]
    all_gather x1, waiting for transfers between devices: 0.01 us -> 11.3 us  [per_device(): blocks = lax.all_gather(mine, 'row')]
    all_to_all x2 -> x1, blocking collectives: 21.7 us -> 11.5 us  [exchange(): return lax.all_to_all(value, axes, split_axis=0, concat_axis=0, tiled=True)]
    ppermute x2 -> x0, starting transfers between devices: 7.51 us -> none  [gather_col_permuted(): other = lax.ppermute(along, 'col_0', [(i, i ^ 1 << bit) for i in range(4)])]
    all_gather x1, waiting for transfers between devices: 38.4 us -> 30.9 us  [per_device(): every_col = lax.all_gather(pair, COL)]
    all_to_all x5 -> x6, starting transfers between devices: 29.7 us -> 36.2 us  [exchange(): return lax.all_to_all(value, axes, split_axis=0, concat_axis=0, tiled=True)]
    all_gather x1, waiting for transfers between devices: 62.1 us -> 65.6 us  [per_device(): every_leaf = lax.all_gather(top, 'leaf')]
  transfers between devices with their start and end apart: 15 -> 15, of which waited for: 7 -> 8; matrix products, arithmetic and copies ran while one was open for 5% -> 6% of each run, Pallas kernels for 11% -> 12%
where the time goes in v4:
time: 291 us; the launch traced here: 286 us
  waiting for transfers between devices  139 us (48%)
  starting transfers between devices  51.9 us (18%)
  Pallas kernels  47.5 us (16%)
  between operations  14.6 us (5%)
  local copies, waits for them, and re-layouts  12.9 us (4%)
  blocking collectives  11.5 us (4%)
  other arithmetic  5.98 us (2%)
    all_gather x1, waiting for transfers between devices, per_device(): every_leaf = lax.all_gather(top, 'leaf')  65.6 us
    all_to_all x6, starting transfers between devices, exchange(): return lax.all_to_all(value, axes, split_axis=0, concat_axis=0, tiled=True)  36.2 us
    all_gather x1, waiting for transfers between devices, per_device(): every_col = lax.all_gather(pair, COL)  30.9 us
    all_to_all x6, waiting for transfers between devices, exchange(): return lax.all_to_all(value, axes, split_axis=0, concat_axis=0, tiled=True)  30 us
    pallas_call x1, Pallas kernels, parent_base(): pl.pallas_call(parent_kernel, out_shape=jax.ShapeDtypeStruct(parent.shape...  16 us
    pallas_call x1, Pallas kernels, lower_inverse(): pl.pallas_call(inverse_kernel, out_shape=jax.ShapeDtypeStruct((size, size...  12.3 us
    all_to_all x1, blocking collectives, exchange(): return lax.all_to_all(value, axes, split_axis=0, concat_axis=0, tiled=True)  11.5 us
    all_gather x1, waiting for transfers between devices, per_device(): blocks = lax.all_gather(mine, 'row')  11.3 us
  transfers between devices with their start and end apart: 15, of which 8 were waited for; matrix products, arithmetic and copies ran while one was open for 6% of the time, Pallas kernels for 12%

profile of v4, /device:TPU:1, one launch (start us, length us, event | category | flops | bytes accessed | tf_op | source)
XLA Modules:
  0.0 285.6 jit_solution(13526995341150480115)
XLA Ops:
  7.2 1.6 slice.39
  10.7 10.2 %all-to-all-start = ((f32[8,64,256]{2,1,0:T(8,128)}), f32[8,64,256]{2,1,0:T(8,128)S(1)}, u32[]{:S(2)}, u32[]{:S(2)}) async-start(f32[8,64,256]{2,1,0:T(8,128)} %bitcast.3), calls=%async_computation | async-start | bytes 1048576 | tf_op jit(solution)/shard_map/all_to_all | solution.py:45
  21.5 8.8 %all-to-all-done = f32[8,64,256]{2,1,0:T(8,128)S(1)} async-done(((f32[8,64,256]{2,1,0:T(8,128)}), f32[8,64,256]{2,1,0:T(8,128)S(1)}, u32[]{:S(2)}, u32[]{:S(2)}) %all-to-all-start) | async-done | bytes 524320 | tf_op jit(solution)/shard_map/all_to_all | solution.py:45
  30.3 6.1 %collective-permute-start.1 = (f32[32,256]{1,0:T(8,128)S(1)}, f32[32,256]{1,0:T(8,128)S(1)}, u32[]{:S(2)}, u32[]{:S(2)}) collective-permute-start(f32[32,256]{1,0:T(8,128)S(1)} %slice_bitcast_fusion.3), channel_id=1, source_target_pairs={{0,32},{1,33},{2,34},{3,35},{4,36},{5,37},{6,38},{7,39},{64,96},{6... | collective-permute-start | bytes 98312 | tf_op jit(solution)/shard_map/ppermute | solution.py:311
  39.6 3.4 %all-to-all-start.1 = ((f32[4,64,256]{2,1,0:T(8,128)}), f32[4,64,256]{2,1,0:T(8,128)S(1)}, u32[]{:S(2)}, u32[]{:S(2)}) async-start(f32[4,64,256]{2,1,0:T(8,128)} %broadcast_in_dim.97), calls=%async_computation.1 | async-start | bytes 524288 | tf_op jit(solution)/shard_map/all_to_all | solution.py:45
  44.3 4.2 %all-to-all-done.1 = f32[4,64,256]{2,1,0:T(8,128)S(1)} async-done(((f32[4,64,256]{2,1,0:T(8,128)}), f32[4,64,256]{2,1,0:T(8,128)S(1)}, u32[]{:S(2)}, u32[]{:S(2)}) %all-to-all-start.1) | async-done | bytes 262176 | tf_op jit(solution)/shard_map/all_to_all | solution.py:45
  48.5 4.8 %collective-permute-start = (f32[4,64,256]{2,1,0:T(8,128)S(1)}, f32[4,64,256]{2,1,0:T(8,128)S(1)}, u32[]{:S(2)}, u32[]{:S(2)}) collective-permute-start(f32[4,64,256]{2,1,0:T(8,128)S(1)} %all-to-all-done.1), channel_id=1, source_target_pairs={{0,1},{1,0},{2,3},{3,2},{4,5},{5,4},{6,7},{7,6},{8,9},{9,8},{10,11... | collective-permute-start | bytes 786440 | tf_op jit(solution)/shard_map/ppermute | solution.py:300
  55.0 6.4 %pick_columns.1 = f32[8,512,128]{2,1,0:T(8,128)} custom-call(s32[8]{0:T(128)} %fusion.10.index_ref, f32[512,512]{1,0:T(8,128)} %bitcast.64), custom_call_target="tpu_custom_call" | custom-call | tf_op jit(solution)/shard_map/pick_columns/pallas_call | solution.py:181
  62.0 3.3 %all-to-all-start.2 = ((f32[4,32,256]{2,1,0:T(8,128)}), f32[4,32,256]{2,1,0:T(8,128)S(1)}, u32[]{:S(2)}, u32[]{:S(2)}) async-start(f32[4,32,256]{2,1,0:T(8,128)} %broadcast_in_dim.100), calls=%async_computation.2 | async-start | bytes 262144 | tf_op jit(solution)/shard_map/all_to_all | solution.py:45
  67.2 3.3 %all-to-all-done.2 = f32[4,32,256]{2,1,0:T(8,128)S(1)} async-done(((f32[4,32,256]{2,1,0:T(8,128)}), f32[4,32,256]{2,1,0:T(8,128)S(1)}, u32[]{:S(2)}, u32[]{:S(2)}) %all-to-all-start.2) | async-done | bytes 131104 | tf_op jit(solution)/shard_map/all_to_all | solution.py:45
  70.4 3.8 %all-to-all-start.3 = ((f32[8,512,128]{2,1,0:T(8,128)}), f32[8,512,128]{2,1,0:T(8,128)S(1)}, u32[]{:S(2)}, u32[]{:S(2)}) async-start(f32[8,512,128]{2,1,0:T(8,128)} %pick_columns.1), calls=%async_computation.3 | async-start | bytes 4194304 | tf_op jit(solution)/shard_map/all_to_all | solution.py:45
  75.6 2.0 collective-permute-start.4
  80.2 12.3 %lower_inverse.1.inverse_ref = f32[256,256]{1,0:T(8,128)} custom-call(f32[256,256]{1,0:T(8,128)} %bitcast.70), custom_call_target="tpu_custom_call" | custom-call | tf_op jit(solution)/shard_map/lower_inverse/pallas_call | solution.py:118
  92.5 2.4 fusion.12.factor_ref
  94.9 11.3 %all-gather.11.cloned.1.call-done = f32[1024,256]{1,0:T(8,128)} async-done(((f32[128,256]{1,0:T(8,128)}), f32[1024,256]{1,0:T(8,128)}) %all-gather.11.cloned.1.call-update) | async-done | bytes 1048592 | tf_op jit(solution)/shard_map/all_gather | solution.py:353
  107.6 8.7 %schur_pieces.1 = (f32[64,128,128]{2,1,0:T(8,128)}, f32[8,128,128]{2,1,0:T(8,128)}) custom-call(s32[8]{0:T(128)} %select_reduce_fusion.5.slot_ref, s32[8]{0:T(128)} %convert_element_type.8.live_ref, s32[8]{0:T(128)} %fusion.11.piece_ref, s32[8]{0:T(128)} %fusion.9.valid_ref, f32[8,512,128]{2,1,0:T(8,128)} %copy-done, f32[512,256]{1,0:T(8,128)} %fusion.12.factor_ref, ...), custom_call_target="tpu_custom_call" | custom-call | tf_op jit(solution)/shard_map/schur_pieces/pallas_call | solution.py:245
  116.3 9.7 %all-to-all-start.4 = ((f32[64,16,128]{2,1,0:T(8,128)}), f32[64,16,128]{2,1,0:T(8,128)S(1)}, u32[]{:S(2)}, u32[]{:S(2)}) async-start(f32[64,16,128]{2,1,0:T(8,128)} %bitcast.73), calls=%async_computation.4 | async-start | bytes 1048576 | tf_op jit(solution)/shard_map/all_to_all | solution.py:45
  126.6 13.7 %all-to-all-done.4 = f32[64,16,128]{2,1,0:T(8,128)S(1)} async-done(((f32[64,16,128]{2,1,0:T(8,128)}), f32[64,16,128]{2,1,0:T(8,128)S(1)}, u32[]{:S(2)}, u32[]{:S(2)}) %all-to-all-start.4) | async-done | bytes 524320 | tf_op jit(solution)/shard_map/all_to_all | solution.py:45
  140.6 11.5 %all_to_all.35 = f32[8,2,16,128]{3,2,1,0:T(8,128)S(1)} all-to-all(f32[8,2,16,128]{3,2,1,0:T(8,128)S(1)} %broadcast_in_dim.111), channel_id=1, replica_groups=mesh['leaf'=8,'row'=8,'col_0'=4,'col_1'=2] {'row'}, dimensions={0} | all-to-all | bytes 262144 | tf_op jit(solution)/shard_map/all_to_all | solution.py:45
  152.1 5.7 %all-to-all-start.6 = ((f32[64,128,128]{2,1,0:T(8,128)}), f32[64,128,128]{2,1,0:T(8,128)}, u32[]{:S(2)}, u32[]{:S(2)}) async-start(f32[64,128,128]{2,1,0:T(8,128)} %get-tuple-element.13), calls=%async_computation.6 | async-start | bytes 8388608 | tf_op jit(solution)/shard_map/all_to_all | solution.py:45
  158.6 65.6 %all-gather.13.cloned.1.call-done = f32[2048,128]{1,0:T(8,128)} async-done(((f32[256,128]{1,0:T(8,128)}), f32[2048,128]{1,0:T(8,128)}) %all-gather.13.cloned.1.call-update) | async-done | bytes 1048592 | tf_op jit(solution)/shard_map/all_gather | solution.py:389
  228.1 30.9 %all-gather.15.cloned.1.call-done = f32[16,256,128]{2,1,0:T(8,128)} async-done(((f32[2,256,128]{2,1,0:T(8,128)}), f32[16,256,128]{2,1,0:T(8,128)}) %all-gather.15.cloned.1.call-update) | async-done | bytes 2097168 | tf_op jit(solution)/shard_map/all_gather | solution.py:391
  259.0 16.0 %parent_base.1.base_ref = f32[1024,128]{1,0:T(8,128)} custom-call(s32[2]{0:T(128)} %pad_add_fusion.where_ref, f32[8,2,256,128]{3,2,1,0:T(8,128)} %bitcast.66, f32[256,128]{1,0:T(8,128)} %bitcast_add_fusion.top_ref, f32[1024,128]{1,0:T(8,128)} %bitcast.72), custom_call_target="tpu_custom_call" | custom-call | tf_op jit(solution)/shard_map/parent_base/pallas_call | solution.py:161
  275.0 4.1 %place_blocks.1 = f32[1024,128]{1,0:T(8,128)} custom-call(s32[64]{0:T(128)} %select_n.185.slot_ref, f32[1024,128]{1,0:T(8,128)} %parent_base.1.base_ref, f32[64,128,128]{2,1,0:T(8,128)} %all-to-all-done.6.blocks_ref), custom_call_target="tpu_custom_call" | custom-call | tf_op jit(solution)/shard_map/place_blocks/pallas_call | solution.py:280
  (74 shorter events, 21.0 us)
Async XLA Ops:
  7.2 13.8 %copy-start.1 = (s32[8,30]{1,0:T(8,128)S(1)}, s32[8,30]{1,0:T(8,128)}, u32[]{:S(2)}) copy-start(s32[8,30]{1,0:T(8,128)} %param.5) | copy-start | bytes 2884
  7.2 59.1 %all-gather.9.cloned.1.call-start = ((), (), s32[]{:S(2)}) async-start(), calls=%async_computation.7 | async-start | bytes 1179648 | tf_op jit(solution)/shard_map/all_gather | solution.py:342
  10.7 19.6 %all-to-all-start = ((f32[8,64,256]{2,1,0:T(8,128)}), f32[8,64,256]{2,1,0:T(8,128)S(1)}, u32[]{:S(2)}, u32[]{:S(2)}) async-start(f32[8,64,256]{2,1,0:T(8,128)} %bitcast.3), calls=%async_computation | async-start | bytes 1048576 | tf_op jit(solution)/shard_map/all_to_all | solution.py:45
  30.3 7.2 %collective-permute-start.1 = (f32[32,256]{1,0:T(8,128)S(1)}, f32[32,256]{1,0:T(8,128)S(1)}, u32[]{:S(2)}, u32[]{:S(2)}) collective-permute-start(f32[32,256]{1,0:T(8,128)S(1)} %slice_bitcast_fusion.3), channel_id=1, source_target_pairs={{0,32},{1,33},{2,34},{3,35},{4,36},{5,37},{6,38},{7,39},{64,96},{6... | collective-permute-start | bytes 98312 | tf_op jit(solution)/shard_map/ppermute | solution.py:311
  37.6 5.4 %collective-permute-start.2 = (f32[32,256]{1,0:T(8,128)S(1)}, f32[32,256]{1,0:T(8,128)S(1)}, u32[]{:S(2)}, u32[]{:S(2)}) collective-permute-start(f32[32,256]{1,0:T(8,128)S(1)} %broadcast_select_fusion), channel_id=1, source_target_pairs={{0,16},{32,48},{1,17},{33,49},{2,18},{34,50},{3,19},{35,51},{4,20}... | collective-permute-start | bytes 98312 | tf_op jit(solution)/shard_map/ppermute | solution.py:311
  39.6 8.9 %all-to-all-start.1 = ((f32[4,64,256]{2,1,0:T(8,128)}), f32[4,64,256]{2,1,0:T(8,128)S(1)}, u32[]{:S(2)}, u32[]{:S(2)}) async-start(f32[4,64,256]{2,1,0:T(8,128)} %broadcast_in_dim.97), calls=%async_computation.1 | async-start | bytes 524288 | tf_op jit(solution)/shard_map/all_to_all | solution.py:45
  43.0 18.3 %collective-permute-start.3 = (f32[32,256]{1,0:T(8,128)S(1)}, f32[32,256]{1,0:T(8,128)S(1)}, u32[]{:S(2)}, u32[]{:S(2)}) collective-permute-start(f32[32,256]{1,0:T(8,128)S(1)} %broadcast_select_fusion.1), channel_id=1, source_target_pairs={{0,8},{16,24},{32,40},{48,56},{1,9},{17,25},{33,41},{49,57},{2,10}... | collective-permute-start | bytes 98312 | tf_op jit(solution)/shard_map/ppermute | solution.py:311
  48.5 16.9 %collective-permute-start = (f32[4,64,256]{2,1,0:T(8,128)S(1)}, f32[4,64,256]{2,1,0:T(8,128)S(1)}, u32[]{:S(2)}, u32[]{:S(2)}) collective-permute-start(f32[4,64,256]{2,1,0:T(8,128)S(1)} %all-to-all-done.1), channel_id=1, source_target_pairs={{0,1},{1,0},{2,3},{3,2},{4,5},{5,4},{6,7},{7,6},{8,9},{9,8},{10,11... | collective-permute-start | bytes 786440 | tf_op jit(solution)/shard_map/ppermute | solution.py:300
  62.0 8.4 %all-to-all-start.2 = ((f32[4,32,256]{2,1,0:T(8,128)}), f32[4,32,256]{2,1,0:T(8,128)S(1)}, u32[]{:S(2)}, u32[]{:S(2)}) async-start(f32[4,32,256]{2,1,0:T(8,128)} %broadcast_in_dim.100), calls=%async_computation.2 | async-start | bytes 262144 | tf_op jit(solution)/shard_map/all_to_all | solution.py:45
  65.4 40.9 %all-gather.11.cloned.1.call-start = ((), (), s32[]{:S(2)}) async-start(), calls=%async_computation.8 | async-start | bytes 1179648 | tf_op jit(solution)/shard_map/all_gather | solution.py:353
  70.4 35.8 %all-to-all-start.3 = ((f32[8,512,128]{2,1,0:T(8,128)}), f32[8,512,128]{2,1,0:T(8,128)S(1)}, u32[]{:S(2)}, u32[]{:S(2)}) async-start(f32[8,512,128]{2,1,0:T(8,128)} %pick_columns.1), calls=%async_computation.3 | async-start | bytes 4194304 | tf_op jit(solution)/shard_map/all_to_all | solution.py:45
  75.6 3.8 %collective-permute-start.4 = (f32[4,32,256]{2,1,0:T(8,128)S(1)}, f32[4,32,256]{2,1,0:T(8,128)S(1)}, u32[]{:S(2)}, u32[]{:S(2)}) collective-permute-start(f32[4,32,256]{2,1,0:T(8,128)S(1)} %all-to-all-done.2), channel_id=1, source_target_pairs={{0,1},{1,0},{2,3},{3,2},{4,5},{5,4},{6,7},{7,6},{8,9},{9,8},{10,11... | collective-permute-start | bytes 393224 | tf_op jit(solution)/shard_map/ppermute | solution.py:300
  106.2 1.3 copy-start
  116.3 24.1 %all-to-all-start.4 = ((f32[64,16,128]{2,1,0:T(8,128)}), f32[64,16,128]{2,1,0:T(8,128)S(1)}, u32[]{:S(2)}, u32[]{:S(2)}) async-start(f32[64,16,128]{2,1,0:T(8,128)} %bitcast.73), calls=%async_computation.4 | async-start | bytes 1048576 | tf_op jit(solution)/shard_map/all_to_all | solution.py:45
  152.1 122.9 %all-to-all-start.6 = ((f32[64,128,128]{2,1,0:T(8,128)}), f32[64,128,128]{2,1,0:T(8,128)}, u32[]{:S(2)}, u32[]{:S(2)}) async-start(f32[64,128,128]{2,1,0:T(8,128)} %get-tuple-element.13), calls=%async_computation.6 | async-start | bytes 8388608 | tf_op jit(solution)/shard_map/all_to_all | solution.py:45
  157.8 66.4 %all-gather.13.cloned.1.call-start = ((), (), s32[]{:S(2)}) async-start(), calls=%async_computation.9 | async-start | bytes 1179648 | tf_op jit(solution)/shard_map/all_gather | solution.py:389
  158.5 100.4 %all-gather.15.cloned.1.call-start = ((), (), s32[]{:S(2)}) async-start(), calls=%async_computation.10 | async-start | bytes 2359296 | tf_op jit(solution)/shard_map/all_gather | solution.py:391
Sparse Core Ops, SparseCore 0:
  10.6 42.7 all-gather.8
  68.3 37.9 all-gather.10
  160.7 63.5 all-gather.12
  226.9 31.9 all-gather.14

commit v5 on v4

--- a/solution.py
+++ b/solution.py
@@ -123,12 +123,10 @@
     )(corner)
 
 
-def parent_kernel(where_ref, tops_ref, top_ref, parent_ref, out_ref, inverse_ref, work_ref):
+def parent_kernel(where_ref, inverse_ref, tops_ref, top_ref, parent_ref, out_ref):
     row_id, own_column = where_ref[0], where_ref[1]
     lead = PANEL // BLOCK
     blocks = tops_ref.shape[0]
-    corner = jnp.concatenate([tops_ref[i, 1] for i in range(lead)], axis=1)
-    invert(corner, inverse_ref, work_ref)
 
     @pl.when(own_column >= lead)
     def _():
@@ -136,7 +134,7 @@
 
         def body(block, carry):
             part = pl.ds(pl.multiple_of(block * BLOCK, BLOCK), BLOCK)
-            change = matmul_tn(matmul(inverse_ref[...], tops_ref[block, 0]), upper)
+            change = matmul_tn(matmul(inverse_ref[...], tops_ref[block]), upper)
             first = (row_id == 0) & (block < lead)
             out_ref[part, :] = parent_ref[part, :] - jnp.where(first, 0.0, change)
             return carry
@@ -150,25 +148,21 @@
 
         def body(block, carry):
             part = pl.ds(pl.multiple_of(block * BLOCK, BLOCK), BLOCK)
-            out_ref[part, :] = matmul(rows, tops_ref[block, 0]).T
+            out_ref[part, :] = matmul(rows, tops_ref[block]).T
             return carry
 
         lax.fori_loop(0, blocks, body, 0)
 
 
-def parent_base(where, tops, top, parent):
+def parent_base(where, inverse, tops, top, parent):
     vmem = pl.BlockSpec(memory_space=pltpu.VMEM)
     return pl.pallas_call(
         parent_kernel,
         out_shape=jax.ShapeDtypeStruct(parent.shape, jnp.float32),
-        in_specs=[pl.BlockSpec(memory_space=pltpu.SMEM), vmem, vmem, vmem],
+        in_specs=[pl.BlockSpec(memory_space=pltpu.SMEM), vmem, vmem, vmem, vmem],
         out_specs=vmem,
-        scratch_shapes=[
-            pltpu.VMEM((PANEL, PANEL), jnp.float32),
-            pltpu.VMEM((PANEL, 2 * PANEL), jnp.float32),
-        ],
         name="parent_base",
-    )(where, tops, top, parent)
+    )(where, inverse, tops, top, parent)
 
 
 def pick_kernel(index_ref, front_ref, out_ref):
@@ -303,12 +297,12 @@
     return both.reshape(-1, *along.shape[1:])
 
 
-def from_first_row(value):
-    index = lax.axis_index("row")
-    stride = lax.axis_size("row") // 2
+def from_first(value, axis):
+    index = lax.axis_index(axis)
+    stride = lax.axis_size(axis) // 2
     while stride:
-        pairs = [(i, i + stride) for i in range(0, lax.axis_size("row"), 2 * stride)]
-        other = lax.ppermute(value, "row", pairs)
+        pairs = [(i, i + stride) for i in range(0, lax.axis_size(axis), 2 * stride)]
+        other = lax.ppermute(value, axis, pairs)
         value = jnp.where(index % (2 * stride) == stride, other, value)
         stride //= 2
     return value
@@ -339,22 +333,25 @@
     column_index = at(own_lo_index, col_id, 1)
     column_valid = at(own_lo_valid, col_id, 1)
 
-    parent_top = lax.all_gather(parent[:PANEL], "row")[0]
     share = PANEL // grid_cols
     deals = front[:, :PANEL].reshape(-1, grid_cols, share, PANEL).transpose(1, 0, 2, 3)
     deal = exchange(deals.reshape(grid_cols, -1, PANEL), COL)[0]
+    picked = pick_columns(at(own_lo_index, col_id), front)
+    deal, picked = lax.optimization_barrier((deal, picked))
     along = spread(deal, "col_0", lax.axis_size("col_0"))
-    corner = spread(from_first_row(deal[:share]), "col_0", lax.axis_size("col_0"))
-    picked = pick_columns(at(own_lo_index, col_id), front)
+    corner, along = lax.optimization_barrier((from_first(deal[:share], "row"), along))
+    corner = spread(corner, "col_0", lax.axis_size("col_0"))
     raw = swapped_core(along).reshape(grid_cols, -1, share, PANEL)
     raw = raw.transpose(1, 0, 2, 3).reshape(rows, PANEL)
     mine = lax.dynamic_slice_in_dim(raw, at(column_index, row_id) * BLOCK, BLOCK, 0)
-    mine, parent_top = lax.optimization_barrier((mine, parent_top))
     blocks = lax.all_gather(mine, "row")
     picked, corner, mine = lax.optimization_barrier((picked, corner, mine))
     corner = swapped_core(corner).reshape(PANEL, PANEL)
     cols = exchange(picked, COL)
     inverse = lower_inverse(corner)
+    parent_top, inverse = lax.optimization_barrier((parent[:PANEL], inverse))
+    parent_top = from_first(parent_top, "row")
+    cols, parent_top = lax.optimization_barrier((cols, parent_top))
     factor = matmul_nt(raw, inverse)
 
     column_band = jnp.sum(
@@ -387,9 +384,11 @@
     arrived = exchange(pieces, LEAF_ROW)
 
     every_leaf = lax.all_gather(top, "leaf")
-    pair = jnp.stack([at(every_leaf, row_id), every_leaf[0]])
-    every_col = lax.all_gather(pair, COL)
-    base = parent_base(jnp.stack([row_id, own_column]).astype(jnp.int32), every_col, top, parent)
+    tops = lax.all_gather(at(every_leaf, row_id), COL)
+    corner = from_first(every_leaf[0], "col_0")
+    corner = lower_inverse(jnp.concatenate(list(swapped_core(corner[None])), axis=1))
+    place = jnp.stack([row_id, own_column]).astype(jnp.int32)
+    base = parent_base(place, corner, tops, top, parent)
     slots = jnp.where(own_column < lead, -1, at(row_slot, row_id, 2)).reshape(-1)
     result = place_blocks(slots, base, arrived)
     return (factor[None], result[:, None, None, :])

time: 291 us -> 295 us (1.014)
  the two profiles are of different devices: /device:TPU:1 before, /device:TPU:79 now
where the time goes in v5:
time: 295 us; the launch traced here: 293 us
  waiting for transfers between devices  132 us (45%)
  starting transfers between devices  59 us (20%)
  Pallas kernels  52.8 us (18%)
  between operations  14.8 us (5%)
  local copies, waits for them, and re-layouts  12.7 us (4%)
  blocking collectives  12.1 us (4%)
  other arithmetic  6.94 us (2%)
    all_gather x1, waiting for transfers between devices, per_device(): every_leaf = lax.all_gather(top, 'leaf')  71.8 us
    ppermute x8, waiting for transfers between devices, from_first(): other = lax.ppermute(value, axis, pairs)  43.8 us
    all_to_all x6, starting transfers between devices, exchange(): return lax.all_to_all(value, axes, split_axis=0, concat_axis=0, tiled=True)  40.4 us
    pallas_call x2, Pallas kernels, lower_inverse(): pl.pallas_call(inverse_kernel, out_shape=jax.ShapeDtypeStruct((size, size...  24.7 us
    all_to_all x6, waiting for transfers between devices, exchange(): return lax.all_to_all(value, axes, split_axis=0, concat_axis=0, tiled=True)  16.2 us
    all_to_all x1, blocking collectives, exchange(): return lax.all_to_all(value, axes, split_axis=0, concat_axis=0, tiled=True)  12.1 us
    ppermute x3, starting transfers between devices, swapped_core(): other = lax.ppermute(along, 'col_1', [(0, 1), (1, 0)])  11.4 us
    pallas_call x1, Pallas kernels, parent_base(): pl.pallas_call(parent_kernel, out_shape=jax.ShapeDtypeStruct(parent.shape...  9.23 us
  transfers between devices with their start and end apart: 20, of which 6 were waited for; matrix products, arithmetic and copies ran while one was open for 6% of the time, Pallas kernels for 14%

profile of v5, /device:TPU:79, one launch (start us, length us, event | category | flops | bytes accessed | tf_op | source)
XLA Modules:
  0.0 292.7 jit_solution(15053328545855481168)
XLA Ops:
  9.1 5.1 %all-to-all-start = ((f32[8,64,256]{2,1,0:T(8,128)}), f32[8,64,256]{2,1,0:T(8,128)S(1)}, u32[]{:S(2)}, u32[]{:S(2)}) async-start(f32[8,64,256]{2,1,0:T(8,128)} %bitcast.3), calls=%async_computation | async-start | bytes 1048576 | tf_op jit(solution)/shard_map/all_to_all | solution.py:45
  16.0 6.0 %pick_columns.1 = f32[8,512,128]{2,1,0:T(8,128)} custom-call(s32[8]{0:T(128)} %fusion.10.index_ref, f32[512,512]{1,0:T(8,128)} %bitcast.63), custom_call_target="tpu_custom_call" | custom-call | tf_op jit(solution)/shard_map/pick_columns/pallas_call | solution.py:175
  25.5 4.9 %all-to-all-start.1 = ((f32[4,64,256]{2,1,0:T(8,128)}), f32[4,64,256]{2,1,0:T(8,128)S(1)}, u32[]{:S(2)}, u32[]{:S(2)}) async-start(f32[4,64,256]{2,1,0:T(8,128)} %broadcast_in_dim.100), calls=%async_computation.1 | async-start | bytes 524288 | tf_op jit(solution)/shard_map/all_to_all | solution.py:45
  30.4 7.5 %collective-permute-done.2 = f32[32,256]{1,0:T(8,128)S(1)} collective-permute-done((f32[32,256]{1,0:T(8,128)S(1)}, f32[32,256]{1,0:T(8,128)S(1)}, u32[]{:S(2)}, u32[]{:S(2)}) %collective-permute-start.2) | collective-permute-done | bytes 32800 | tf_op jit(solution)/shard_map/ppermute | solution.py:305
  38.0 4.9 %collective-permute-start.3 = (f32[4,64,256]{2,1,0:T(8,128)S(1)}, f32[4,64,256]{2,1,0:T(8,128)S(1)}, u32[]{:S(2)}, u32[]{:S(2)}) collective-permute-start(f32[4,64,256]{2,1,0:T(8,128)S(1)} %all-to-all-done.1), channel_id=1, source_target_pairs={{0,1},{1,0},{2,3},{3,2},{4,5},{5,4},{6,7},{7,6},{8,9},{9,8},{10,11... | collective-permute-start | bytes 786440 | tf_op jit(solution)/shard_map/ppermute | solution.py:294
  45.9 5.1 %all-to-all-start.2 = ((f32[4,32,256]{2,1,0:T(8,128)}), f32[4,32,256]{2,1,0:T(8,128)S(1)}, u32[]{:S(2)}, u32[]{:S(2)}) async-start(f32[4,32,256]{2,1,0:T(8,128)} %broadcast_in_dim.101), calls=%async_computation.2 | async-start | bytes 262144 | tf_op jit(solution)/shard_map/all_to_all | solution.py:45
  51.8 2.4 all-to-all-done.2
  54.3 3.1 %collective-permute-start.4 = (f32[4,32,256]{2,1,0:T(8,128)S(1)}, f32[4,32,256]{2,1,0:T(8,128)S(1)}, u32[]{:S(2)}, u32[]{:S(2)}) collective-permute-start(f32[4,32,256]{2,1,0:T(8,128)S(1)} %all-to-all-done.2), channel_id=1, source_target_pairs={{0,1},{1,0},{2,3},{3,2},{4,5},{5,4},{6,7},{7,6},{8,9},{9,8},{10,11... | collective-permute-start | bytes 393224 | tf_op jit(solution)/shard_map/ppermute | solution.py:294
  57.8 5.2 %all-to-all-start.3 = ((f32[8,512,128]{2,1,0:T(8,128)}), f32[8,512,128]{2,1,0:T(8,128)S(1)}, u32[]{:S(2)}, u32[]{:S(2)}) async-start(f32[8,512,128]{2,1,0:T(8,128)} %pick_columns.1), calls=%async_computation.3 | async-start | bytes 4194304 | tf_op jit(solution)/shard_map/all_to_all | solution.py:45
  63.8 12.3 %lower_inverse.2.inverse_ref = f32[256,256]{1,0:T(8,128)} custom-call(f32[256,256]{1,0:T(8,128)} %bitcast.68), custom_call_target="tpu_custom_call" | custom-call | tf_op jit(solution)/shard_map/lower_inverse/pallas_call | solution.py:118
  81.5 2.4 fusion.12.factor_ref
  83.8 22.8 %collective-permute-done.7 = f32[256,128]{1,0:T(8,128)S(1)} collective-permute-done((f32[256,128]{1,0:T(8,128)S(1)}, f32[256,128]{1,0:T(8,128)S(1)}, u32[]{:S(2)}, u32[]{:S(2)}) %collective-permute-start.7) | collective-permute-done | bytes 131104 | tf_op jit(solution)/shard_map/ppermute | solution.py:305
  108.0 8.7 %schur_pieces.1 = (f32[64,128,128]{2,1,0:T(8,128)}, f32[8,128,128]{2,1,0:T(8,128)}) custom-call(s32[8]{0:T(128)} %select_reduce_fusion.5.slot_ref, s32[8]{0:T(128)} %convert_element_type.8.live_ref, s32[8]{0:T(128)} %fusion.11.piece_ref, s32[8]{0:T(128)} %fusion.9.valid_ref, f32[8,512,128]{2,1,0:T(8,128)} %copy-done, f32[512,256]{1,0:T(8,128)} %fusion.12.factor_ref, ...), custom_call_target="tpu_custom_call" | custom-call | tf_op jit(solution)/shard_map/schur_pieces/pallas_call | solution.py:239
  116.7 13.2 %all-to-all-start.4 = ((f32[64,16,128]{2,1,0:T(8,128)}), f32[64,16,128]{2,1,0:T(8,128)S(1)}, u32[]{:S(2)}, u32[]{:S(2)}) async-start(f32[64,16,128]{2,1,0:T(8,128)} %bitcast.71), calls=%async_computation.4 | async-start | bytes 1048576 | tf_op jit(solution)/shard_map/all_to_all | solution.py:45
  130.5 13.7 %all-to-all-done.4 = f32[64,16,128]{2,1,0:T(8,128)S(1)} async-done(((f32[64,16,128]{2,1,0:T(8,128)}), f32[64,16,128]{2,1,0:T(8,128)S(1)}, u32[]{:S(2)}, u32[]{:S(2)}) %all-to-all-start.4) | async-done | bytes 524320 | tf_op jit(solution)/shard_map/all_to_all | solution.py:45
  144.4 12.1 %all_to_all.35 = f32[8,2,16,128]{3,2,1,0:T(8,128)S(1)} all-to-all(f32[8,2,16,128]{3,2,1,0:T(8,128)S(1)} %broadcast_in_dim.112), channel_id=1, replica_groups=mesh['leaf'=8,'row'=8,'col_0'=4,'col_1'=2] {'row'}, dimensions={0} | all-to-all | bytes 262144 | tf_op jit(solution)/shard_map/all_to_all | solution.py:45
  156.6 6.9 %all-to-all-start.6 = ((f32[64,128,128]{2,1,0:T(8,128)}), f32[64,128,128]{2,1,0:T(8,128)}, u32[]{:S(2)}, u32[]{:S(2)}) async-start(f32[64,128,128]{2,1,0:T(8,128)} %get-tuple-element.25), calls=%async_computation.6 | async-start | bytes 8388608 | tf_op jit(solution)/shard_map/all_to_all | solution.py:45
  164.3 71.8 %all-gather.10.cloned.1.call-done = f32[2048,128]{1,0:T(8,128)} async-done(((f32[256,128]{1,0:T(8,128)}), f32[2048,128]{1,0:T(8,128)}) %all-gather.10.cloned.1.call-update) | async-done | bytes 1048592 | tf_op jit(solution)/shard_map/all_gather | solution.py:386
  236.0 1.6 constant_dynamic-slice_fusion
  241.5 13.4 %collective-permute-done.9 = f32[256,128]{1,0:T(8,128)S(1)} collective-permute-done((f32[256,128]{1,0:T(8,128)S(1)}, f32[256,128]{1,0:T(8,128)S(1)}, u32[]{:S(2)}, u32[]{:S(2)}) %collective-permute-start.9) | collective-permute-done | bytes 131104 | tf_op jit(solution)/shard_map/ppermute | solution.py:305
  254.9 3.4 %collective-permute-start.10 = (f32[1,256,128]{2,1,0:T(8,128)S(1)}, f32[1,256,128]{2,1,0:T(8,128)S(1)}, u32[]{:S(2)}, u32[]{:S(2)}) collective-permute-start(f32[1,256,128]{2,1,0:T(8,128)S(1)} %select_bitcast_fusion.4), channel_id=1, source_target_pairs={{0,1},{1,0},{2,3},{3,2},{4,5},{5,4},{6,7},{7,6},{8,9},{9,8},{10,11... | collective-permute-start | bytes 393224 | tf_op jit(solution)/shard_map/ppermute | solution.py:294
  260.3 12.4 %lower_inverse.3.inverse_ref = f32[256,256]{1,0:T(8,128)} custom-call(f32[256,256]{1,0:T(8,128)} %pad_maximum_fusion.2.corner_ref), custom_call_target="tpu_custom_call" | custom-call | tf_op jit(solution)/shard_map/lower_inverse/pallas_call | solution.py:118
  272.7 9.2 %parent_base.1.base_ref = f32[1024,128]{1,0:T(8,128)} custom-call(s32[2]{0:T(128)} %pad_add_fusion.where_ref, f32[256,256]{1,0:T(8,128)} %lower_inverse.3.inverse_ref, f32[8,256,128]{2,1,0:T(8,128)} %all-gather.6.cloned.1.call-done.tops_ref, f32[256,128]{1,0:T(8,128)} %bitcast_add_fusion.top_ref, f32[1024,128]{1,0:T(8,128)} %bitcast.70), custom_call_target="tpu_custom_call" | custom-call | tf_op jit(solution)/shard_map/parent_base/pallas_call | solution.py:159
  281.9 4.2 %place_blocks.1 = f32[1024,128]{1,0:T(8,128)} custom-call(s32[64]{0:T(128)} %select_n.243.slot_ref, f32[1024,128]{1,0:T(8,128)} %parent_base.1.base_ref, f32[64,128,128]{2,1,0:T(8,128)} %all-to-all-done.6.blocks_ref), custom_call_target="tpu_custom_call" | custom-call | tf_op jit(solution)/shard_map/place_blocks/pallas_call | solution.py:274
  (87 shorter events, 25.5 us)
Async XLA Ops:
  9.1 13.0 %all-to-all-start = ((f32[8,64,256]{2,1,0:T(8,128)}), f32[8,64,256]{2,1,0:T(8,128)S(1)}, u32[]{:S(2)}, u32[]{:S(2)}) async-start(f32[8,64,256]{2,1,0:T(8,128)} %bitcast.3), calls=%async_computation | async-start | bytes 1048576 | tf_op jit(solution)/shard_map/all_to_all | solution.py:45
  22.1 0.7 collective-permute-start
  22.8 0.7 collective-permute-start.1
  23.5 14.5 %collective-permute-start.2 = (f32[32,256]{1,0:T(8,128)S(1)}, f32[32,256]{1,0:T(8,128)S(1)}, u32[]{:S(2)}, u32[]{:S(2)}) collective-permute-start(f32[32,256]{1,0:T(8,128)S(1)} %broadcast_select_fusion.5), channel_id=1, source_target_pairs={{0,8},{16,24},{32,40},{48,56},{1,9},{17,25},{33,41},{49,57},{2,10}... | collective-permute-start | bytes 98312 | tf_op jit(solution)/shard_map/ppermute | solution.py:305
  25.5 12.4 %all-to-all-start.1 = ((f32[4,64,256]{2,1,0:T(8,128)}), f32[4,64,256]{2,1,0:T(8,128)S(1)}, u32[]{:S(2)}, u32[]{:S(2)}) async-start(f32[4,64,256]{2,1,0:T(8,128)} %broadcast_in_dim.100), calls=%async_computation.1 | async-start | bytes 524288 | tf_op jit(solution)/shard_map/all_to_all | solution.py:45
  38.0 13.0 %collective-permute-start.3 = (f32[4,64,256]{2,1,0:T(8,128)S(1)}, f32[4,64,256]{2,1,0:T(8,128)S(1)}, u32[]{:S(2)}, u32[]{:S(2)}) collective-permute-start(f32[4,64,256]{2,1,0:T(8,128)S(1)} %all-to-all-done.1), channel_id=1, source_target_pairs={{0,1},{1,0},{2,3},{3,2},{4,5},{5,4},{6,7},{7,6},{8,9},{9,8},{10,11... | collective-permute-start | bytes 786440 | tf_op jit(solution)/shard_map/ppermute | solution.py:294
  45.9 8.3 %all-to-all-start.2 = ((f32[4,32,256]{2,1,0:T(8,128)}), f32[4,32,256]{2,1,0:T(8,128)S(1)}, u32[]{:S(2)}, u32[]{:S(2)}) async-start(f32[4,32,256]{2,1,0:T(8,128)} %broadcast_in_dim.101), calls=%async_computation.2 | async-start | bytes 262144 | tf_op jit(solution)/shard_map/all_to_all | solution.py:45
  51.0 55.7 %all-gather.8.cloned.1.call-start = ((), (), s32[]{:S(2)}) async-start(), calls=%async_computation.8 | async-start | bytes 1179648 | tf_op jit(solution)/shard_map/all_gather | solution.py:347
  54.3 8.7 %collective-permute-start.4 = (f32[4,32,256]{2,1,0:T(8,128)S(1)}, f32[4,32,256]{2,1,0:T(8,128)S(1)}, u32[]{:S(2)}, u32[]{:S(2)}) collective-permute-start(f32[4,32,256]{2,1,0:T(8,128)S(1)} %all-to-all-done.2), channel_id=1, source_target_pairs={{0,1},{1,0},{2,3},{3,2},{4,5},{5,4},{6,7},{7,6},{8,9},{9,8},{10,11... | collective-permute-start | bytes 393224 | tf_op jit(solution)/shard_map/ppermute | solution.py:294
  57.8 48.9 %all-to-all-start.3 = ((f32[8,512,128]{2,1,0:T(8,128)}), f32[8,512,128]{2,1,0:T(8,128)S(1)}, u32[]{:S(2)}, u32[]{:S(2)}) async-start(f32[8,512,128]{2,1,0:T(8,128)} %pick_columns.1), calls=%async_computation.3 | async-start | bytes 4194304 | tf_op jit(solution)/shard_map/all_to_all | solution.py:45
  76.1 1.5 collective-permute-start.5
  77.7 2.5 collective-permute-start.6
  80.2 26.5 %collective-permute-start.7 = (f32[256,128]{1,0:T(8,128)S(1)}, f32[256,128]{1,0:T(8,128)S(1)}, u32[]{:S(2)}, u32[]{:S(2)}) collective-permute-start(f32[256,128]{1,0:T(8,128)S(1)} %broadcast_select_fusion.1), channel_id=1, source_target_pairs={{0,8},{16,24},{32,40},{48,56},{1,9},{17,25},{33,41},{49,57},{2,10}... | collective-permute-start | bytes 393224 | tf_op jit(solution)/shard_map/ppermute | solution.py:305
  106.7 1.3 copy-start
  116.7 27.5 %all-to-all-start.4 = ((f32[64,16,128]{2,1,0:T(8,128)}), f32[64,16,128]{2,1,0:T(8,128)S(1)}, u32[]{:S(2)}, u32[]{:S(2)}) async-start(f32[64,16,128]{2,1,0:T(8,128)} %bitcast.71), calls=%async_computation.4 | async-start | bytes 1048576 | tf_op jit(solution)/shard_map/all_to_all | solution.py:45
  156.6 125.4 %all-to-all-start.6 = ((f32[64,128,128]{2,1,0:T(8,128)}), f32[64,128,128]{2,1,0:T(8,128)}, u32[]{:S(2)}, u32[]{:S(2)}) async-start(f32[64,128,128]{2,1,0:T(8,128)} %get-tuple-element.25), calls=%async_computation.6 | async-start | bytes 8388608 | tf_op jit(solution)/shard_map/all_to_all | solution.py:45
  163.5 72.6 %all-gather.10.cloned.1.call-start = ((), (), s32[]{:S(2)}) async-start(), calls=%async_computation.9 | async-start | bytes 1179648 | tf_op jit(solution)/shard_map/all_gather | solution.py:386
  164.2 108.5 %all-gather.6.cloned.1.call-start = ((), (), s32[]{:S(2)}) async-start(), calls=%async_computation.7 | async-start | bytes 1179648 | tf_op jit(solution)/shard_map/all_gather | solution.py:387
  238.5 0.7 collective-permute-start.8
  240.1 14.8 %collective-permute-start.9 = (f32[256,128]{1,0:T(8,128)S(1)}, f32[256,128]{1,0:T(8,128)S(1)}, u32[]{:S(2)}, u32[]{:S(2)}) collective-permute-start(f32[256,128]{1,0:T(8,128)S(1)} %broadcast_select_fusion.3), channel_id=1, source_target_pairs={{0,2},{4,6},{1,3},{5,7},{8,10},{12,14},{9,11},{13,15},{16,18},{20,... | collective-permute-start | bytes 393224 | tf_op jit(solution)/shard_map/ppermute | solution.py:305
  254.9 4.7 %collective-permute-start.10 = (f32[1,256,128]{2,1,0:T(8,128)S(1)}, f32[1,256,128]{2,1,0:T(8,128)S(1)}, u32[]{:S(2)}, u32[]{:S(2)}) collective-permute-start(f32[1,256,128]{2,1,0:T(8,128)S(1)} %select_bitcast_fusion.4), channel_id=1, source_target_pairs={{0,1},{1,0},{2,3},{3,2},{4,5},{5,4},{6,7},{7,6},{8,9},{9,8},{10,11... | collective-permute-start | bytes 393224 | tf_op jit(solution)/shard_map/ppermute | solution.py:294
Sparse Core Ops, SparseCore 0:
  57.9 47.5 all-gather.7
  166.4 69.6 all-gather.9
  238.2 20.0 all-gather.5

commit v6 on v5

--- a/solution.py
+++ b/solution.py
@@ -297,15 +297,19 @@
     return both.reshape(-1, *along.shape[1:])
 
 
-def from_first(value, axis):
+def from_first(value, axis, stride=None):
     index = lax.axis_index(axis)
-    stride = lax.axis_size(axis) // 2
+    stride = stride or lax.axis_size(axis) // 2
     while stride:
-        pairs = [(i, i + stride) for i in range(0, lax.axis_size(axis), 2 * stride)]
-        other = lax.ppermute(value, axis, pairs)
-        value = jnp.where(index % (2 * stride) == stride, other, value)
+        value = tree_round(value, axis, index, stride)
         stride //= 2
     return value
+
+
+def tree_round(value, axis, index, stride):
+    pairs = [(i, i + stride) for i in range(0, lax.axis_size(axis), 2 * stride)]
+    other = lax.ppermute(value, axis, pairs)
+    return jnp.where(index % (2 * stride) == stride, other, value)
 
 
 def per_device(child_front, parent_front, block_map):
@@ -339,19 +343,20 @@
     picked = pick_columns(at(own_lo_index, col_id), front)
     deal, picked = lax.optimization_barrier((deal, picked))
     along = spread(deal, "col_0", lax.axis_size("col_0"))
-    corner, along = lax.optimization_barrier((from_first(deal[:share], "row"), along))
-    corner = spread(corner, "col_0", lax.axis_size("col_0"))
+    half = grid_rows // 2
+    corner = tree_round(deal[:share], "row", row_id, half)
+    parent_top = from_first(parent[:PANEL], "row")
+    corner, along = lax.optimization_barrier((corner, along))
     raw = swapped_core(along).reshape(grid_cols, -1, share, PANEL)
     raw = raw.transpose(1, 0, 2, 3).reshape(rows, PANEL)
     mine = lax.dynamic_slice_in_dim(raw, at(column_index, row_id) * BLOCK, BLOCK, 0)
+    corner, mine = lax.optimization_barrier((from_first(corner, "row", half // 2), mine))
     blocks = lax.all_gather(mine, "row")
-    picked, corner, mine = lax.optimization_barrier((picked, corner, mine))
+    corner = spread(corner, "col_0", lax.axis_size("col_0"))
+    picked, corner, parent_top = lax.optimization_barrier((picked, corner, parent_top))
     corner = swapped_core(corner).reshape(PANEL, PANEL)
     cols = exchange(picked, COL)
     inverse = lower_inverse(corner)
-    parent_top, inverse = lax.optimization_barrier((parent[:PANEL], inverse))
-    parent_top = from_first(parent_top, "row")
-    cols, parent_top = lax.optimization_barrier((cols, parent_top))
     factor = matmul_nt(raw, inverse)
 
     column_band = jnp.sum(

time: 295 us -> 275 us (0.932)
  the two profiles are of different devices: /device:TPU:79 before, /device:TPU:214 now
where the time goes in v6:
time: 275 us; the launch traced here: 273 us
  waiting for transfers between devices  118 us (43%)
  starting transfers between devices  55.2 us (20%)
  Pallas kernels  52.9 us (19%)
  between operations  14.8 us (5%)
  local copies, waits for them, and re-layouts  11.9 us (4%)
  blocking collectives  10.8 us (4%)
  other arithmetic  6.96 us (3%)
    all_gather x1, waiting for transfers between devices, per_device(): every_leaf = lax.all_gather(top, 'leaf')  56.7 us
    all_to_all x6, starting transfers between devices, exchange(): return lax.all_to_all(value, axes, split_axis=0, concat_axis=0, tiled=True)  42.1 us
    all_to_all x6, waiting for transfers between devices, exchange(): return lax.all_to_all(value, axes, split_axis=0, concat_axis=0, tiled=True)  26.9 us
    pallas_call x2, Pallas kernels, lower_inverse(): pl.pallas_call(inverse_kernel, out_shape=jax.ShapeDtypeStruct((size, size...  24.8 us
    ppermute x8, waiting for transfers between devices, tree_round(): other = lax.ppermute(value, axis, pairs)  20.8 us
    all_gather x1, waiting for transfers between devices, per_device(): blocks = lax.all_gather(mine, 'row')  12.3 us
    all_to_all x1, blocking collectives, exchange(): return lax.all_to_all(value, axes, split_axis=0, concat_axis=0, tiled=True)  10.8 us
    pallas_call x1, Pallas kernels, parent_base(): pl.pallas_call(parent_kernel, out_shape=jax.ShapeDtypeStruct(parent.shape...  9.23 us
  transfers between devices with their start and end apart: 20, of which 10 were waited for; matrix products, arithmetic and copies ran while one was open for 6% of the time, Pallas kernels for 15%

profile of v6, /device:TPU:214, one launch (start us, length us, event | category | flops | bytes accessed | tf_op | source)
XLA Modules:
  0.0 272.5 jit_solution(6974953863934066932)
XLA Ops:
  9.1 4.8 %all-to-all-start = ((f32[8,64,256]{2,1,0:T(8,128)}), f32[8,64,256]{2,1,0:T(8,128)S(1)}, u32[]{:S(2)}, u32[]{:S(2)}) async-start(f32[8,64,256]{2,1,0:T(8,128)} %bitcast.3), calls=%async_computation | async-start | bytes 1048576 | tf_op jit(solution)/shard_map/all_to_all | solution.py:45
  15.8 5.9 %pick_columns.1 = f32[8,512,128]{2,1,0:T(8,128)} custom-call(s32[8]{0:T(128)} %fusion.10.index_ref, f32[512,512]{1,0:T(8,128)} %bitcast.65), custom_call_target="tpu_custom_call" | custom-call | tf_op jit(solution)/shard_map/pick_columns/pallas_call | solution.py:175
  25.6 5.4 %all-to-all-start.1 = ((f32[4,64,256]{2,1,0:T(8,128)}), f32[4,64,256]{2,1,0:T(8,128)S(1)}, u32[]{:S(2)}, u32[]{:S(2)}) async-start(f32[4,64,256]{2,1,0:T(8,128)} %broadcast_in_dim.100), calls=%async_computation.1 | async-start | bytes 524288 | tf_op jit(solution)/shard_map/all_to_all | solution.py:45
  31.0 4.6 %all-to-all-done.1 = f32[4,64,256]{2,1,0:T(8,128)S(1)} async-done(((f32[4,64,256]{2,1,0:T(8,128)}), f32[4,64,256]{2,1,0:T(8,128)S(1)}, u32[]{:S(2)}, u32[]{:S(2)}) %all-to-all-start.1) | async-done | bytes 262176 | tf_op jit(solution)/shard_map/all_to_all | solution.py:45
  41.6 10.2 %collective-permute-done.3 = f32[32,256]{1,0:T(8,128)S(1)} collective-permute-done((f32[32,256]{1,0:T(8,128)S(1)}, f32[32,256]{1,0:T(8,128)S(1)}, u32[]{:S(2)}, u32[]{:S(2)}) %collective-permute-start.3) | collective-permute-done | bytes 32800 | tf_op jit(solution)/shard_map/ppermute | solution.py:311
  53.3 5.3 %all-to-all-start.2 = ((f32[4,32,256]{2,1,0:T(8,128)}), f32[4,32,256]{2,1,0:T(8,128)S(1)}, u32[]{:S(2)}, u32[]{:S(2)}) async-start(f32[4,32,256]{2,1,0:T(8,128)} %broadcast_in_dim.101), calls=%async_computation.2 | async-start | bytes 262144 | tf_op jit(solution)/shard_map/all_to_all | solution.py:45
  59.3 3.2 %all-to-all-done.2 = f32[4,32,256]{2,1,0:T(8,128)S(1)} async-done(((f32[4,32,256]{2,1,0:T(8,128)}), f32[4,32,256]{2,1,0:T(8,128)S(1)}, u32[]{:S(2)}, u32[]{:S(2)}) %all-to-all-start.2) | async-done | bytes 131104 | tf_op jit(solution)/shard_map/all_to_all | solution.py:45
  62.5 5.6 %all-to-all-start.3 = ((f32[8,512,128]{2,1,0:T(8,128)}), f32[8,512,128]{2,1,0:T(8,128)S(1)}, u32[]{:S(2)}, u32[]{:S(2)}) async-start(f32[8,512,128]{2,1,0:T(8,128)} %pick_columns.1), calls=%async_computation.3 | async-start | bytes 4194304 | tf_op jit(solution)/shard_map/all_to_all | solution.py:45
  69.5 2.0 collective-permute-start.7
  74.1 12.4 %lower_inverse.2.inverse_ref = f32[256,256]{1,0:T(8,128)} custom-call(f32[256,256]{1,0:T(8,128)} %bitcast.73), custom_call_target="tpu_custom_call" | custom-call | tf_op jit(solution)/shard_map/lower_inverse/pallas_call | solution.py:118
  86.5 2.4 fusion.12.factor_ref
  88.8 12.3 %all-gather.8.cloned.1.call-done = f32[1024,256]{1,0:T(8,128)} async-done(((f32[128,256]{1,0:T(8,128)}), f32[1024,256]{1,0:T(8,128)}) %all-gather.8.cloned.1.call-update) | async-done | bytes 1048592 | tf_op jit(solution)/shard_map/all_gather | solution.py:354
  102.5 8.7 %schur_pieces.1 = (f32[64,128,128]{2,1,0:T(8,128)}, f32[8,128,128]{2,1,0:T(8,128)}) custom-call(s32[8]{0:T(128)} %select_reduce_fusion.5.slot_ref, s32[8]{0:T(128)} %convert_element_type.8.live_ref, s32[8]{0:T(128)} %fusion.11.piece_ref, s32[8]{0:T(128)} %fusion.9.valid_ref, f32[8,512,128]{2,1,0:T(8,128)} %copy-done, f32[512,256]{1,0:T(8,128)} %fusion.12.factor_ref, ...), custom_call_target="tpu_custom_call" | custom-call | tf_op jit(solution)/shard_map/schur_pieces/pallas_call | solution.py:239
  111.3 10.8 %all-to-all-start.4 = ((f32[64,16,128]{2,1,0:T(8,128)}), f32[64,16,128]{2,1,0:T(8,128)S(1)}, u32[]{:S(2)}, u32[]{:S(2)}) async-start(f32[64,16,128]{2,1,0:T(8,128)} %bitcast.74), calls=%async_computation.4 | async-start | bytes 1048576 | tf_op jit(solution)/shard_map/all_to_all | solution.py:45
  122.7 12.1 %all-to-all-done.4 = f32[64,16,128]{2,1,0:T(8,128)S(1)} async-done(((f32[64,16,128]{2,1,0:T(8,128)}), f32[64,16,128]{2,1,0:T(8,128)S(1)}, u32[]{:S(2)}, u32[]{:S(2)}) %all-to-all-start.4) | async-done | bytes 524320 | tf_op jit(solution)/shard_map/all_to_all | solution.py:45
  135.1 10.8 %all_to_all.35 = f32[8,2,16,128]{3,2,1,0:T(8,128)S(1)} all-to-all(f32[8,2,16,128]{3,2,1,0:T(8,128)S(1)} %broadcast_in_dim.112), channel_id=1, replica_groups=mesh['leaf'=8,'row'=8,'col_0'=4,'col_1'=2] {'row'}, dimensions={0} | all-to-all | bytes 262144 | tf_op jit(solution)/shard_map/all_to_all | solution.py:45
  145.9 10.2 %all-to-all-start.6 = ((f32[64,128,128]{2,1,0:T(8,128)}), f32[64,128,128]{2,1,0:T(8,128)}, u32[]{:S(2)}, u32[]{:S(2)}) async-start(f32[64,128,128]{2,1,0:T(8,128)} %get-tuple-element.23), calls=%async_computation.6 | async-start | bytes 8388608 | tf_op jit(solution)/shard_map/all_to_all | solution.py:45
  156.9 56.7 %all-gather.10.cloned.1.call-done = f32[2048,128]{1,0:T(8,128)} async-done(((f32[256,128]{1,0:T(8,128)}), f32[2048,128]{1,0:T(8,128)}) %all-gather.10.cloned.1.call-update) | async-done | bytes 1048592 | tf_op jit(solution)/shard_map/all_gather | solution.py:391
  219.0 10.5 %collective-permute-done.9 = f32[256,128]{1,0:T(8,128)S(1)} collective-permute-done((f32[256,128]{1,0:T(8,128)S(1)}, f32[256,128]{1,0:T(8,128)S(1)}, u32[]{:S(2)}, u32[]{:S(2)}) %collective-permute-start.9) | collective-permute-done | bytes 131104 | tf_op jit(solution)/shard_map/ppermute | solution.py:311
  229.5 1.9 collective-permute-start.10
  233.5 12.4 %lower_inverse.3.inverse_ref = f32[256,256]{1,0:T(8,128)} custom-call(f32[256,256]{1,0:T(8,128)} %pad_maximum_fusion.2.corner_ref), custom_call_target="tpu_custom_call" | custom-call | tf_op jit(solution)/shard_map/lower_inverse/pallas_call | solution.py:118
  245.9 9.2 %parent_base.1.base_ref = f32[1024,128]{1,0:T(8,128)} custom-call(s32[2]{0:T(128)} %pad_add_fusion.where_ref, f32[256,256]{1,0:T(8,128)} %lower_inverse.3.inverse_ref, f32[8,256,128]{2,1,0:T(8,128)} %all-gather.6.cloned.1.call-done.tops_ref, f32[256,128]{1,0:T(8,128)} %bitcast_add_fusion.top_ref, f32[1024,128]{1,0:T(8,128)} %bitcast.69), custom_call_target="tpu_custom_call" | custom-call | tf_op jit(solution)/shard_map/parent_base/pallas_call | solution.py:159
  255.1 6.6 %all-to-all-done.6.blocks_ref = f32[64,128,128]{2,1,0:T(8,128)} async-done(((f32[64,128,128]{2,1,0:T(8,128)}), f32[64,128,128]{2,1,0:T(8,128)}, u32[]{:S(2)}, u32[]{:S(2)}) %all-to-all-start.6) | async-done | bytes 4194336 | tf_op jit(solution)/shard_map/all_to_all | solution.py:45
  261.8 4.2 %place_blocks.1 = f32[1024,128]{1,0:T(8,128)} custom-call(s32[64]{0:T(128)} %select_n.249.slot_ref, f32[1024,128]{1,0:T(8,128)} %parent_base.1.base_ref, f32[64,128,128]{2,1,0:T(8,128)} %all-to-all-done.6.blocks_ref), custom_call_target="tpu_custom_call" | custom-call | tf_op jit(solution)/shard_map/place_blocks/pallas_call | solution.py:274
  (89 shorter events, 29.3 us)
Async XLA Ops:
  7.2 15.7 %copy-start.1 = (f32[1024,1,1,128]{3,2,1,0:T(1,128)S(1)}, f32[1024,1,1,128]{3,2,1,0:T(1,128)}, u32[]{:S(2)}) copy-start(f32[1024,1,1,128]{3,2,1,0:T(1,128)} %param.4) | copy-start | bytes 1572868
  9.1 13.0 %all-to-all-start = ((f32[8,64,256]{2,1,0:T(8,128)}), f32[8,64,256]{2,1,0:T(8,128)S(1)}, u32[]{:S(2)}, u32[]{:S(2)}) async-start(f32[8,64,256]{2,1,0:T(8,128)} %bitcast.3), calls=%async_computation | async-start | bytes 1048576 | tf_op jit(solution)/shard_map/all_to_all | solution.py:45
  22.2 8.8 %collective-permute-start = (f32[32,256]{1,0:T(8,128)S(1)}, f32[32,256]{1,0:T(8,128)S(1)}, u32[]{:S(2)}, u32[]{:S(2)}) collective-permute-start(f32[32,256]{1,0:T(8,128)S(1)} %slice.25), channel_id=1, source_target_pairs={{0,32},{1,33},{2,34},{3,35},{4,36},{5,37},{6,38},{7,39},{64,96},{6... | collective-permute-start | bytes 98312 | tf_op jit(solution)/shard_map/ppermute | solution.py:311
  22.9 13.4 %collective-permute-start.4 = (f32[256,128]{1,0:T(8,128)S(1)}, f32[256,128]{1,0:T(8,128)S(1)}, u32[]{:S(2)}, u32[]{:S(2)}) collective-permute-start(f32[256,128]{1,0:T(8,128)S(1)} %slice_bitcast_fusion), channel_id=1, source_target_pairs={{0,32},{1,33},{2,34},{3,35},{4,36},{5,37},{6,38},{7,39},{64,96},{6... | collective-permute-start | bytes 393224 | tf_op jit(solution)/shard_map/ppermute | solution.py:311
  25.6 10.1 %all-to-all-start.1 = ((f32[4,64,256]{2,1,0:T(8,128)}), f32[4,64,256]{2,1,0:T(8,128)S(1)}, u32[]{:S(2)}, u32[]{:S(2)}) async-start(f32[4,64,256]{2,1,0:T(8,128)} %broadcast_in_dim.100), calls=%async_computation.1 | async-start | bytes 524288 | tf_op jit(solution)/shard_map/all_to_all | solution.py:45
  35.6 3.3 %collective-permute-start.2 = (f32[32,256]{1,0:T(8,128)S(1)}, f32[32,256]{1,0:T(8,128)S(1)}, u32[]{:S(2)}, u32[]{:S(2)}) collective-permute-start(f32[32,256]{1,0:T(8,128)S(1)} %broadcast_select_fusion.6), channel_id=1, source_target_pairs={{0,16},{32,48},{1,17},{33,49},{2,18},{34,50},{3,19},{35,51},{4,20}... | collective-permute-start | bytes 98312 | tf_op jit(solution)/shard_map/ppermute | solution.py:311
  36.3 3.9 %collective-permute-start.5 = (f32[256,128]{1,0:T(8,128)S(1)}, f32[256,128]{1,0:T(8,128)S(1)}, u32[]{:S(2)}, u32[]{:S(2)}) collective-permute-start(f32[256,128]{1,0:T(8,128)S(1)} %broadcast_select_fusion.1), channel_id=1, source_target_pairs={{0,16},{32,48},{1,17},{33,49},{2,18},{34,50},{3,19},{35,51},{4,20}... | collective-permute-start | bytes 393224 | tf_op jit(solution)/shard_map/ppermute | solution.py:311
  37.0 14.8 %collective-permute-start.1 = (f32[4,64,256]{2,1,0:T(8,128)S(1)}, f32[4,64,256]{2,1,0:T(8,128)S(1)}, u32[]{:S(2)}, u32[]{:S(2)}) collective-permute-start(f32[4,64,256]{2,1,0:T(8,128)S(1)} %all-to-all-done.1), channel_id=1, source_target_pairs={{0,1},{1,0},{2,3},{3,2},{4,5},{5,4},{6,7},{7,6},{8,9},{9,8},{10,11... | collective-permute-start | bytes 786440 | tf_op jit(solution)/shard_map/ppermute | solution.py:294
  39.0 12.9 %collective-permute-start.3 = (f32[32,256]{1,0:T(8,128)S(1)}, f32[32,256]{1,0:T(8,128)S(1)}, u32[]{:S(2)}, u32[]{:S(2)}) collective-permute-start(f32[32,256]{1,0:T(8,128)S(1)} %broadcast_select_fusion.4), channel_id=1, source_target_pairs={{0,8},{16,24},{32,40},{48,56},{1,9},{17,25},{33,41},{49,57},{2,10}... | collective-permute-start | bytes 98312 | tf_op jit(solution)/shard_map/ppermute | solution.py:311
  40.3 18.3 %collective-permute-start.6 = (f32[256,128]{1,0:T(8,128)S(1)}, f32[256,128]{1,0:T(8,128)S(1)}, u32[]{:S(2)}, u32[]{:S(2)}) collective-permute-start(f32[256,128]{1,0:T(8,128)S(1)} %broadcast_select_fusion.2), channel_id=1, source_target_pairs={{0,8},{16,24},{32,40},{48,56},{1,9},{17,25},{33,41},{49,57},{2,10}... | collective-permute-start | bytes 393224 | tf_op jit(solution)/shard_map/ppermute | solution.py:311
  53.3 9.2 %all-to-all-start.2 = ((f32[4,32,256]{2,1,0:T(8,128)}), f32[4,32,256]{2,1,0:T(8,128)S(1)}, u32[]{:S(2)}, u32[]{:S(2)}) async-start(f32[4,32,256]{2,1,0:T(8,128)} %broadcast_in_dim.101), calls=%async_computation.2 | async-start | bytes 262144 | tf_op jit(solution)/shard_map/all_to_all | solution.py:45
  58.6 42.6 %all-gather.8.cloned.1.call-start = ((), (), s32[]{:S(2)}) async-start(), calls=%async_computation.8 | async-start | bytes 1179648 | tf_op jit(solution)/shard_map/all_gather | solution.py:354
  62.5 38.7 %all-to-all-start.3 = ((f32[8,512,128]{2,1,0:T(8,128)}), f32[8,512,128]{2,1,0:T(8,128)S(1)}, u32[]{:S(2)}, u32[]{:S(2)}) async-start(f32[8,512,128]{2,1,0:T(8,128)} %pick_columns.1), calls=%async_computation.3 | async-start | bytes 4194304 | tf_op jit(solution)/shard_map/all_to_all | solution.py:45
  69.5 3.8 %collective-permute-start.7 = (f32[4,32,256]{2,1,0:T(8,128)S(1)}, f32[4,32,256]{2,1,0:T(8,128)S(1)}, u32[]{:S(2)}, u32[]{:S(2)}) collective-permute-start(f32[4,32,256]{2,1,0:T(8,128)S(1)} %all-to-all-done.2), channel_id=1, source_target_pairs={{0,1},{1,0},{2,3},{3,2},{4,5},{5,4},{6,7},{7,6},{8,9},{9,8},{10,11... | collective-permute-start | bytes 393224 | tf_op jit(solution)/shard_map/ppermute | solution.py:294
  101.2 1.3 copy-start
  111.3 23.6 %all-to-all-start.4 = ((f32[64,16,128]{2,1,0:T(8,128)}), f32[64,16,128]{2,1,0:T(8,128)S(1)}, u32[]{:S(2)}, u32[]{:S(2)}) async-start(f32[64,16,128]{2,1,0:T(8,128)} %bitcast.74), calls=%async_computation.4 | async-start | bytes 1048576 | tf_op jit(solution)/shard_map/all_to_all | solution.py:45
  145.9 115.9 %all-to-all-start.6 = ((f32[64,128,128]{2,1,0:T(8,128)}), f32[64,128,128]{2,1,0:T(8,128)}, u32[]{:S(2)}, u32[]{:S(2)}) async-start(f32[64,128,128]{2,1,0:T(8,128)} %get-tuple-element.23), calls=%async_computation.6 | async-start | bytes 8388608 | tf_op jit(solution)/shard_map/all_to_all | solution.py:45
  156.1 57.5 %all-gather.10.cloned.1.call-start = ((), (), s32[]{:S(2)}) async-start(), calls=%async_computation.9 | async-start | bytes 1179648 | tf_op jit(solution)/shard_map/all_gather | solution.py:391
  156.8 89.1 %all-gather.6.cloned.1.call-start = ((), (), s32[]{:S(2)}) async-start(), calls=%async_computation.7 | async-start | bytes 1179648 | tf_op jit(solution)/shard_map/all_gather | solution.py:392
  216.1 0.7 collective-permute-start.8
  217.7 11.8 %collective-permute-start.9 = (f32[256,128]{1,0:T(8,128)S(1)}, f32[256,128]{1,0:T(8,128)S(1)}, u32[]{:S(2)}, u32[]{:S(2)}) collective-permute-start(f32[256,128]{1,0:T(8,128)S(1)} %broadcast_select_fusion), channel_id=1, source_target_pairs={{0,2},{4,6},{1,3},{5,7},{8,10},{12,14},{9,11},{13,15},{16,18},{20,... | collective-permute-start | bytes 393224 | tf_op jit(solution)/shard_map/ppermute | solution.py:311
  229.5 3.2 %collective-permute-start.10 = (f32[1,256,128]{2,1,0:T(8,128)S(1)}, f32[1,256,128]{2,1,0:T(8,128)S(1)}, u32[]{:S(2)}, u32[]{:S(2)}) collective-permute-start(f32[1,256,128]{2,1,0:T(8,128)S(1)} %select_bitcast_fusion.4), channel_id=1, source_target_pairs={{0,1},{1,0},{2,3},{3,2},{4,5},{5,4},{6,7},{7,6},{8,9},{9,8},{10,11... | collective-permute-start | bytes 393224 | tf_op jit(solution)/shard_map/ppermute | solution.py:294
Sparse Core Ops, SparseCore 0:
  61.5 39.6 all-gather.7
  159.0 54.5 all-gather.9
  215.7 29.7 all-gather.5

commit v7 on v6

--- a/solution.py
+++ b/solution.py
@@ -337,26 +337,22 @@
     column_index = at(own_lo_index, col_id, 1)
     column_valid = at(own_lo_valid, col_id, 1)
 
-    share = PANEL // grid_cols
-    deals = front[:, :PANEL].reshape(-1, grid_cols, share, PANEL).transpose(1, 0, 2, 3)
-    deal = exchange(deals.reshape(grid_cols, -1, PANEL), COL)[0]
+    half = grid_rows // 2
+    deal = exchange(front[:, :PANEL].reshape(grid_cols, -1, PANEL), COL)[0]
     picked = pick_columns(at(own_lo_index, col_id), front)
-    deal, picked = lax.optimization_barrier((deal, picked))
+    parent_top = tree_round(parent[:PANEL], "row", row_id, half)
+    deal, picked, parent_top = lax.optimization_barrier((deal, picked, parent_top))
     along = spread(deal, "col_0", lax.axis_size("col_0"))
-    half = grid_rows // 2
-    corner = tree_round(deal[:share], "row", row_id, half)
-    parent_top = from_first(parent[:PANEL], "row")
-    corner, along = lax.optimization_barrier((corner, along))
-    raw = swapped_core(along).reshape(grid_cols, -1, share, PANEL)
-    raw = raw.transpose(1, 0, 2, 3).reshape(rows, PANEL)
+    parent_top = tree_round(parent_top, "row", row_id, half // 2)
+    along, parent_top = lax.optimization_barrier((along, parent_top))
+    raw = swapped_core(along)
+    parent_top = from_first(parent_top, "row", half // 4)
+    picked, raw, parent_top = lax.optimization_barrier((picked, raw, parent_top))
+    cols = exchange(picked, COL)
+    raw = raw.reshape(rows, PANEL)
     mine = lax.dynamic_slice_in_dim(raw, at(column_index, row_id) * BLOCK, BLOCK, 0)
-    corner, mine = lax.optimization_barrier((from_first(corner, "row", half // 2), mine))
     blocks = lax.all_gather(mine, "row")
-    corner = spread(corner, "col_0", lax.axis_size("col_0"))
-    picked, corner, parent_top = lax.optimization_barrier((picked, corner, parent_top))
-    corner = swapped_core(corner).reshape(PANEL, PANEL)
-    cols = exchange(picked, COL)
-    inverse = lower_inverse(corner)
+    inverse = lower_inverse(from_first(raw[:PANEL], "row"))
     factor = matmul_nt(raw, inverse)
 
     column_band = jnp.sum(

time: 275 us -> 279 us (1.015)
  the two profiles are of different devices: /device:TPU:214 before, /device:TPU:15 now
where the time goes in v7:
time: 279 us; the launch traced here: 276 us
  waiting for transfers between devices  103 us (37%)
  starting transfers between devices  66.7 us (24%)
  Pallas kernels  53.3 us (19%)
  between operations  14.8 us (5%)
  local copies, waits for them, and re-layouts  13.5 us (5%)
  blocking collectives  11.2 us (4%)
  other arithmetic  11.1 us (4%)
    all_gather x1, waiting for transfers between devices, per_device(): every_leaf = lax.all_gather(top, 'leaf')  65.5 us
    all_to_all x5, starting transfers between devices, exchange(): return lax.all_to_all(value, axes, split_axis=0, concat_axis=0, tiled=True)  38.5 us
    pallas_call x2, Pallas kernels, lower_inverse(): pl.pallas_call(inverse_kernel, out_shape=jax.ShapeDtypeStruct((size, size...  24.7 us
    ppermute x8, starting transfers between devices, tree_round(): other = lax.ppermute(value, axis, pairs)  20.9 us
    ppermute x8, waiting for transfers between devices, tree_round(): other = lax.ppermute(value, axis, pairs)  17.9 us
    all_to_all x5, waiting for transfers between devices, exchange(): return lax.all_to_all(value, axes, split_axis=0, concat_axis=0, tiled=True)  16.9 us
    all_to_all x1, blocking collectives, exchange(): return lax.all_to_all(value, axes, split_axis=0, concat_axis=0, tiled=True)  11.2 us
    pallas_call x1, Pallas kernels, parent_base(): pl.pallas_call(parent_kernel, out_shape=jax.ShapeDtypeStruct(parent.shape...  9.23 us
  transfers between devices with their start and end apart: 18, of which 8 were waited for; matrix products, arithmetic and copies ran while one was open for 9% of the time, Pallas kernels for 15%

profile of v7, /device:TPU:15, one launch (start us, length us, event | category | flops | bytes accessed | tf_op | source)
XLA Modules:
  0.0 276.1 jit_solution(9949658675376256141)
XLA Ops:
  8.1 10.6 %collective-permute-start = (f32[256,128]{1,0:T(8,128)S(1)}, f32[256,128]{1,0:T(8,128)S(1)}, u32[]{:S(2)}, u32[]{:S(2)}) collective-permute-start(f32[256,128]{1,0:T(8,128)S(1)} %slice_bitcast_fusion), channel_id=1, source_target_pairs={{0,32},{1,33},{2,34},{3,35},{4,36},{5,37},{6,38},{7,39},{64,96},{6... | collective-permute-start | bytes 393224 | tf_op jit(solution)/shard_map/ppermute | solution.py:311
  20.6 5.3 %all-to-all-start = ((f32[8,64,256]{2,1,0:T(8,128)}), f32[8,64,256]{2,1,0:T(8,128)S(1)}, u32[]{:S(2)}, u32[]{:S(2)}) async-start(f32[8,64,256]{2,1,0:T(8,128)} %bitcast.1), calls=%async_computation | async-start | bytes 1048576 | tf_op jit(solution)/shard_map/all_to_all | solution.py:45
  28.5 6.5 %pick_columns.1 = f32[8,512,128]{2,1,0:T(8,128)} custom-call(s32[8]{0:T(128)} %fusion.10.index_ref, f32[512,512]{1,0:T(8,128)} %bitcast.56), custom_call_target="tpu_custom_call" | custom-call | tf_op jit(solution)/shard_map/pick_columns/pallas_call | solution.py:175
  38.0 3.9 %all-to-all-start.1 = ((f32[4,64,256]{2,1,0:T(8,128)}), f32[4,64,256]{2,1,0:T(8,128)S(1)}, u32[]{:S(2)}, u32[]{:S(2)}) async-start(f32[4,64,256]{2,1,0:T(8,128)} %broadcast_in_dim.94), calls=%async_computation.1 | async-start | bytes 524288 | tf_op jit(solution)/shard_map/all_to_all | solution.py:45
  42.0 4.2 %all-to-all-done.1 = f32[4,64,256]{2,1,0:T(8,128)S(1)} async-done(((f32[4,64,256]{2,1,0:T(8,128)}), f32[4,64,256]{2,1,0:T(8,128)S(1)}, u32[]{:S(2)}, u32[]{:S(2)}) %all-to-all-start.1) | async-done | bytes 262176 | tf_op jit(solution)/shard_map/all_to_all | solution.py:45
  47.4 3.5 %collective-permute-start.2 = (f32[4,64,256]{2,1,0:T(8,128)S(1)}, f32[4,64,256]{2,1,0:T(8,128)S(1)}, u32[]{:S(2)}, u32[]{:S(2)}) collective-permute-start(f32[4,64,256]{2,1,0:T(8,128)S(1)} %all-to-all-done.1), channel_id=1, source_target_pairs={{0,1},{1,0},{2,3},{3,2},{4,5},{5,4},{6,7},{7,6},{8,9},{9,8},{10,11... | collective-permute-start | bytes 786440 | tf_op jit(solution)/shard_map/ppermute | solution.py:294
  52.4 5.4 %all-to-all-start.2 = ((f32[8,512,128]{2,1,0:T(8,128)}), f32[8,512,128]{2,1,0:T(8,128)S(1)}, u32[]{:S(2)}, u32[]{:S(2)}) async-start(f32[8,512,128]{2,1,0:T(8,128)} %pick_columns.1), calls=%async_computation.2 | async-start | bytes 4194304 | tf_op jit(solution)/shard_map/all_to_all | solution.py:45
  57.9 3.1 %collective-permute-start.4 = (f32[256,256]{1,0:T(8,128)S(1)}, f32[256,256]{1,0:T(8,128)S(1)}, u32[]{:S(2)}, u32[]{:S(2)}) collective-permute-start(f32[256,256]{1,0:T(8,128)S(1)} %bitcast.62), channel_id=1, source_target_pairs={{0,32},{1,33},{2,34},{3,35},{4,36},{5,37},{6,38},{7,39},{64,96},{6... | collective-permute-start | bytes 786440 | tf_op jit(solution)/shard_map/ppermute | solution.py:311
  63.1 3.1 %collective-permute-done.4 = f32[256,256]{1,0:T(8,128)S(1)} collective-permute-done((f32[256,256]{1,0:T(8,128)S(1)}, f32[256,256]{1,0:T(8,128)S(1)}, u32[]{:S(2)}, u32[]{:S(2)}) %collective-permute-start.4) | collective-permute-done | bytes 262176 | tf_op jit(solution)/shard_map/ppermute | solution.py:311
  70.4 1.9 collective-permute-done.5
  79.1 12.3 %lower_inverse.2.inverse_ref = f32[256,256]{1,0:T(8,128)} custom-call(f32[256,256]{1,0:T(8,128)} %broadcast_select_fusion.2.corner_ref), custom_call_target="tpu_custom_call" | custom-call | tf_op jit(solution)/shard_map/lower_inverse/pallas_call | solution.py:118
  91.4 2.4 fusion.12.factor_ref
  93.8 2.7 all-gather.8.cloned.1.call-done
  96.5 8.7 %schur_pieces.1 = (f32[64,128,128]{2,1,0:T(8,128)}, f32[8,128,128]{2,1,0:T(8,128)}) custom-call(s32[8]{0:T(128)} %select_reduce_fusion.5.slot_ref, s32[8]{0:T(128)} %convert_element_type.8.live_ref, s32[8]{0:T(128)} %fusion.11.piece_ref, s32[8]{0:T(128)} %fusion.9.valid_ref, f32[8,512,128]{2,1,0:T(8,128)} %copy-done, f32[512,256]{1,0:T(8,128)} %fusion.12.factor_ref, ...), custom_call_target="tpu_custom_call" | custom-call | tf_op jit(solution)/shard_map/schur_pieces/pallas_call | solution.py:239
  105.2 17.6 %all-to-all-start.3 = ((f32[64,16,128]{2,1,0:T(8,128)}), f32[64,16,128]{2,1,0:T(8,128)S(1)}, u32[]{:S(2)}, u32[]{:S(2)}) async-start(f32[64,16,128]{2,1,0:T(8,128)} %bitcast.63), calls=%async_computation.3 | async-start | bytes 1048576 | tf_op jit(solution)/shard_map/all_to_all | solution.py:45
  124.2 12.7 %all-to-all-done.3 = f32[64,16,128]{2,1,0:T(8,128)S(1)} async-done(((f32[64,16,128]{2,1,0:T(8,128)}), f32[64,16,128]{2,1,0:T(8,128)S(1)}, u32[]{:S(2)}, u32[]{:S(2)}) %all-to-all-start.3) | async-done | bytes 524320 | tf_op jit(solution)/shard_map/all_to_all | solution.py:45
  137.1 11.2 %all_to_all.30 = f32[8,2,16,128]{3,2,1,0:T(8,128)S(1)} all-to-all(f32[8,2,16,128]{3,2,1,0:T(8,128)S(1)} %broadcast_in_dim.105), channel_id=1, replica_groups=mesh['leaf'=8,'row'=8,'col_0'=4,'col_1'=2] {'row'}, dimensions={0} | all-to-all | bytes 262144 | tf_op jit(solution)/shard_map/all_to_all | solution.py:45
  148.3 6.2 %all-to-all-start.5 = ((f32[64,128,128]{2,1,0:T(8,128)}), f32[64,128,128]{2,1,0:T(8,128)}, u32[]{:S(2)}, u32[]{:S(2)}) async-start(f32[64,128,128]{2,1,0:T(8,128)} %get-tuple-element.21), calls=%async_computation.5 | async-start | bytes 8388608 | tf_op jit(solution)/shard_map/all_to_all | solution.py:45
  155.3 65.5 %all-gather.10.cloned.1.call-done = f32[2048,128]{1,0:T(8,128)} async-done(((f32[256,128]{1,0:T(8,128)}), f32[2048,128]{1,0:T(8,128)}) %all-gather.10.cloned.1.call-update) | async-done | bytes 1048592 | tf_op jit(solution)/shard_map/all_gather | solution.py:387
  226.3 11.8 %collective-permute-done.8 = f32[256,128]{1,0:T(8,128)S(1)} collective-permute-done((f32[256,128]{1,0:T(8,128)S(1)}, f32[256,128]{1,0:T(8,128)S(1)}, u32[]{:S(2)}, u32[]{:S(2)}) %collective-permute-start.8) | collective-permute-done | bytes 131104 | tf_op jit(solution)/shard_map/ppermute | solution.py:311
  238.1 3.6 %collective-permute-start.9 = (f32[1,256,128]{2,1,0:T(8,128)S(1)}, f32[1,256,128]{2,1,0:T(8,128)S(1)}, u32[]{:S(2)}, u32[]{:S(2)}) collective-permute-start(f32[1,256,128]{2,1,0:T(8,128)S(1)} %select_bitcast_fusion.4), channel_id=1, source_target_pairs={{0,1},{1,0},{2,3},{3,2},{4,5},{5,4},{6,7},{7,6},{8,9},{9,8},{10,11... | collective-permute-start | bytes 393224 | tf_op jit(solution)/shard_map/ppermute | solution.py:294
  243.7 12.4 %lower_inverse.3.inverse_ref = f32[256,256]{1,0:T(8,128)} custom-call(f32[256,256]{1,0:T(8,128)} %pad_maximum_fusion.1.corner_ref), custom_call_target="tpu_custom_call" | custom-call | tf_op jit(solution)/shard_map/lower_inverse/pallas_call | solution.py:118
  256.1 9.2 %parent_base.1.base_ref = f32[1024,128]{1,0:T(8,128)} custom-call(s32[2]{0:T(128)} %pad_add_fusion.where_ref, f32[256,256]{1,0:T(8,128)} %lower_inverse.3.inverse_ref, f32[8,256,128]{2,1,0:T(8,128)} %all-gather.6.cloned.1.call-done.tops_ref, f32[256,128]{1,0:T(8,128)} %bitcast_add_fusion.top_ref, f32[1024,128]{1,0:T(8,128)} %bitcast.60), custom_call_target="tpu_custom_call" | custom-call | tf_op jit(solution)/shard_map/parent_base/pallas_call | solution.py:159
  265.3 4.2 %place_blocks.1 = f32[1024,128]{1,0:T(8,128)} custom-call(s32[64]{0:T(128)} %select_n.232.slot_ref, f32[1024,128]{1,0:T(8,128)} %parent_base.1.base_ref, f32[64,128,128]{2,1,0:T(8,128)} %all-to-all-done.5.blocks_ref), custom_call_target="tpu_custom_call" | custom-call | tf_op jit(solution)/shard_map/place_blocks/pallas_call | solution.py:274
  (86 shorter events, 33.1 us)
Async XLA Ops:
  8.1 26.9 %collective-permute-start = (f32[256,128]{1,0:T(8,128)S(1)}, f32[256,128]{1,0:T(8,128)S(1)}, u32[]{:S(2)}, u32[]{:S(2)}) collective-permute-start(f32[256,128]{1,0:T(8,128)S(1)} %slice_bitcast_fusion), channel_id=1, source_target_pairs={{0,32},{1,33},{2,34},{3,35},{4,36},{5,37},{6,38},{7,39},{64,96},{6... | collective-permute-start | bytes 393224 | tf_op jit(solution)/shard_map/ppermute | solution.py:311
  20.6 15.3 %all-to-all-start = ((f32[8,64,256]{2,1,0:T(8,128)}), f32[8,64,256]{2,1,0:T(8,128)S(1)}, u32[]{:S(2)}, u32[]{:S(2)}) async-start(f32[8,64,256]{2,1,0:T(8,128)} %bitcast.1), calls=%async_computation | async-start | bytes 1048576 | tf_op jit(solution)/shard_map/all_to_all | solution.py:45
  26.8 8.2 %copy-start.1 = (s32[8,8,4]{0,2,1:T(4,128)}, s32[8,8,4]{0,2,1:T(4,128)S(1)}, u32[]{:S(2)}) copy-start(s32[8,8,4]{0,2,1:T(4,128)S(1)} %get-tuple-element.43) | copy-start | bytes 3076
  26.9 25.5 %copy-start.3 = (pred[8,8,4]{1,2,0:T(4,128)(4,1)}, pred[8,8,4]{1,2,0:T(4,128)(4,1)S(1)}, u32[]{:S(2)}) copy-start(pred[8,8,4]{1,2,0:T(4,128)(4,1)S(1)} %copy.44) | copy-start | bytes 772
  27.2 25.2 %copy-start.2 = (s32[8,8,8]{2,1,0:T(8,128)}, s32[8,8,8]{2,1,0:T(8,128)S(1)}, u32[]{:S(2)}) copy-start(s32[8,8,8]{2,1,0:T(8,128)S(1)} %select_reduce_fusion.2) | copy-start | bytes 6148
  27.9 24.5 %copy-start.4 = (s32[8,8,8]{2,1,0:T(8,128)}, s32[8,8,8]{2,1,0:T(8,128)S(1)}, u32[]{:S(2)}) copy-start(s32[8,8,8]{2,1,0:T(8,128)S(1)} %get-tuple-element.35) | copy-start | bytes 6148
  35.9 6.0 %collective-permute-start.1 = (f32[256,128]{1,0:T(8,128)S(1)}, f32[256,128]{1,0:T(8,128)S(1)}, u32[]{:S(2)}, u32[]{:S(2)}) collective-permute-start(f32[256,128]{1,0:T(8,128)S(1)} %broadcast_select_fusion.6), channel_id=1, source_target_pairs={{0,16},{32,48},{1,17},{33,49},{2,18},{34,50},{3,19},{35,51},{4,20}... | collective-permute-start | bytes 393224 | tf_op jit(solution)/shard_map/ppermute | solution.py:311
  38.0 8.1 %all-to-all-start.1 = ((f32[4,64,256]{2,1,0:T(8,128)}), f32[4,64,256]{2,1,0:T(8,128)S(1)}, u32[]{:S(2)}, u32[]{:S(2)}) async-start(f32[4,64,256]{2,1,0:T(8,128)} %broadcast_in_dim.94), calls=%async_computation.1 | async-start | bytes 524288 | tf_op jit(solution)/shard_map/all_to_all | solution.py:45
  46.1 6.1 %collective-permute-start.3 = (f32[256,128]{1,0:T(8,128)S(1)}, f32[256,128]{1,0:T(8,128)S(1)}, u32[]{:S(2)}, u32[]{:S(2)}) collective-permute-start(f32[256,128]{1,0:T(8,128)S(1)} %broadcast_select_fusion.5), channel_id=1, source_target_pairs={{0,8},{16,24},{32,40},{48,56},{1,9},{17,25},{33,41},{49,57},{2,10}... | collective-permute-start | bytes 393224 | tf_op jit(solution)/shard_map/ppermute | solution.py:311
  47.4 4.9 %collective-permute-start.2 = (f32[4,64,256]{2,1,0:T(8,128)S(1)}, f32[4,64,256]{2,1,0:T(8,128)S(1)}, u32[]{:S(2)}, u32[]{:S(2)}) collective-permute-start(f32[4,64,256]{2,1,0:T(8,128)S(1)} %all-to-all-done.1), channel_id=1, source_target_pairs={{0,1},{1,0},{2,3},{3,2},{4,5},{5,4},{6,7},{7,6},{8,9},{9,8},{10,11... | collective-permute-start | bytes 786440 | tf_op jit(solution)/shard_map/ppermute | solution.py:294
  52.4 41.3 %all-to-all-start.2 = ((f32[8,512,128]{2,1,0:T(8,128)}), f32[8,512,128]{2,1,0:T(8,128)S(1)}, u32[]{:S(2)}, u32[]{:S(2)}) async-start(f32[8,512,128]{2,1,0:T(8,128)} %pick_columns.1), calls=%async_computation.2 | async-start | bytes 4194304 | tf_op jit(solution)/shard_map/all_to_all | solution.py:45
  57.8 38.7 %all-gather.8.cloned.1.call-start = ((), (), s32[]{:S(2)}) async-start(), calls=%async_computation.7 | async-start | bytes 1179648 | tf_op jit(solution)/shard_map/all_gather | solution.py:354
  57.9 8.4 %collective-permute-start.4 = (f32[256,256]{1,0:T(8,128)S(1)}, f32[256,256]{1,0:T(8,128)S(1)}, u32[]{:S(2)}, u32[]{:S(2)}) collective-permute-start(f32[256,256]{1,0:T(8,128)S(1)} %bitcast.62), channel_id=1, source_target_pairs={{0,32},{1,33},{2,34},{3,35},{4,36},{5,37},{6,38},{7,39},{64,96},{6... | collective-permute-start | bytes 786440 | tf_op jit(solution)/shard_map/ppermute | solution.py:311
  66.3 6.0 %collective-permute-start.5 = (f32[256,256]{1,0:T(8,128)S(1)}, f32[256,256]{1,0:T(8,128)S(1)}, u32[]{:S(2)}, u32[]{:S(2)}) collective-permute-start(f32[256,256]{1,0:T(8,128)S(1)} %broadcast_select_fusion), channel_id=1, source_target_pairs={{0,16},{32,48},{1,17},{33,49},{2,18},{34,50},{3,19},{35,51},{4,20}... | collective-permute-start | bytes 786440 | tf_op jit(solution)/shard_map/ppermute | solution.py:311
  72.3 6.0 %collective-permute-start.6 = (f32[256,256]{1,0:T(8,128)S(1)}, f32[256,256]{1,0:T(8,128)S(1)}, u32[]{:S(2)}, u32[]{:S(2)}) collective-permute-start(f32[256,256]{1,0:T(8,128)S(1)} %broadcast_select_fusion.1), channel_id=1, source_target_pairs={{0,8},{16,24},{32,40},{48,56},{1,9},{17,25},{33,41},{49,57},{2,10}... | collective-permute-start | bytes 786440 | tf_op jit(solution)/shard_map/ppermute | solution.py:311
  93.8 2.8 copy-start
  105.2 31.7 %all-to-all-start.3 = ((f32[64,16,128]{2,1,0:T(8,128)}), f32[64,16,128]{2,1,0:T(8,128)S(1)}, u32[]{:S(2)}, u32[]{:S(2)}) async-start(f32[64,16,128]{2,1,0:T(8,128)} %bitcast.63), calls=%async_computation.3 | async-start | bytes 1048576 | tf_op jit(solution)/shard_map/all_to_all | solution.py:45
  148.3 117.0 %all-to-all-start.5 = ((f32[64,128,128]{2,1,0:T(8,128)}), f32[64,128,128]{2,1,0:T(8,128)}, u32[]{:S(2)}, u32[]{:S(2)}) async-start(f32[64,128,128]{2,1,0:T(8,128)} %get-tuple-element.21), calls=%async_computation.5 | async-start | bytes 8388608 | tf_op jit(solution)/shard_map/all_to_all | solution.py:45
  154.5 66.3 %all-gather.10.cloned.1.call-start = ((), (), s32[]{:S(2)}) async-start(), calls=%async_computation.8 | async-start | bytes 1179648 | tf_op jit(solution)/shard_map/all_gather | solution.py:387
  155.2 100.9 %all-gather.6.cloned.1.call-start = ((), (), s32[]{:S(2)}) async-start(), calls=%async_computation.6 | async-start | bytes 1179648 | tf_op jit(solution)/shard_map/all_gather | solution.py:388
  223.3 0.7 collective-permute-start.7
  225.0 13.1 %collective-permute-start.8 = (f32[256,128]{1,0:T(8,128)S(1)}, f32[256,128]{1,0:T(8,128)S(1)}, u32[]{:S(2)}, u32[]{:S(2)}) collective-permute-start(f32[256,128]{1,0:T(8,128)S(1)} %broadcast_select_fusion.3), channel_id=1, source_target_pairs={{0,2},{4,6},{1,3},{5,7},{8,10},{12,14},{9,11},{13,15},{16,18},{20,... | collective-permute-start | bytes 393224 | tf_op jit(solution)/shard_map/ppermute | solution.py:311
  238.1 4.9 %collective-permute-start.9 = (f32[1,256,128]{2,1,0:T(8,128)S(1)}, f32[1,256,128]{2,1,0:T(8,128)S(1)}, u32[]{:S(2)}, u32[]{:S(2)}) collective-permute-start(f32[1,256,128]{2,1,0:T(8,128)S(1)} %select_bitcast_fusion.4), channel_id=1, source_target_pairs={{0,1},{1,0},{2,3},{3,2},{4,5},{5,4},{6,7},{7,6},{8,9},{9,8},{10,11... | collective-permute-start | bytes 393224 | tf_op jit(solution)/shard_map/ppermute | solution.py:294
Sparse Core Ops, SparseCore 0:
  61.8 34.6 all-gather.7
  157.4 63.4 all-gather.9
  223.0 28.4 all-gather.5

commit v8 on v7

--- a/solution.py
+++ b/solution.py
@@ -6,7 +6,6 @@
 from jax.sharding import Mesh
 from jax.sharding import PartitionSpec as P
 
-FP = 8192
 PANEL = 256
 BLOCK = 128
 COL = ("col_0", "col_1")
@@ -312,7 +311,7 @@
     return jnp.where(index % (2 * stride) == stride, other, value)
 
 
-def per_device(child_front, parent_front, block_map):
+def eliminate_and_assemble(child_front, parent_front, block_map):
     front = child_front[0]
     parent = parent_front[:, 0, 0, :]
     grid_rows = lax.axis_size("row")
@@ -324,7 +323,6 @@
     rows = front.shape[0]
     child_blocks = rows // BLOCK
     lead = PANEL // BLOCK
-    parent_rows = parent.shape[0]
 
     padded = jnp.concatenate([jnp.full((leaves, lead), -1, jnp.int32), block_map], axis=1)
     maps = padded.reshape(leaves, grid_rows, child_blocks)
@@ -339,9 +337,10 @@
 
     half = grid_rows // 2
     deal = exchange(front[:, :PANEL].reshape(grid_cols, -1, PANEL), COL)[0]
-    picked = pick_columns(at(own_lo_index, col_id), front)
     parent_top = tree_round(parent[:PANEL], "row", row_id, half)
-    deal, picked, parent_top = lax.optimization_barrier((deal, picked, parent_top))
+    send_index = at(own_lo_index, col_id)
+    deal, send_index, parent_top = lax.optimization_barrier((deal, send_index, parent_top))
+    picked = pick_columns(send_index, front)
     along = spread(deal, "col_0", lax.axis_size("col_0"))
     parent_top = tree_round(parent_top, "row", row_id, half // 2)
     along, parent_top = lax.optimization_barrier((along, parent_top))
@@ -403,5 +402,5 @@
     in_specs = (P("leaf", "row", COL), P("row", None, LEAF_COL, None), P())
     out_specs = (P("leaf", "row", None), P("row", None, LEAF_COL, None))
     return jax.shard_map(
-        per_device, mesh=torus, in_specs=in_specs, out_specs=out_specs, check_vma=False
-    )
+        eliminate_and_assemble, mesh=torus, in_specs=in_specs, out_specs=out_specs, check_vma=False
+    )

time: 279 us -> 285 us (1.022)
  the two profiles are of different devices: /device:TPU:15 before, /device:TPU:64 now
where the time goes in v8:
time: 285 us; the launch traced here: 284 us
  waiting for transfers between devices  130 us (46%)
  starting transfers between devices  51.5 us (18%)
  Pallas kernels  46.8 us (16%)
  local copies, waits for them, and re-layouts  14.9 us (5%)
  between operations  14.8 us (5%)
  blocking collectives  12.4 us (4%)
  other arithmetic  11.1 us (4%)
    all_gather x1, waiting for transfers between devices, eliminate_and_assemble(): every_leaf = lax.all_gather(top, 'leaf')  57.8 us
    all_to_all x5, waiting for transfers between devices, exchange(): return lax.all_to_all(value, axes, split_axis=0, concat_axis=0, tiled=True)  37.7 us
    all_to_all x5, starting transfers between devices, exchange(): return lax.all_to_all(value, axes, split_axis=0, concat_axis=0, tiled=True)  36.5 us
    ppermute x8, waiting for transfers between devices, tree_round(): other = lax.ppermute(value, axis, pairs)  34.6 us
    pallas_call x2, Pallas kernels, lower_inverse(): pl.pallas_call(inverse_kernel, out_shape=jax.ShapeDtypeStruct((size, size...  24.7 us
    all_to_all x1, blocking collectives, exchange(): return lax.all_to_all(value, axes, split_axis=0, concat_axis=0, tiled=True)  12.4 us
    ppermute x8, starting transfers between devices, tree_round(): other = lax.ppermute(value, axis, pairs)  11.1 us
    pallas_call x1, Pallas kernels, schur_pieces(): pl.pallas_call(schur_kernel, out_shape=(jax.ShapeDtypeStruct((leaves * ba...  7.44 us
  transfers between devices with their start and end apart: 18, of which 9 were waited for; matrix products, arithmetic and copies ran while one was open for 9% of the time, Pallas kernels for 12%

profile of v8, /device:TPU:64, one launch (start us, length us, event | category | flops | bytes accessed | tf_op | source)
XLA Modules:
  0.0 284.0 jit_solution(14757709312176388392)
XLA Ops:
  10.6 4.3 %all-to-all-start = ((f32[8,64,256]{2,1,0:T(8,128)}), f32[8,64,256]{2,1,0:T(8,128)S(1)}, u32[]{:S(2)}, u32[]{:S(2)}) async-start(f32[8,64,256]{2,1,0:T(8,128)} %bitcast.1), calls=%async_computation | async-start | bytes 1048576 | tf_op jit(solution)/shard_map/all_to_all | solution.py:44
  18.4 6.8 %all-to-all-done = f32[8,64,256]{2,1,0:T(8,128)S(1)} async-done(((f32[8,64,256]{2,1,0:T(8,128)}), f32[8,64,256]{2,1,0:T(8,128)S(1)}, u32[]{:S(2)}, u32[]{:S(2)}) %all-to-all-start) | async-done | bytes 524320 | tf_op jit(solution)/shard_map/all_to_all | solution.py:44
  26.7 3.4 %all-to-all-start.1 = ((f32[4,64,256]{2,1,0:T(8,128)}), f32[4,64,256]{2,1,0:T(8,128)S(1)}, u32[]{:S(2)}, u32[]{:S(2)}) async-start(f32[4,64,256]{2,1,0:T(8,128)} %broadcast_in_dim.94), calls=%async_computation.1 | async-start | bytes 524288 | tf_op jit(solution)/shard_map/all_to_all | solution.py:44
  30.1 6.6 %all-to-all-done.1 = f32[4,64,256]{2,1,0:T(8,128)S(1)} async-done(((f32[4,64,256]{2,1,0:T(8,128)}), f32[4,64,256]{2,1,0:T(8,128)S(1)}, u32[]{:S(2)}, u32[]{:S(2)}) %all-to-all-start.1) | async-done | bytes 262176 | tf_op jit(solution)/shard_map/all_to_all | solution.py:44
  38.0 1.9 collective-permute-start.2
  41.2 5.5 %pick_columns.1 = f32[8,512,128]{2,1,0:T(8,128)} custom-call(s32[8]{0:T(128)} %fusion.10.index_ref, f32[512,512]{1,0:T(8,128)} %bitcast.56), custom_call_target="tpu_custom_call" | custom-call | tf_op jit(solution)/shard_map/pick_columns/pallas_call | solution.py:174
  46.7 4.8 %collective-permute-done.3 = f32[256,128]{1,0:T(8,128)S(1)} collective-permute-done((f32[256,128]{1,0:T(8,128)S(1)}, f32[256,128]{1,0:T(8,128)S(1)}, u32[]{:S(2)}, u32[]{:S(2)}) %collective-permute-start.3) | collective-permute-done | bytes 131104 | tf_op jit(solution)/shard_map/ppermute | solution.py:310
  51.6 3.6 %all-to-all-start.2 = ((f32[8,512,128]{2,1,0:T(8,128)}), f32[8,512,128]{2,1,0:T(8,128)S(1)}, u32[]{:S(2)}, u32[]{:S(2)}) async-start(f32[8,512,128]{2,1,0:T(8,128)} %pick_columns.1), calls=%async_computation.2 | async-start | bytes 4194304 | tf_op jit(solution)/shard_map/all_to_all | solution.py:44
  66.6 24.8 %collective-permute-done.6 = f32[256,256]{1,0:T(8,128)S(1)} collective-permute-done((f32[256,256]{1,0:T(8,128)S(1)}, f32[256,256]{1,0:T(8,128)S(1)}, u32[]{:S(2)}, u32[]{:S(2)}) %collective-permute-start.6) | collective-permute-done | bytes 262176 | tf_op jit(solution)/shard_map/ppermute | solution.py:310
  92.1 12.4 %lower_inverse.2.inverse_ref = f32[256,256]{1,0:T(8,128)} custom-call(f32[256,256]{1,0:T(8,128)} %broadcast_select_fusion.2.corner_ref), custom_call_target="tpu_custom_call" | custom-call | tf_op jit(solution)/shard_map/lower_inverse/pallas_call | solution.py:117
  104.5 2.4 fusion.12.factor_ref
  108.2 7.4 %schur_pieces.1 = (f32[64,128,128]{2,1,0:T(8,128)}, f32[8,128,128]{2,1,0:T(8,128)}) custom-call(s32[8]{0:T(128)} %select_reduce_fusion.5.slot_ref, s32[8]{0:T(128)} %convert_element_type.8.live_ref, s32[8]{0:T(128)} %fusion.11.piece_ref, s32[8]{0:T(128)} %fusion.9.valid_ref, f32[8,512,128]{2,1,0:T(8,128)} %copy-done, f32[512,256]{1,0:T(8,128)} %fusion.12.factor_ref, ...), custom_call_target="tpu_custom_call" | custom-call | tf_op jit(solution)/shard_map/schur_pieces/pallas_call | solution.py:238
  115.6 18.6 %all-to-all-start.3 = ((f32[64,16,128]{2,1,0:T(8,128)}), f32[64,16,128]{2,1,0:T(8,128)S(1)}, u32[]{:S(2)}, u32[]{:S(2)}) async-start(f32[64,16,128]{2,1,0:T(8,128)} %bitcast.63), calls=%async_computation.3 | async-start | bytes 1048576 | tf_op jit(solution)/shard_map/all_to_all | solution.py:44
  135.6 14.8 %all-to-all-done.3 = f32[64,16,128]{2,1,0:T(8,128)S(1)} async-done(((f32[64,16,128]{2,1,0:T(8,128)}), f32[64,16,128]{2,1,0:T(8,128)S(1)}, u32[]{:S(2)}, u32[]{:S(2)}) %all-to-all-start.3) | async-done | bytes 524320 | tf_op jit(solution)/shard_map/all_to_all | solution.py:44
  150.6 12.4 %all_to_all.30 = f32[8,2,16,128]{3,2,1,0:T(8,128)S(1)} all-to-all(f32[8,2,16,128]{3,2,1,0:T(8,128)S(1)} %broadcast_in_dim.105), channel_id=1, replica_groups=mesh['leaf'=8,'row'=8,'col_0'=4,'col_1'=2] {'row'}, dimensions={0} | all-to-all | bytes 262144 | tf_op jit(solution)/shard_map/all_to_all | solution.py:44
  163.0 6.5 %all-to-all-start.5 = ((f32[64,128,128]{2,1,0:T(8,128)}), f32[64,128,128]{2,1,0:T(8,128)}, u32[]{:S(2)}, u32[]{:S(2)}) async-start(f32[64,128,128]{2,1,0:T(8,128)} %get-tuple-element.21), calls=%async_computation.5 | async-start | bytes 8388608 | tf_op jit(solution)/shard_map/all_to_all | solution.py:44
  170.3 57.8 %all-gather.10.cloned.1.call-done = f32[2048,128]{1,0:T(8,128)} async-done(((f32[256,128]{1,0:T(8,128)}), f32[2048,128]{1,0:T(8,128)}) %all-gather.10.cloned.1.call-update) | async-done | bytes 1048592 | tf_op jit(solution)/shard_map/all_gather | solution.py:386
  230.7 4.6 %collective-permute-start.7 = (f32[256,128]{1,0:T(8,128)S(1)}, f32[256,128]{1,0:T(8,128)S(1)}, u32[]{:S(2)}, u32[]{:S(2)}) collective-permute-start(f32[256,128]{1,0:T(8,128)S(1)} %slice.39), channel_id=1, source_target_pairs={{0,4},{1,5},{8,12},{9,13},{16,20},{17,21},{24,28},{25,29},{32,36},... | collective-permute-start | bytes 393224 | tf_op jit(solution)/shard_map/ppermute | solution.py:310
  235.2 2.5 collective-permute-done.7
  240.0 2.5 collective-permute-done.8
  246.5 12.4 %lower_inverse.3.inverse_ref = f32[256,256]{1,0:T(8,128)} custom-call(f32[256,256]{1,0:T(8,128)} %pad_maximum_fusion.1.corner_ref), custom_call_target="tpu_custom_call" | custom-call | tf_op jit(solution)/shard_map/lower_inverse/pallas_call | solution.py:117
  258.8 5.0 %parent_base.1.base_ref = f32[1024,128]{1,0:T(8,128)} custom-call(s32[2]{0:T(128)} %pad_add_fusion.where_ref, f32[256,256]{1,0:T(8,128)} %lower_inverse.3.inverse_ref, f32[8,256,128]{2,1,0:T(8,128)} %all-gather.6.cloned.1.call-done.tops_ref, f32[256,128]{1,0:T(8,128)} %bitcast_add_fusion.top_ref, f32[1024,128]{1,0:T(8,128)} %bitcast.60), custom_call_target="tpu_custom_call" | custom-call | tf_op jit(solution)/shard_map/parent_base/pallas_call | solution.py:158
  263.8 9.5 %all-to-all-done.5.blocks_ref = f32[64,128,128]{2,1,0:T(8,128)} async-done(((f32[64,128,128]{2,1,0:T(8,128)}), f32[64,128,128]{2,1,0:T(8,128)}, u32[]{:S(2)}, u32[]{:S(2)}) %all-to-all-start.5) | async-done | bytes 4194336 | tf_op jit(solution)/shard_map/all_to_all | solution.py:44
  273.4 4.1 %place_blocks.1 = f32[1024,128]{1,0:T(8,128)} custom-call(s32[64]{0:T(128)} %select_n.232.slot_ref, f32[1024,128]{1,0:T(8,128)} %parent_base.1.base_ref, f32[64,128,128]{2,1,0:T(8,128)} %all-to-all-done.5.blocks_ref), custom_call_target="tpu_custom_call" | custom-call | tf_op jit(solution)/shard_map/place_blocks/pallas_call | solution.py:273
  (86 shorter events, 34.6 us)
Async XLA Ops:
  8.1 9.4 %collective-permute-start = (f32[256,128]{1,0:T(8,128)S(1)}, f32[256,128]{1,0:T(8,128)S(1)}, u32[]{:S(2)}, u32[]{:S(2)}) collective-permute-start(f32[256,128]{1,0:T(8,128)S(1)} %slice_bitcast_fusion), channel_id=1, source_target_pairs={{0,32},{1,33},{2,34},{3,35},{4,36},{5,37},{6,38},{7,39},{64,96},{6... | collective-permute-start | bytes 393224 | tf_op jit(solution)/shard_map/ppermute | solution.py:310
  10.6 14.6 %all-to-all-start = ((f32[8,64,256]{2,1,0:T(8,128)}), f32[8,64,256]{2,1,0:T(8,128)S(1)}, u32[]{:S(2)}, u32[]{:S(2)}) async-start(f32[8,64,256]{2,1,0:T(8,128)} %bitcast.1), calls=%async_computation | async-start | bytes 1048576 | tf_op jit(solution)/shard_map/all_to_all | solution.py:44
  15.8 1.7 copy-start.1
  15.9 35.7 %copy-start.3 = (pred[8,8,4]{1,2,0:T(4,128)(4,1)}, pred[8,8,4]{1,2,0:T(4,128)(4,1)S(1)}, u32[]{:S(2)}) copy-start(pred[8,8,4]{1,2,0:T(4,128)(4,1)S(1)} %copy.44) | copy-start | bytes 772
  16.2 35.4 %copy-start.2 = (s32[8,8,8]{2,1,0:T(8,128)}, s32[8,8,8]{2,1,0:T(8,128)S(1)}, u32[]{:S(2)}) copy-start(s32[8,8,8]{2,1,0:T(8,128)S(1)} %select_reduce_fusion.2) | copy-start | bytes 6148
  16.9 34.7 %copy-start.4 = (s32[8,8,8]{2,1,0:T(8,128)}, s32[8,8,8]{2,1,0:T(8,128)S(1)}, u32[]{:S(2)}) copy-start(s32[8,8,8]{2,1,0:T(8,128)S(1)} %get-tuple-element.35) | copy-start | bytes 6148
  25.3 4.8 %collective-permute-start.1 = (f32[256,128]{1,0:T(8,128)S(1)}, f32[256,128]{1,0:T(8,128)S(1)}, u32[]{:S(2)}, u32[]{:S(2)}) collective-permute-start(f32[256,128]{1,0:T(8,128)S(1)} %broadcast_select_fusion.6), channel_id=1, source_target_pairs={{0,16},{32,48},{1,17},{33,49},{2,18},{34,50},{3,19},{35,51},{4,20}... | collective-permute-start | bytes 393224 | tf_op jit(solution)/shard_map/ppermute | solution.py:310
  26.7 10.1 %all-to-all-start.1 = ((f32[4,64,256]{2,1,0:T(8,128)}), f32[4,64,256]{2,1,0:T(8,128)S(1)}, u32[]{:S(2)}, u32[]{:S(2)}) async-start(f32[4,64,256]{2,1,0:T(8,128)} %broadcast_in_dim.94), calls=%async_computation.1 | async-start | bytes 524288 | tf_op jit(solution)/shard_map/all_to_all | solution.py:44
  36.7 14.7 %collective-permute-start.3 = (f32[256,128]{1,0:T(8,128)S(1)}, f32[256,128]{1,0:T(8,128)S(1)}, u32[]{:S(2)}, u32[]{:S(2)}) collective-permute-start(f32[256,128]{1,0:T(8,128)S(1)} %broadcast_select_fusion.5), channel_id=1, source_target_pairs={{0,8},{16,24},{32,40},{48,56},{1,9},{17,25},{33,41},{49,57},{2,10}... | collective-permute-start | bytes 393224 | tf_op jit(solution)/shard_map/ppermute | solution.py:310
  38.0 13.5 %collective-permute-start.2 = (f32[4,64,256]{2,1,0:T(8,128)S(1)}, f32[4,64,256]{2,1,0:T(8,128)S(1)}, u32[]{:S(2)}, u32[]{:S(2)}) collective-permute-start(f32[4,64,256]{2,1,0:T(8,128)S(1)} %all-to-all-done.1), channel_id=1, source_target_pairs={{0,1},{1,0},{2,3},{3,2},{4,5},{5,4},{6,7},{7,6},{8,9},{9,8},{10,11... | collective-permute-start | bytes 786440 | tf_op jit(solution)/shard_map/ppermute | solution.py:293
  51.6 55.2 %all-to-all-start.2 = ((f32[8,512,128]{2,1,0:T(8,128)}), f32[8,512,128]{2,1,0:T(8,128)S(1)}, u32[]{:S(2)}, u32[]{:S(2)}) async-start(f32[8,512,128]{2,1,0:T(8,128)} %pick_columns.1), calls=%async_computation.2 | async-start | bytes 4194304 | tf_op jit(solution)/shard_map/all_to_all | solution.py:44
  55.2 51.6 %all-gather.8.cloned.1.call-start = ((), (), s32[]{:S(2)}) async-start(), calls=%async_computation.7 | async-start | bytes 1179648 | tf_op jit(solution)/shard_map/all_gather | solution.py:353
  55.3 2.8 %collective-permute-start.4 = (f32[256,256]{1,0:T(8,128)S(1)}, f32[256,256]{1,0:T(8,128)S(1)}, u32[]{:S(2)}, u32[]{:S(2)}) collective-permute-start(f32[256,256]{1,0:T(8,128)S(1)} %bitcast.62), channel_id=1, source_target_pairs={{0,32},{1,33},{2,34},{3,35},{4,36},{5,37},{6,38},{7,39},{64,96},{6... | collective-permute-start | bytes 786440 | tf_op jit(solution)/shard_map/ppermute | solution.py:310
  58.2 3.5 %collective-permute-start.5 = (f32[256,256]{1,0:T(8,128)S(1)}, f32[256,256]{1,0:T(8,128)S(1)}, u32[]{:S(2)}, u32[]{:S(2)}) collective-permute-start(f32[256,256]{1,0:T(8,128)S(1)} %broadcast_select_fusion), channel_id=1, source_target_pairs={{0,16},{32,48},{1,17},{33,49},{2,18},{34,50},{3,19},{35,51},{4,20}... | collective-permute-start | bytes 786440 | tf_op jit(solution)/shard_map/ppermute | solution.py:310
  61.7 29.7 %collective-permute-start.6 = (f32[256,256]{1,0:T(8,128)S(1)}, f32[256,256]{1,0:T(8,128)S(1)}, u32[]{:S(2)}, u32[]{:S(2)}) collective-permute-start(f32[256,256]{1,0:T(8,128)S(1)} %broadcast_select_fusion.1), channel_id=1, source_target_pairs={{0,8},{16,24},{32,40},{48,56},{1,9},{17,25},{33,41},{49,57},{2,10}... | collective-permute-start | bytes 786440 | tf_op jit(solution)/shard_map/ppermute | solution.py:310
  106.9 1.3 copy-start
  115.6 34.8 %all-to-all-start.3 = ((f32[64,16,128]{2,1,0:T(8,128)}), f32[64,16,128]{2,1,0:T(8,128)S(1)}, u32[]{:S(2)}, u32[]{:S(2)}) async-start(f32[64,16,128]{2,1,0:T(8,128)} %bitcast.63), calls=%async_computation.3 | async-start | bytes 1048576 | tf_op jit(solution)/shard_map/all_to_all | solution.py:44
  163.0 110.4 %all-to-all-start.5 = ((f32[64,128,128]{2,1,0:T(8,128)}), f32[64,128,128]{2,1,0:T(8,128)}, u32[]{:S(2)}, u32[]{:S(2)}) async-start(f32[64,128,128]{2,1,0:T(8,128)} %get-tuple-element.21), calls=%async_computation.5 | async-start | bytes 8388608 | tf_op jit(solution)/shard_map/all_to_all | solution.py:44
  169.5 58.7 %all-gather.10.cloned.1.call-start = ((), (), s32[]{:S(2)}) async-start(), calls=%async_computation.8 | async-start | bytes 1179648 | tf_op jit(solution)/shard_map/all_gather | solution.py:386
  170.3 88.6 %all-gather.6.cloned.1.call-start = ((), (), s32[]{:S(2)}) async-start(), calls=%async_computation.6 | async-start | bytes 1179648 | tf_op jit(solution)/shard_map/all_gather | solution.py:387
  230.7 7.1 %collective-permute-start.7 = (f32[256,128]{1,0:T(8,128)S(1)}, f32[256,128]{1,0:T(8,128)S(1)}, u32[]{:S(2)}, u32[]{:S(2)}) collective-permute-start(f32[256,128]{1,0:T(8,128)S(1)} %slice.39), channel_id=1, source_target_pairs={{0,4},{1,5},{8,12},{9,13},{16,20},{17,21},{24,28},{25,29},{32,36},... | collective-permute-start | bytes 393224 | tf_op jit(solution)/shard_map/ppermute | solution.py:310
  238.6 3.8 %collective-permute-start.8 = (f32[256,128]{1,0:T(8,128)S(1)}, f32[256,128]{1,0:T(8,128)S(1)}, u32[]{:S(2)}, u32[]{:S(2)}) collective-permute-start(f32[256,128]{1,0:T(8,128)S(1)} %broadcast_select_fusion.3), channel_id=1, source_target_pairs={{0,2},{4,6},{1,3},{5,7},{8,10},{12,14},{9,11},{13,15},{16,18},{20,... | collective-permute-start | bytes 393224 | tf_op jit(solution)/shard_map/ppermute | solution.py:310
  242.5 3.2 %collective-permute-start.9 = (f32[1,256,128]{2,1,0:T(8,128)S(1)}, f32[1,256,128]{2,1,0:T(8,128)S(1)}, u32[]{:S(2)}, u32[]{:S(2)}) collective-permute-start(f32[1,256,128]{2,1,0:T(8,128)S(1)} %select_bitcast_fusion.4), channel_id=1, source_target_pairs={{0,1},{1,0},{2,3},{3,2},{4,5},{5,4},{6,7},{7,6},{8,9},{9,8},{10,11... | collective-permute-start | bytes 393224 | tf_op jit(solution)/shard_map/ppermute | solution.py:293
Sparse Core Ops, SparseCore 0:
  58.1 45.7 all-gather.7
  172.4 55.7 all-gather.9
  230.3 28.3 all-gather.5

commit v9 on v8

--- a/solution.py
+++ b/solution.py
@@ -108,18 +108,22 @@
             work_ref[stop:, :] = work_ref[stop:, :] - matmul_tn(upper[:, stop:size], upper)
 
 
-def inverse_kernel(corner_ref, out_ref, work_ref):
-    invert(corner_ref[...], out_ref, work_ref)
-
-
-def lower_inverse(corner):
-    size = corner.shape[0]
+def inverse_kernel(lower_ref, out_ref, work_ref):
+    side = lower_ref.shape[1]
+    below = lower_ref[side : 2 * side, :]
+    top = jnp.concatenate([lower_ref[:side, :], below.T], axis=1)
+    bottom = jnp.concatenate([below, lower_ref[2 * side :, :]], axis=1)
+    invert(jnp.concatenate([top, bottom], axis=0), out_ref, work_ref)
+
+
+def lower_inverse(lower):
+    size = 2 * lower.shape[1]
     return pl.pallas_call(
         inverse_kernel,
         out_shape=jax.ShapeDtypeStruct((size, size), jnp.float32),
         scratch_shapes=[pltpu.VMEM((size, 2 * size), jnp.float32)],
         name="lower_inverse",
-    )(corner)
+    )(lower)
 
 
 def parent_kernel(where_ref, inverse_ref, tops_ref, top_ref, parent_ref, out_ref):
@@ -186,26 +190,23 @@
 
 def schur_kernel(
     slot_ref, live_ref, piece_ref, valid_ref, cols_ref, factor_ref, inverse_ref, block_ref,
-    out_ref, top_ref, tmp_ref, sems, top_sems,
+    out_ref, tmp_ref, sems,
 ):
     leaves = live_ref.shape[0]
     bands = valid_ref.shape[0]
 
-    def copies(leaf, dest):
+    def copy(leaf, dest):
         start = pl.multiple_of(piece_ref[dest] * BLOCK, BLOCK)
         piece = tmp_ref.at[leaf, pl.ds(start, BLOCK), :]
         item = leaf * bands + dest
-        yield pltpu.make_async_copy(piece, out_ref.at[item], sems.at[item])
-        if dest == 0:
-            yield pltpu.make_async_copy(piece, top_ref.at[leaf], top_sems.at[leaf])
+        return pltpu.make_async_copy(piece, out_ref.at[item], sems.at[item])
 
     def each(leaf, act):
         for dest in range(bands):
 
             @pl.when(valid_ref[dest] > 0)
             def _(dest=dest):
-                for copy in copies(leaf, dest):
-                    act(copy)
+                act(copy(leaf, dest))
 
     def start(leaf, carry):
         @pl.when(live_ref[leaf] > 0)
@@ -237,19 +238,45 @@
     anywhere = pl.BlockSpec(memory_space=pl.ANY)
     return pl.pallas_call(
         schur_kernel,
-        out_shape=(
-            jax.ShapeDtypeStruct((leaves * bands, BLOCK, BLOCK), jnp.float32),
-            jax.ShapeDtypeStruct((leaves, BLOCK, BLOCK), jnp.float32),
-        ),
+        out_shape=jax.ShapeDtypeStruct((leaves * bands, BLOCK, BLOCK), jnp.float32),
         in_specs=[smem] * 4 + [vmem] * 4,
-        out_specs=(anywhere, anywhere),
+        out_specs=anywhere,
         scratch_shapes=[
             pltpu.VMEM((leaves, rows, BLOCK), jnp.float32),
             pltpu.SemaphoreType.DMA((leaves * bands,)),
-            pltpu.SemaphoreType.DMA((leaves,)),
         ],
         name="schur_pieces",
     )(slot, live, piece, valid, cols, factor, inverse, blocks)
+
+
+def top_kernel(slot_ref, live_ref, row_ref, cols_ref, raw_ref, inverse_ref, block_ref, out_ref):
+    @pl.when(row_ref[1] > 0)
+    def _():
+        part = pl.ds(pl.multiple_of(row_ref[0] * BLOCK, BLOCK), BLOCK)
+        factor = matmul_nt(raw_ref[part, :], inverse_ref[...])
+
+        def body(leaf, carry):
+            @pl.when(live_ref[leaf] > 0)
+            def _():
+                slot = slot_ref[leaf]
+                block = matmul_nt(block_ref[slot], inverse_ref[...])
+                out_ref[leaf] = cols_ref[slot, part, :] - matmul_nt(factor, block)
+
+            return carry
+
+        lax.fori_loop(0, live_ref.shape[0], body, 0)
+
+
+def top_pieces(slot, live, row, cols, raw, inverse, blocks):
+    smem = pl.BlockSpec(memory_space=pltpu.SMEM)
+    vmem = pl.BlockSpec(memory_space=pltpu.VMEM)
+    return pl.pallas_call(
+        top_kernel,
+        out_shape=jax.ShapeDtypeStruct((slot.shape[0], BLOCK, BLOCK), jnp.float32),
+        in_specs=[smem] * 3 + [vmem] * 4,
+        out_specs=vmem,
+        name="top_pieces",
+    )(slot, live, row, cols, raw, inverse, blocks)
 
 
 def place_kernel(slot_ref, base_ref, blocks_ref, out_ref):
@@ -351,23 +378,22 @@
     raw = raw.reshape(rows, PANEL)
     mine = lax.dynamic_slice_in_dim(raw, at(column_index, row_id) * BLOCK, BLOCK, 0)
     blocks = lax.all_gather(mine, "row")
-    inverse = lower_inverse(from_first(raw[:PANEL], "row"))
-    factor = matmul_nt(raw, inverse)
-
+    corner = jnp.concatenate([raw[:PANEL, :BLOCK], raw[BLOCK:PANEL, BLOCK:]])
+    inverse = lower_inverse(from_first(corner, "row"))
     column_band = jnp.sum(
         jnp.where(jnp.arange(child_blocks) == column_index[:, None], at(band, leaf_id), 0), axis=-1
     )
     slot, slot_valid = locate(column_band, column_valid, leaves)
-    pieces, tops = schur_pieces(
-        slot,
-        slot_valid.astype(jnp.int32),
-        at(at(hi_index, leaf_id), row_id),
-        at(at(hi_valid, leaf_id), row_id).astype(jnp.int32),
-        cols,
-        factor,
-        inverse,
-        blocks,
-    )
+    live = slot_valid.astype(jnp.int32)
+    piece = at(at(hi_index, leaf_id), row_id)
+    valid = at(at(hi_valid, leaf_id), row_id)
+    first = jnp.sum(
+        jnp.where(jnp.arange(child_blocks) == piece[0], at(at(residue, leaf_id), row_id), 0)
+    )
+    row = jnp.stack([piece[0], (valid[0] & (first < lead)).astype(jnp.int32)])
+    tops = top_pieces(slot, live, row, cols, raw, inverse, blocks)
+    factor = matmul_nt(raw, inverse)
+    pieces = schur_pieces(slot, live, piece, valid.astype(jnp.int32), cols, factor, inverse, blocks)
 
     own_column = leaf_id * grid_cols + col_id
     present = jnp.any((maps == own_column) & usable, axis=(1, 2))
@@ -386,7 +412,8 @@
     every_leaf = lax.all_gather(top, "leaf")
     tops = lax.all_gather(at(every_leaf, row_id), COL)
     corner = from_first(every_leaf[0], "col_0")
-    corner = lower_inverse(jnp.concatenate(list(swapped_core(corner[None])), axis=1))
+    corner = swapped_core(corner[None])
+    corner = lower_inverse(jnp.concatenate([corner[0], corner[1, BLOCK:]]))
     place = jnp.stack([row_id, own_column]).astype(jnp.int32)
     base = parent_base(place, corner, tops, top, parent)
     slots = jnp.where(own_column < lead, -1, at(row_slot, row_id, 2)).reshape(-1)

time: 285 us -> 290 us (1.018)
  the two profiles are of different devices: /device:TPU:64 before, /device:TPU:216 now
where the time goes in v9:
time: 290 us; the launch traced here: 289 us
  waiting for transfers between devices  135 us (47%)
  starting transfers between devices  59.2 us (20%)
  Pallas kernels  55.2 us (19%)
  between operations  15.5 us (5%)
  local copies, waits for them, and re-layouts  11.5 us (4%)
  other arithmetic  9.2 us (3%)
    all_gather x1, waiting for transfers between devices, eliminate_and_assemble(): every_leaf = lax.all_gather(top, 'leaf')  66.4 us
    all_to_all x6, starting transfers between devices, exchange(): return lax.all_to_all(value, axes, split_axis=0, concat_axis=0, tiled=True)  47.4 us
    all_to_all x6, waiting for transfers between devices, exchange(): return lax.all_to_all(value, axes, split_axis=0, concat_axis=0, tiled=True)  34.5 us
    ppermute x8, waiting for transfers between devices, tree_round(): other = lax.ppermute(value, axis, pairs)  32.3 us
    pallas_call x2, Pallas kernels, lower_inverse(): pl.pallas_call(inverse_kernel, out_shape=jax.ShapeDtypeStruct((size, size...  24.8 us
    pallas_call x1, Pallas kernels, parent_base(): pl.pallas_call(parent_kernel, out_shape=jax.ShapeDtypeStruct(parent.shape...  9.23 us
    pallas_call x1, Pallas kernels, schur_pieces(): pl.pallas_call(schur_kernel, out_shape=jax.ShapeDtypeStruct((leaves * ban...  8.63 us
    ppermute x8, starting transfers between devices, tree_round(): other = lax.ppermute(value, axis, pairs)  7.84 us
  transfers between devices with their start and end apart: 19, of which 10 were waited for; matrix products, arithmetic and copies ran while one was open for 7% of the time, Pallas kernels for 17%

profile of v9, /device:TPU:216, one launch (start us, length us, event | category | flops | bytes accessed | tf_op | source)
XLA Modules:
  0.0 288.5 jit_solution(13966523510424448631)
XLA Ops:
  10.6 4.3 %all-to-all-start = ((f32[8,64,256]{2,1,0:T(8,128)}), f32[8,64,256]{2,1,0:T(8,128)S(1)}, u32[]{:S(2)}, u32[]{:S(2)}) async-start(f32[8,64,256]{2,1,0:T(8,128)} %bitcast.1), calls=%async_computation | async-start | bytes 1048576 | tf_op jit(solution)/shard_map/all_to_all | solution.py:44
  17.8 7.5 %all-to-all-done = f32[8,64,256]{2,1,0:T(8,128)S(1)} async-done(((f32[8,64,256]{2,1,0:T(8,128)}), f32[8,64,256]{2,1,0:T(8,128)S(1)}, u32[]{:S(2)}, u32[]{:S(2)}) %all-to-all-start) | async-done | bytes 524320 | tf_op jit(solution)/shard_map/all_to_all | solution.py:44
  26.7 3.4 %all-to-all-start.1 = ((f32[4,64,256]{2,1,0:T(8,128)}), f32[4,64,256]{2,1,0:T(8,128)S(1)}, u32[]{:S(2)}, u32[]{:S(2)}) async-start(f32[4,64,256]{2,1,0:T(8,128)} %broadcast_in_dim.98), calls=%async_computation.1 | async-start | bytes 524288 | tf_op jit(solution)/shard_map/all_to_all | solution.py:44
  30.1 6.6 %all-to-all-done.1 = f32[4,64,256]{2,1,0:T(8,128)S(1)} async-done(((f32[4,64,256]{2,1,0:T(8,128)}), f32[4,64,256]{2,1,0:T(8,128)S(1)}, u32[]{:S(2)}, u32[]{:S(2)}) %all-to-all-start.1) | async-done | bytes 262176 | tf_op jit(solution)/shard_map/all_to_all | solution.py:44
  38.0 1.9 collective-permute-start.2
  41.6 5.5 %pick_columns.1 = f32[8,512,128]{2,1,0:T(8,128)} custom-call(s32[8]{0:T(128)} %fusion.12.index_ref, f32[512,512]{1,0:T(8,128)} %bitcast.70), custom_call_target="tpu_custom_call" | custom-call | tf_op jit(solution)/shard_map/pick_columns/pallas_call | solution.py:178
  47.2 3.6 %all-to-all-start.2 = ((f32[8,512,128]{2,1,0:T(8,128)}), f32[8,512,128]{2,1,0:T(8,128)S(1)}, u32[]{:S(2)}, u32[]{:S(2)}) async-start(f32[8,512,128]{2,1,0:T(8,128)} %pick_columns.1), calls=%async_computation.2 | async-start | bytes 4194304 | tf_op jit(solution)/shard_map/all_to_all | solution.py:44
  58.9 27.0 %collective-permute-done.6 = f32[384,128]{1,0:T(8,128)S(1)} collective-permute-done((f32[384,128]{1,0:T(8,128)S(1)}, f32[384,128]{1,0:T(8,128)S(1)}, u32[]{:S(2)}, u32[]{:S(2)}) %collective-permute-start.6) | collective-permute-done | bytes 196640 | tf_op jit(solution)/shard_map/ppermute | solution.py:337
  86.6 12.4 %lower_inverse.2.inverse_ref = f32[256,256]{1,0:T(8,128)} custom-call(f32[384,128]{1,0:T(8,128)} %broadcast_select_fusion.2.lower_ref), custom_call_target="tpu_custom_call" | custom-call | tf_op jit(solution)/shard_map/lower_inverse/pallas_call | solution.py:121
  99.0 2.0 all-gather.8.cloned.1.call-done
  101.0 2.9 %top_pieces.1 = f32[8,128,128]{2,1,0:T(8,128)} custom-call(s32[8]{0:T(128)} %select_reduce_fusion.5.slot_ref, s32[8]{0:T(128)} %convert_element_type.9.live_ref, s32[2]{0:T(128)} %pad_add_fusion.1.row_ref, f32[8,512,128]{2,1,0:T(8,128)} %copy-done, f32[512,256]{1,0:T(8,128)} %bitcast.65, f32[256,256]{1,0:T(8,128)} %lower_inverse.2.inverse_ref, ...), custom_call_target="tpu_custom_call" | custom-call | tf_op jit(solution)/shard_map/top_pieces/pallas_call | solution.py:273
  104.0 18.9 %all-to-all-start.3 = ((f32[64,16,128]{2,1,0:T(8,128)}), f32[64,16,128]{2,1,0:T(8,128)S(1)}, u32[]{:S(2)}, u32[]{:S(2)}) async-start(f32[64,16,128]{2,1,0:T(8,128)} %bitcast.72), calls=%async_computation.3 | async-start | bytes 1048576 | tf_op jit(solution)/shard_map/all_to_all | solution.py:44
  124.0 12.7 %all-to-all-done.3 = f32[64,16,128]{2,1,0:T(8,128)S(1)} async-done(((f32[64,16,128]{2,1,0:T(8,128)}), f32[64,16,128]{2,1,0:T(8,128)S(1)}, u32[]{:S(2)}, u32[]{:S(2)}) %all-to-all-start.3) | async-done | bytes 524320 | tf_op jit(solution)/shard_map/all_to_all | solution.py:44
  137.6 6.4 %all-to-all-start.4 = ((f32[8,2,16,128]{3,2,1,0:T(8,128)}), f32[8,2,16,128]{3,2,1,0:T(8,128)S(1)}, u32[]{:S(2)}, u32[]{:S(2)}) async-start(f32[8,2,16,128]{3,2,1,0:T(8,128)} %broadcast_in_dim.110), calls=%async_computation.4 | async-start | bytes 262144 | tf_op jit(solution)/shard_map/all_to_all | solution.py:44
  144.0 2.5 fusion.13.factor_ref
  146.5 8.6 %schur_pieces.1 = f32[64,128,128]{2,1,0:T(8,128)} custom-call(s32[8]{0:T(128)} %select_reduce_fusion.5.slot_ref, s32[8]{0:T(128)} %convert_element_type.9.live_ref, s32[8]{0:T(128)} %fusion.16.piece_ref, s32[8]{0:T(128)} %get-tuple-element.36.valid_ref, f32[8,512,128]{2,1,0:T(8,128)} %copy-done, f32[512,256]{1,0:T(8,128)} %fusion.13.factor_ref, ...), custom_call_target="tpu_custom_call" | custom-call | tf_op jit(solution)/shard_map/schur_pieces/pallas_call | solution.py:239
  155.1 10.7 %all-to-all-start.5 = ((f32[64,128,128]{2,1,0:T(8,128)}), f32[64,128,128]{2,1,0:T(8,128)}, u32[]{:S(2)}, u32[]{:S(2)}) async-start(f32[64,128,128]{2,1,0:T(8,128)} %schur_pieces.1), calls=%async_computation.5 | async-start | bytes 8388608 | tf_op jit(solution)/shard_map/all_to_all | solution.py:44
  166.7 66.4 %all-gather.10.cloned.1.call-done = f32[2048,128]{1,0:T(8,128)} async-done(((f32[256,128]{1,0:T(8,128)}), f32[2048,128]{1,0:T(8,128)}) %all-gather.10.cloned.1.call-update) | async-done | bytes 1048592 | tf_op jit(solution)/shard_map/all_gather | solution.py:412
  236.9 2.8 collective-permute-done.7
  241.9 2.5 collective-permute-done.8
  248.5 12.4 %lower_inverse.3.inverse_ref = f32[256,256]{1,0:T(8,128)} custom-call(f32[384,128]{1,0:T(8,128)} %pad_maximum_fusion.2.lower_ref), custom_call_target="tpu_custom_call" | custom-call | tf_op jit(solution)/shard_map/lower_inverse/pallas_call | solution.py:121
  260.9 9.2 %parent_base.1.base_ref = f32[1024,128]{1,0:T(8,128)} custom-call(s32[2]{0:T(128)} %pad_add_fusion.where_ref, f32[256,256]{1,0:T(8,128)} %lower_inverse.3.inverse_ref, f32[8,256,128]{2,1,0:T(8,128)} %all-gather.6.cloned.1.call-done.tops_ref, f32[256,128]{1,0:T(8,128)} %bitcast_add_fusion.top_ref, f32[1024,128]{1,0:T(8,128)} %bitcast.75), custom_call_target="tpu_custom_call" | custom-call | tf_op jit(solution)/shard_map/parent_base/pallas_call | solution.py:162
  270.1 7.7 %all-to-all-done.5.blocks_ref = f32[64,128,128]{2,1,0:T(8,128)} async-done(((f32[64,128,128]{2,1,0:T(8,128)}), f32[64,128,128]{2,1,0:T(8,128)}, u32[]{:S(2)}, u32[]{:S(2)}) %all-to-all-start.5) | async-done | bytes 4194336 | tf_op jit(solution)/shard_map/all_to_all | solution.py:44
  277.8 4.2 %place_blocks.1 = f32[1024,128]{1,0:T(8,128)} custom-call(s32[64]{0:T(128)} %select_n.239.slot_ref, f32[1024,128]{1,0:T(8,128)} %parent_base.1.base_ref, f32[64,128,128]{2,1,0:T(8,128)} %all-to-all-done.5.blocks_ref), custom_call_target="tpu_custom_call" | custom-call | tf_op jit(solution)/shard_map/place_blocks/pallas_call | solution.py:300
  (92 shorter events, 30.8 us)
Async XLA Ops:
  8.1 8.8 %collective-permute-start = (f32[256,128]{1,0:T(8,128)S(1)}, f32[256,128]{1,0:T(8,128)S(1)}, u32[]{:S(2)}, u32[]{:S(2)}) collective-permute-start(f32[256,128]{1,0:T(8,128)S(1)} %slice_bitcast_fusion), channel_id=1, source_target_pairs={{0,32},{1,33},{2,34},{3,35},{4,36},{5,37},{6,38},{7,39},{64,96},{6... | collective-permute-start | bytes 393224 | tf_op jit(solution)/shard_map/ppermute | solution.py:337
  10.6 14.6 %all-to-all-start = ((f32[8,64,256]{2,1,0:T(8,128)}), f32[8,64,256]{2,1,0:T(8,128)S(1)}, u32[]{:S(2)}, u32[]{:S(2)}) async-start(f32[8,64,256]{2,1,0:T(8,128)} %bitcast.1), calls=%async_computation | async-start | bytes 1048576 | tf_op jit(solution)/shard_map/all_to_all | solution.py:44
  25.3 4.8 %collective-permute-start.1 = (f32[256,128]{1,0:T(8,128)S(1)}, f32[256,128]{1,0:T(8,128)S(1)}, u32[]{:S(2)}, u32[]{:S(2)}) collective-permute-start(f32[256,128]{1,0:T(8,128)S(1)} %broadcast_select_fusion.7), channel_id=1, source_target_pairs={{0,16},{32,48},{1,17},{33,49},{2,18},{34,50},{3,19},{35,51},{4,20}... | collective-permute-start | bytes 393224 | tf_op jit(solution)/shard_map/ppermute | solution.py:337
  26.7 10.1 %all-to-all-start.1 = ((f32[4,64,256]{2,1,0:T(8,128)}), f32[4,64,256]{2,1,0:T(8,128)S(1)}, u32[]{:S(2)}, u32[]{:S(2)}) async-start(f32[4,64,256]{2,1,0:T(8,128)} %broadcast_in_dim.98), calls=%async_computation.1 | async-start | bytes 524288 | tf_op jit(solution)/shard_map/all_to_all | solution.py:44
  36.7 10.3 %collective-permute-start.3 = (f32[256,128]{1,0:T(8,128)S(1)}, f32[256,128]{1,0:T(8,128)S(1)}, u32[]{:S(2)}, u32[]{:S(2)}) collective-permute-start(f32[256,128]{1,0:T(8,128)S(1)} %broadcast_select_fusion.6), channel_id=1, source_target_pairs={{0,8},{16,24},{32,40},{48,56},{1,9},{17,25},{33,41},{49,57},{2,10}... | collective-permute-start | bytes 393224 | tf_op jit(solution)/shard_map/ppermute | solution.py:337
  38.0 9.1 %collective-permute-start.2 = (f32[4,64,256]{2,1,0:T(8,128)S(1)}, f32[4,64,256]{2,1,0:T(8,128)S(1)}, u32[]{:S(2)}, u32[]{:S(2)}) collective-permute-start(f32[4,64,256]{2,1,0:T(8,128)S(1)} %all-to-all-done.1), channel_id=1, source_target_pairs={{0,1},{1,0},{2,3},{3,2},{4,5},{5,4},{6,7},{7,6},{8,9},{9,8},{10,11... | collective-permute-start | bytes 786440 | tf_op jit(solution)/shard_map/ppermute | solution.py:320
  47.2 53.9 %copy-start.1 = (f32[4,2,64,256]{3,2,1,0:T(8,128)}, f32[4,2,64,256]{3,2,1,0:T(8,128)S(1)}, u32[]{:S(2)}) copy-start(f32[4,2,64,256]{3,2,1,0:T(8,128)S(1)} %pad_maximum_fusion) | copy-start | bytes 1572868
  47.2 51.8 %all-to-all-start.2 = ((f32[8,512,128]{2,1,0:T(8,128)}), f32[8,512,128]{2,1,0:T(8,128)S(1)}, u32[]{:S(2)}, u32[]{:S(2)}) async-start(f32[8,512,128]{2,1,0:T(8,128)} %pick_columns.1), calls=%async_computation.2 | async-start | bytes 4194304 | tf_op jit(solution)/shard_map/all_to_all | solution.py:44
  50.8 50.2 %all-gather.8.cloned.1.call-start = ((), (), s32[]{:S(2)}) async-start(), calls=%async_computation.7 | async-start | bytes 1179648 | tf_op jit(solution)/shard_map/all_gather | solution.py:380
  52.2 2.6 collective-permute-start.4
  54.8 1.4 collective-permute-start.5
  56.3 29.6 %collective-permute-start.6 = (f32[384,128]{1,0:T(8,128)S(1)}, f32[384,128]{1,0:T(8,128)S(1)}, u32[]{:S(2)}, u32[]{:S(2)}) collective-permute-start(f32[384,128]{1,0:T(8,128)S(1)} %broadcast_select_fusion.1), channel_id=1, source_target_pairs={{0,8},{16,24},{32,40},{48,56},{1,9},{17,25},{33,41},{49,57},{2,10}... | collective-permute-start | bytes 589832 | tf_op jit(solution)/shard_map/ppermute | solution.py:337
  99.0 45.0 %copy-start.2 = (f32[256,256]{1,0:T(8,128)S(1)}, f32[256,256]{1,0:T(8,128)}, u32[]{:S(2)}) copy-start(f32[256,256]{1,0:T(8,128)} %lower_inverse.2.inverse_ref) | copy-start | bytes 786436
  99.0 2.0 copy-start
  104.0 32.7 %all-to-all-start.3 = ((f32[64,16,128]{2,1,0:T(8,128)}), f32[64,16,128]{2,1,0:T(8,128)S(1)}, u32[]{:S(2)}, u32[]{:S(2)}) async-start(f32[64,16,128]{2,1,0:T(8,128)} %bitcast.72), calls=%async_computation.3 | async-start | bytes 1048576 | tf_op jit(solution)/shard_map/all_to_all | solution.py:44
  137.6 17.5 %all-to-all-start.4 = ((f32[8,2,16,128]{3,2,1,0:T(8,128)}), f32[8,2,16,128]{3,2,1,0:T(8,128)S(1)}, u32[]{:S(2)}, u32[]{:S(2)}) async-start(f32[8,2,16,128]{3,2,1,0:T(8,128)} %broadcast_in_dim.110), calls=%async_computation.4 | async-start | bytes 262144 | tf_op jit(solution)/shard_map/all_to_all | solution.py:44
  155.1 122.7 %all-to-all-start.5 = ((f32[64,128,128]{2,1,0:T(8,128)}), f32[64,128,128]{2,1,0:T(8,128)}, u32[]{:S(2)}, u32[]{:S(2)}) async-start(f32[64,128,128]{2,1,0:T(8,128)} %schur_pieces.1), calls=%async_computation.5 | async-start | bytes 8388608 | tf_op jit(solution)/shard_map/all_to_all | solution.py:44
  165.9 67.2 %all-gather.10.cloned.1.call-start = ((), (), s32[]{:S(2)}) async-start(), calls=%async_computation.8 | async-start | bytes 1179648 | tf_op jit(solution)/shard_map/all_gather | solution.py:412
  166.6 94.2 %all-gather.6.cloned.1.call-start = ((), (), s32[]{:S(2)}) async-start(), calls=%async_computation.6 | async-start | bytes 1179648 | tf_op jit(solution)/shard_map/all_gather | solution.py:413
  235.6 4.1 %collective-permute-start.7 = (f32[256,128]{1,0:T(8,128)S(1)}, f32[256,128]{1,0:T(8,128)S(1)}, u32[]{:S(2)}, u32[]{:S(2)}) collective-permute-start(f32[256,128]{1,0:T(8,128)S(1)} %slice.59), channel_id=1, source_target_pairs={{0,4},{1,5},{8,12},{9,13},{16,20},{17,21},{24,28},{25,29},{32,36},... | collective-permute-start | bytes 393224 | tf_op jit(solution)/shard_map/ppermute | solution.py:337
  240.6 3.8 %collective-permute-start.8 = (f32[256,128]{1,0:T(8,128)S(1)}, f32[256,128]{1,0:T(8,128)S(1)}, u32[]{:S(2)}, u32[]{:S(2)}) collective-permute-start(f32[256,128]{1,0:T(8,128)S(1)} %broadcast_select_fusion.3), channel_id=1, source_target_pairs={{0,2},{4,6},{1,3},{5,7},{8,10},{12,14},{9,11},{13,15},{16,18},{20,... | collective-permute-start | bytes 393224 | tf_op jit(solution)/shard_map/ppermute | solution.py:337
  244.4 3.2 %collective-permute-start.9 = (f32[1,256,128]{2,1,0:T(8,128)S(1)}, f32[1,256,128]{2,1,0:T(8,128)S(1)}, u32[]{:S(2)}, u32[]{:S(2)}) collective-permute-start(f32[1,256,128]{2,1,0:T(8,128)S(1)} %select_bitcast_fusion.3), channel_id=1, source_target_pairs={{0,1},{1,0},{2,3},{3,2},{4,5},{5,4},{6,7},{7,6},{8,9},{9,8},{10,11... | collective-permute-start | bytes 393224 | tf_op jit(solution)/shard_map/ppermute | solution.py:320
Sparse Core Ops, SparseCore 0:
  53.7 47.2 all-gather.7
  168.8 64.2 all-gather.9
  235.2 24.6 all-gather.5

commit v10 on v9

--- a/solution.py
+++ b/solution.py
@@ -279,20 +279,32 @@
     )(slot, live, row, cols, raw, inverse, blocks)
 
 
-def place_kernel(slot_ref, base_ref, blocks_ref, out_ref):
-    out_ref[...] = base_ref[...]
-
-    def body(item, carry):
+def place_kernel(slot_ref, base_ref, blocks_ref, out_ref, tmp_ref, sems):
+    def copy(item):
+        return pltpu.make_async_copy(blocks_ref.at[item], tmp_ref.at[item], sems.at[item])
+
+    def start(item, carry):
+        @pl.when(slot_ref[item] >= 0)
+        def _():
+            copy(item).start()
+
+        return carry
+
+    def finish(item, carry):
         slot = slot_ref[item]
 
         @pl.when(slot >= 0)
         def _():
-            start = pl.multiple_of(slot * BLOCK, BLOCK)
-            out_ref[pl.ds(start, BLOCK), :] += blocks_ref[item]
+            copy(item).wait()
+            first = pl.multiple_of(slot * BLOCK, BLOCK)
+            out_ref[pl.ds(first, BLOCK), :] += tmp_ref[item]
 
         return carry
 
-    lax.fori_loop(0, blocks_ref.shape[0], body, 0)
+    count = blocks_ref.shape[0]
+    lax.fori_loop(0, count, start, 0)
+    out_ref[...] = base_ref[...]
+    lax.fori_loop(0, count, finish, 0)
 
 
 def place_blocks(slots, base, blocks):
@@ -300,8 +312,16 @@
     return pl.pallas_call(
         place_kernel,
         out_shape=jax.ShapeDtypeStruct(base.shape, jnp.float32),
-        in_specs=[pl.BlockSpec(memory_space=pltpu.SMEM), vmem, vmem],
+        in_specs=[
+            pl.BlockSpec(memory_space=pltpu.SMEM),
+            vmem,
+            pl.BlockSpec(memory_space=pl.ANY),
+        ],
         out_specs=vmem,
+        scratch_shapes=[
+            pltpu.VMEM(blocks.shape, jnp.float32),
+            pltpu.SemaphoreType.DMA((blocks.shape[0],)),
+        ],
         name="place_blocks",
     )(slots, base, blocks)
 

time: 290 us -> 290 us (level)
  no operation moved by 1% of the time
where the time goes in v10:
time: 290 us; the launch traced here: 289 us
  waiting for transfers between devices  135 us (47%)
  starting transfers between devices  59.2 us (20%)
  Pallas kernels  55.3 us (19%)
  between operations  15.5 us (5%)
  local copies, waits for them, and re-layouts  11.5 us (4%)
  other arithmetic  9.2 us (3%)
    all_gather x1, waiting for transfers between devices, eliminate_and_assemble(): every_leaf = lax.all_gather(top, 'leaf')  66.4 us
    all_to_all x6, starting transfers between devices, exchange(): return lax.all_to_all(value, axes, split_axis=0, concat_axis=0, tiled=True)  47.4 us
    all_to_all x6, waiting for transfers between devices, exchange(): return lax.all_to_all(value, axes, split_axis=0, concat_axis=0, tiled=True)  34.5 us
    ppermute x8, waiting for transfers between devices, tree_round(): other = lax.ppermute(value, axis, pairs)  32.3 us
    pallas_call x2, Pallas kernels, lower_inverse(): pl.pallas_call(inverse_kernel, out_shape=jax.ShapeDtypeStruct((size, size...  24.8 us
    pallas_call x1, Pallas kernels, parent_base(): pl.pallas_call(parent_kernel, out_shape=jax.ShapeDtypeStruct(parent.shape...  9.23 us
    pallas_call x1, Pallas kernels, schur_pieces(): pl.pallas_call(schur_kernel, out_shape=jax.ShapeDtypeStruct((leaves * ban...  8.63 us
    ppermute x8, starting transfers between devices, tree_round(): other = lax.ppermute(value, axis, pairs)  7.84 us
  transfers between devices with their start and end apart: 19, of which 10 were waited for; matrix products, arithmetic and copies ran while one was open for 7% of the time, Pallas kernels for 17%

profile of v10, /device:TPU:216, one launch (start us, length us, event | category | flops | bytes accessed | tf_op | source)
XLA Modules:
  0.0 288.6 jit_solution(9480862882748505199)
XLA Ops:
  10.6 4.3 %all-to-all-start = ((f32[8,64,256]{2,1,0:T(8,128)}), f32[8,64,256]{2,1,0:T(8,128)S(1)}, u32[]{:S(2)}, u32[]{:S(2)}) async-start(f32[8,64,256]{2,1,0:T(8,128)} %bitcast.1), calls=%async_computation | async-start | bytes 1048576 | tf_op jit(solution)/shard_map/all_to_all | solution.py:44
  17.8 7.5 %all-to-all-done = f32[8,64,256]{2,1,0:T(8,128)S(1)} async-done(((f32[8,64,256]{2,1,0:T(8,128)}), f32[8,64,256]{2,1,0:T(8,128)S(1)}, u32[]{:S(2)}, u32[]{:S(2)}) %all-to-all-start) | async-done | bytes 524320 | tf_op jit(solution)/shard_map/all_to_all | solution.py:44
  26.7 3.4 %all-to-all-start.1 = ((f32[4,64,256]{2,1,0:T(8,128)}), f32[4,64,256]{2,1,0:T(8,128)S(1)}, u32[]{:S(2)}, u32[]{:S(2)}) async-start(f32[4,64,256]{2,1,0:T(8,128)} %broadcast_in_dim.98), calls=%async_computation.1 | async-start | bytes 524288 | tf_op jit(solution)/shard_map/all_to_all | solution.py:44
  30.1 6.6 %all-to-all-done.1 = f32[4,64,256]{2,1,0:T(8,128)S(1)} async-done(((f32[4,64,256]{2,1,0:T(8,128)}), f32[4,64,256]{2,1,0:T(8,128)S(1)}, u32[]{:S(2)}, u32[]{:S(2)}) %all-to-all-start.1) | async-done | bytes 262176 | tf_op jit(solution)/shard_map/all_to_all | solution.py:44
  38.0 1.9 collective-permute-start.2
  41.6 5.5 %pick_columns.1 = f32[8,512,128]{2,1,0:T(8,128)} custom-call(s32[8]{0:T(128)} %fusion.12.index_ref, f32[512,512]{1,0:T(8,128)} %bitcast.70), custom_call_target="tpu_custom_call" | custom-call | tf_op jit(solution)/shard_map/pick_columns/pallas_call | solution.py:178
  47.2 3.6 %all-to-all-start.2 = ((f32[8,512,128]{2,1,0:T(8,128)}), f32[8,512,128]{2,1,0:T(8,128)S(1)}, u32[]{:S(2)}, u32[]{:S(2)}) async-start(f32[8,512,128]{2,1,0:T(8,128)} %pick_columns.1), calls=%async_computation.2 | async-start | bytes 4194304 | tf_op jit(solution)/shard_map/all_to_all | solution.py:44
  58.9 27.0 %collective-permute-done.6 = f32[384,128]{1,0:T(8,128)S(1)} collective-permute-done((f32[384,128]{1,0:T(8,128)S(1)}, f32[384,128]{1,0:T(8,128)S(1)}, u32[]{:S(2)}, u32[]{:S(2)}) %collective-permute-start.6) | collective-permute-done | bytes 196640 | tf_op jit(solution)/shard_map/ppermute | solution.py:357
  86.6 12.4 %lower_inverse.2.inverse_ref = f32[256,256]{1,0:T(8,128)} custom-call(f32[384,128]{1,0:T(8,128)} %broadcast_select_fusion.2.lower_ref), custom_call_target="tpu_custom_call" | custom-call | tf_op jit(solution)/shard_map/lower_inverse/pallas_call | solution.py:121
  99.0 2.0 all-gather.8.cloned.1.call-done
  101.0 2.9 %top_pieces.1 = f32[8,128,128]{2,1,0:T(8,128)} custom-call(s32[8]{0:T(128)} %select_reduce_fusion.5.slot_ref, s32[8]{0:T(128)} %convert_element_type.9.live_ref, s32[2]{0:T(128)} %pad_add_fusion.1.row_ref, f32[8,512,128]{2,1,0:T(8,128)} %copy-done, f32[512,256]{1,0:T(8,128)} %bitcast.65, f32[256,256]{1,0:T(8,128)} %lower_inverse.2.inverse_ref, ...), custom_call_target="tpu_custom_call" | custom-call | tf_op jit(solution)/shard_map/top_pieces/pallas_call | solution.py:273
  104.0 18.9 %all-to-all-start.3 = ((f32[64,16,128]{2,1,0:T(8,128)}), f32[64,16,128]{2,1,0:T(8,128)S(1)}, u32[]{:S(2)}, u32[]{:S(2)}) async-start(f32[64,16,128]{2,1,0:T(8,128)} %bitcast.72), calls=%async_computation.3 | async-start | bytes 1048576 | tf_op jit(solution)/shard_map/all_to_all | solution.py:44
  124.0 12.7 %all-to-all-done.3 = f32[64,16,128]{2,1,0:T(8,128)S(1)} async-done(((f32[64,16,128]{2,1,0:T(8,128)}), f32[64,16,128]{2,1,0:T(8,128)S(1)}, u32[]{:S(2)}, u32[]{:S(2)}) %all-to-all-start.3) | async-done | bytes 524320 | tf_op jit(solution)/shard_map/all_to_all | solution.py:44
  137.6 6.4 %all-to-all-start.4 = ((f32[8,2,16,128]{3,2,1,0:T(8,128)}), f32[8,2,16,128]{3,2,1,0:T(8,128)S(1)}, u32[]{:S(2)}, u32[]{:S(2)}) async-start(f32[8,2,16,128]{3,2,1,0:T(8,128)} %broadcast_in_dim.110), calls=%async_computation.4 | async-start | bytes 262144 | tf_op jit(solution)/shard_map/all_to_all | solution.py:44
  144.0 2.5 fusion.13.factor_ref
  146.5 8.6 %schur_pieces.1 = f32[64,128,128]{2,1,0:T(8,128)} custom-call(s32[8]{0:T(128)} %select_reduce_fusion.5.slot_ref, s32[8]{0:T(128)} %convert_element_type.9.live_ref, s32[8]{0:T(128)} %fusion.16.piece_ref, s32[8]{0:T(128)} %get-tuple-element.36.valid_ref, f32[8,512,128]{2,1,0:T(8,128)} %copy-done, f32[512,256]{1,0:T(8,128)} %fusion.13.factor_ref, ...), custom_call_target="tpu_custom_call" | custom-call | tf_op jit(solution)/shard_map/schur_pieces/pallas_call | solution.py:239
  155.1 10.7 %all-to-all-start.5 = ((f32[64,128,128]{2,1,0:T(8,128)}), f32[64,128,128]{2,1,0:T(8,128)}, u32[]{:S(2)}, u32[]{:S(2)}) async-start(f32[64,128,128]{2,1,0:T(8,128)} %schur_pieces.1), calls=%async_computation.5 | async-start | bytes 8388608 | tf_op jit(solution)/shard_map/all_to_all | solution.py:44
  166.7 66.4 %all-gather.10.cloned.1.call-done = f32[2048,128]{1,0:T(8,128)} async-done(((f32[256,128]{1,0:T(8,128)}), f32[2048,128]{1,0:T(8,128)}) %all-gather.10.cloned.1.call-update) | async-done | bytes 1048592 | tf_op jit(solution)/shard_map/all_gather | solution.py:432
  236.9 2.8 collective-permute-done.7
  241.9 2.5 collective-permute-done.8
  248.5 12.4 %lower_inverse.3.inverse_ref = f32[256,256]{1,0:T(8,128)} custom-call(f32[384,128]{1,0:T(8,128)} %pad_maximum_fusion.2.lower_ref), custom_call_target="tpu_custom_call" | custom-call | tf_op jit(solution)/shard_map/lower_inverse/pallas_call | solution.py:121
  260.9 9.2 %parent_base.1.base_ref = f32[1024,128]{1,0:T(8,128)} custom-call(s32[2]{0:T(128)} %pad_add_fusion.where_ref, f32[256,256]{1,0:T(8,128)} %lower_inverse.3.inverse_ref, f32[8,256,128]{2,1,0:T(8,128)} %all-gather.6.cloned.1.call-done.tops_ref, f32[256,128]{1,0:T(8,128)} %bitcast_add_fusion.top_ref, f32[1024,128]{1,0:T(8,128)} %bitcast.75), custom_call_target="tpu_custom_call" | custom-call | tf_op jit(solution)/shard_map/parent_base/pallas_call | solution.py:162
  270.1 7.7 %all-to-all-done.5.blocks_ref = f32[64,128,128]{2,1,0:T(8,128)} async-done(((f32[64,128,128]{2,1,0:T(8,128)}), f32[64,128,128]{2,1,0:T(8,128)}, u32[]{:S(2)}, u32[]{:S(2)}) %all-to-all-start.5) | async-done | bytes 4194336 | tf_op jit(solution)/shard_map/all_to_all | solution.py:44
  277.8 4.2 %place_blocks.1 = f32[1024,128]{1,0:T(8,128)} custom-call(s32[64]{0:T(128)} %select_n.239.slot_ref, f32[1024,128]{1,0:T(8,128)} %parent_base.1.base_ref, f32[64,128,128]{2,1,0:T(8,128)} %all-to-all-done.5.blocks_ref), custom_call_target="tpu_custom_call" | custom-call | tf_op jit(solution)/shard_map/place_blocks/pallas_call | solution.py:312
  (92 shorter events, 30.8 us)
Async XLA Ops:
  8.1 8.8 %collective-permute-start = (f32[256,128]{1,0:T(8,128)S(1)}, f32[256,128]{1,0:T(8,128)S(1)}, u32[]{:S(2)}, u32[]{:S(2)}) collective-permute-start(f32[256,128]{1,0:T(8,128)S(1)} %slice_bitcast_fusion), channel_id=1, source_target_pairs={{0,32},{1,33},{2,34},{3,35},{4,36},{5,37},{6,38},{7,39},{64,96},{6... | collective-permute-start | bytes 393224 | tf_op jit(solution)/shard_map/ppermute | solution.py:357
  10.6 14.6 %all-to-all-start = ((f32[8,64,256]{2,1,0:T(8,128)}), f32[8,64,256]{2,1,0:T(8,128)S(1)}, u32[]{:S(2)}, u32[]{:S(2)}) async-start(f32[8,64,256]{2,1,0:T(8,128)} %bitcast.1), calls=%async_computation | async-start | bytes 1048576 | tf_op jit(solution)/shard_map/all_to_all | solution.py:44
  25.3 4.8 %collective-permute-start.1 = (f32[256,128]{1,0:T(8,128)S(1)}, f32[256,128]{1,0:T(8,128)S(1)}, u32[]{:S(2)}, u32[]{:S(2)}) collective-permute-start(f32[256,128]{1,0:T(8,128)S(1)} %broadcast_select_fusion.7), channel_id=1, source_target_pairs={{0,16},{32,48},{1,17},{33,49},{2,18},{34,50},{3,19},{35,51},{4,20}... | collective-permute-start | bytes 393224 | tf_op jit(solution)/shard_map/ppermute | solution.py:357
  26.7 10.1 %all-to-all-start.1 = ((f32[4,64,256]{2,1,0:T(8,128)}), f32[4,64,256]{2,1,0:T(8,128)S(1)}, u32[]{:S(2)}, u32[]{:S(2)}) async-start(f32[4,64,256]{2,1,0:T(8,128)} %broadcast_in_dim.98), calls=%async_computation.1 | async-start | bytes 524288 | tf_op jit(solution)/shard_map/all_to_all | solution.py:44
  36.7 10.3 %collective-permute-start.3 = (f32[256,128]{1,0:T(8,128)S(1)}, f32[256,128]{1,0:T(8,128)S(1)}, u32[]{:S(2)}, u32[]{:S(2)}) collective-permute-start(f32[256,128]{1,0:T(8,128)S(1)} %broadcast_select_fusion.6), channel_id=1, source_target_pairs={{0,8},{16,24},{32,40},{48,56},{1,9},{17,25},{33,41},{49,57},{2,10}... | collective-permute-start | bytes 393224 | tf_op jit(solution)/shard_map/ppermute | solution.py:357
  38.0 9.1 %collective-permute-start.2 = (f32[4,64,256]{2,1,0:T(8,128)S(1)}, f32[4,64,256]{2,1,0:T(8,128)S(1)}, u32[]{:S(2)}, u32[]{:S(2)}) collective-permute-start(f32[4,64,256]{2,1,0:T(8,128)S(1)} %all-to-all-done.1), channel_id=1, source_target_pairs={{0,1},{1,0},{2,3},{3,2},{4,5},{5,4},{6,7},{7,6},{8,9},{9,8},{10,11... | collective-permute-start | bytes 786440 | tf_op jit(solution)/shard_map/ppermute | solution.py:340
  47.2 53.9 %copy-start.1 = (f32[4,2,64,256]{3,2,1,0:T(8,128)}, f32[4,2,64,256]{3,2,1,0:T(8,128)S(1)}, u32[]{:S(2)}) copy-start(f32[4,2,64,256]{3,2,1,0:T(8,128)S(1)} %pad_maximum_fusion) | copy-start | bytes 1572868
  47.2 51.8 %all-to-all-start.2 = ((f32[8,512,128]{2,1,0:T(8,128)}), f32[8,512,128]{2,1,0:T(8,128)S(1)}, u32[]{:S(2)}, u32[]{:S(2)}) async-start(f32[8,512,128]{2,1,0:T(8,128)} %pick_columns.1), calls=%async_computation.2 | async-start | bytes 4194304 | tf_op jit(solution)/shard_map/all_to_all | solution.py:44
  50.8 50.2 %all-gather.8.cloned.1.call-start = ((), (), s32[]{:S(2)}) async-start(), calls=%async_computation.7 | async-start | bytes 1179648 | tf_op jit(solution)/shard_map/all_gather | solution.py:400
  52.2 2.6 collective-permute-start.4
  54.8 1.4 collective-permute-start.5
  56.3 29.6 %collective-permute-start.6 = (f32[384,128]{1,0:T(8,128)S(1)}, f32[384,128]{1,0:T(8,128)S(1)}, u32[]{:S(2)}, u32[]{:S(2)}) collective-permute-start(f32[384,128]{1,0:T(8,128)S(1)} %broadcast_select_fusion.1), channel_id=1, source_target_pairs={{0,8},{16,24},{32,40},{48,56},{1,9},{17,25},{33,41},{49,57},{2,10}... | collective-permute-start | bytes 589832 | tf_op jit(solution)/shard_map/ppermute | solution.py:357
  99.0 45.0 %copy-start.2 = (f32[256,256]{1,0:T(8,128)S(1)}, f32[256,256]{1,0:T(8,128)}, u32[]{:S(2)}) copy-start(f32[256,256]{1,0:T(8,128)} %lower_inverse.2.inverse_ref) | copy-start | bytes 786436
  99.0 2.0 copy-start
  104.0 32.7 %all-to-all-start.3 = ((f32[64,16,128]{2,1,0:T(8,128)}), f32[64,16,128]{2,1,0:T(8,128)S(1)}, u32[]{:S(2)}, u32[]{:S(2)}) async-start(f32[64,16,128]{2,1,0:T(8,128)} %bitcast.72), calls=%async_computation.3 | async-start | bytes 1048576 | tf_op jit(solution)/shard_map/all_to_all | solution.py:44
  137.6 17.5 %all-to-all-start.4 = ((f32[8,2,16,128]{3,2,1,0:T(8,128)}), f32[8,2,16,128]{3,2,1,0:T(8,128)S(1)}, u32[]{:S(2)}, u32[]{:S(2)}) async-start(f32[8,2,16,128]{3,2,1,0:T(8,128)} %broadcast_in_dim.110), calls=%async_computation.4 | async-start | bytes 262144 | tf_op jit(solution)/shard_map/all_to_all | solution.py:44
  155.1 122.7 %all-to-all-start.5 = ((f32[64,128,128]{2,1,0:T(8,128)}), f32[64,128,128]{2,1,0:T(8,128)}, u32[]{:S(2)}, u32[]{:S(2)}) async-start(f32[64,128,128]{2,1,0:T(8,128)} %schur_pieces.1), calls=%async_computation.5 | async-start | bytes 8388608 | tf_op jit(solution)/shard_map/all_to_all | solution.py:44
  165.9 67.2 %all-gather.10.cloned.1.call-start = ((), (), s32[]{:S(2)}) async-start(), calls=%async_computation.8 | async-start | bytes 1179648 | tf_op jit(solution)/shard_map/all_gather | solution.py:432
  166.6 94.2 %all-gather.6.cloned.1.call-start = ((), (), s32[]{:S(2)}) async-start(), calls=%async_computation.6 | async-start | bytes 1179648 | tf_op jit(solution)/shard_map/all_gather | solution.py:433
  235.6 4.1 %collective-permute-start.7 = (f32[256,128]{1,0:T(8,128)S(1)}, f32[256,128]{1,0:T(8,128)S(1)}, u32[]{:S(2)}, u32[]{:S(2)}) collective-permute-start(f32[256,128]{1,0:T(8,128)S(1)} %slice.59), channel_id=1, source_target_pairs={{0,4},{1,5},{8,12},{9,13},{16,20},{17,21},{24,28},{25,29},{32,36},... | collective-permute-start | bytes 393224 | tf_op jit(solution)/shard_map/ppermute | solution.py:357
  240.6 3.8 %collective-permute-start.8 = (f32[256,128]{1,0:T(8,128)S(1)}, f32[256,128]{1,0:T(8,128)S(1)}, u32[]{:S(2)}, u32[]{:S(2)}) collective-permute-start(f32[256,128]{1,0:T(8,128)S(1)} %broadcast_select_fusion.3), channel_id=1, source_target_pairs={{0,2},{4,6},{1,3},{5,7},{8,10},{12,14},{9,11},{13,15},{16,18},{20,... | collective-permute-start | bytes 393224 | tf_op jit(solution)/shard_map/ppermute | solution.py:357
  244.4 3.2 %collective-permute-start.9 = (f32[1,256,128]{2,1,0:T(8,128)S(1)}, f32[1,256,128]{2,1,0:T(8,128)S(1)}, u32[]{:S(2)}, u32[]{:S(2)}) collective-permute-start(f32[1,256,128]{2,1,0:T(8,128)S(1)} %select_bitcast_fusion.3), channel_id=1, source_target_pairs={{0,1},{1,0},{2,3},{3,2},{4,5},{5,4},{6,7},{7,6},{8,9},{9,8},{10,11... | collective-permute-start | bytes 393224 | tf_op jit(solution)/shard_map/ppermute | solution.py:340
Sparse Core Ops, SparseCore 0:
  53.7 47.2 all-gather.7
  168.8 64.2 all-gather.9
  235.2 24.6 all-gather.5

commit v11 on v10

--- a/solution.py
+++ b/solution.py
@@ -12,12 +12,13 @@
 LEAF_COL = ("leaf", "col_0", "col_1")
 LEAF_ROW = ("leaf", "row")
 HIGHEST = lax.Precision.HIGHEST
+HIGH = lax.Precision.HIGH
 STEP = 64
 GROUP = 8
 
 
-def matmul(left, right):
-    return jnp.dot(left, right, precision=HIGHEST, preferred_element_type=jnp.float32)
+def matmul(left, right, precision=HIGHEST):
+    return jnp.dot(left, right, precision=precision, preferred_element_type=jnp.float32)
 
 
 def matmul_nt(left, right):
@@ -30,12 +31,12 @@
     )
 
 
-def matmul_tn(left, right):
+def matmul_tn(left, right, precision=HIGHEST):
     return lax.dot_general(
         left,
         right,
         (((0,), (0,)), ((), ())),
-        precision=HIGHEST,
+        precision=precision,
         preferred_element_type=jnp.float32,
     )
 
@@ -137,7 +138,8 @@
 
         def body(block, carry):
             part = pl.ds(pl.multiple_of(block * BLOCK, BLOCK), BLOCK)
-            change = matmul_tn(matmul(inverse_ref[...], tops_ref[block]), upper)
+            factor = matmul(inverse_ref[...], tops_ref[block], HIGH)
+            change = matmul_tn(factor, upper, HIGH)
             first = (row_id == 0) & (block < lead)
             out_ref[part, :] = parent_ref[part, :] - jnp.where(first, 0.0, change)
             return carry

time: 290 us -> 290 us (level)
  transfers between devices with their start and end apart: 19 -> 19, of which waited for: 10 -> 10; matrix products, arithmetic and copies ran while one was open for 7% -> 7% of each run, Pallas kernels for 17% -> 16%
where the time goes in v11:
time: 290 us; the launch traced here: 289 us
  waiting for transfers between devices  137 us (47%)
  starting transfers between devices  59.2 us (20%)
  Pallas kernels  53.4 us (18%)
  between operations  15.5 us (5%)
  local copies, waits for them, and re-layouts  11.5 us (4%)
  other arithmetic  9.2 us (3%)
    all_gather x1, waiting for transfers between devices, eliminate_and_assemble(): every_leaf = lax.all_gather(top, 'leaf')  66.4 us
    all_to_all x6, starting transfers between devices, exchange(): return lax.all_to_all(value, axes, split_axis=0, concat_axis=0, tiled=True)  47.4 us
    all_to_all x6, waiting for transfers between devices, exchange(): return lax.all_to_all(value, axes, split_axis=0, concat_axis=0, tiled=True)  36.3 us
    ppermute x8, waiting for transfers between devices, tree_round(): other = lax.ppermute(value, axis, pairs)  32.3 us
    pallas_call x2, Pallas kernels, lower_inverse(): pl.pallas_call(inverse_kernel, out_shape=jax.ShapeDtypeStruct((size, size...  24.8 us
    pallas_call x1, Pallas kernels, schur_pieces(): pl.pallas_call(schur_kernel, out_shape=jax.ShapeDtypeStruct((leaves * ban...  8.63 us
    ppermute x8, starting transfers between devices, tree_round(): other = lax.ppermute(value, axis, pairs)  7.84 us
    pallas_call x1, Pallas kernels, parent_base(): pl.pallas_call(parent_kernel, out_shape=jax.ShapeDtypeStruct(parent.shape...  7.38 us
  transfers between devices with their start and end apart: 19, of which 10 were waited for; matrix products, arithmetic and copies ran while one was open for 7% of the time, Pallas kernels for 16%

profile of v11, /device:TPU:216, one launch (start us, length us, event | category | flops | bytes accessed | tf_op | source)
XLA Modules:
  0.0 288.6 jit_solution(6300662293885820854)
XLA Ops:
  10.6 4.3 %all-to-all-start = ((f32[8,64,256]{2,1,0:T(8,128)}), f32[8,64,256]{2,1,0:T(8,128)S(1)}, u32[]{:S(2)}, u32[]{:S(2)}) async-start(f32[8,64,256]{2,1,0:T(8,128)} %bitcast.1), calls=%async_computation | async-start | bytes 1048576 | tf_op jit(solution)/shard_map/all_to_all | solution.py:45
  17.8 7.5 %all-to-all-done = f32[8,64,256]{2,1,0:T(8,128)S(1)} async-done(((f32[8,64,256]{2,1,0:T(8,128)}), f32[8,64,256]{2,1,0:T(8,128)S(1)}, u32[]{:S(2)}, u32[]{:S(2)}) %all-to-all-start) | async-done | bytes 524320 | tf_op jit(solution)/shard_map/all_to_all | solution.py:45
  26.7 3.4 %all-to-all-start.1 = ((f32[4,64,256]{2,1,0:T(8,128)}), f32[4,64,256]{2,1,0:T(8,128)S(1)}, u32[]{:S(2)}, u32[]{:S(2)}) async-start(f32[4,64,256]{2,1,0:T(8,128)} %broadcast_in_dim.98), calls=%async_computation.1 | async-start | bytes 524288 | tf_op jit(solution)/shard_map/all_to_all | solution.py:45
  30.1 6.6 %all-to-all-done.1 = f32[4,64,256]{2,1,0:T(8,128)S(1)} async-done(((f32[4,64,256]{2,1,0:T(8,128)}), f32[4,64,256]{2,1,0:T(8,128)S(1)}, u32[]{:S(2)}, u32[]{:S(2)}) %all-to-all-start.1) | async-done | bytes 262176 | tf_op jit(solution)/shard_map/all_to_all | solution.py:45
  38.0 1.9 collective-permute-start.2
  41.6 5.5 %pick_columns.1 = f32[8,512,128]{2,1,0:T(8,128)} custom-call(s32[8]{0:T(128)} %fusion.12.index_ref, f32[512,512]{1,0:T(8,128)} %bitcast.70), custom_call_target="tpu_custom_call" | custom-call | tf_op jit(solution)/shard_map/pick_columns/pallas_call | solution.py:180
  47.2 3.6 %all-to-all-start.2 = ((f32[8,512,128]{2,1,0:T(8,128)}), f32[8,512,128]{2,1,0:T(8,128)S(1)}, u32[]{:S(2)}, u32[]{:S(2)}) async-start(f32[8,512,128]{2,1,0:T(8,128)} %pick_columns.1), calls=%async_computation.2 | async-start | bytes 4194304 | tf_op jit(solution)/shard_map/all_to_all | solution.py:45
  58.9 27.0 %collective-permute-done.6 = f32[384,128]{1,0:T(8,128)S(1)} collective-permute-done((f32[384,128]{1,0:T(8,128)S(1)}, f32[384,128]{1,0:T(8,128)S(1)}, u32[]{:S(2)}, u32[]{:S(2)}) %collective-permute-start.6) | collective-permute-done | bytes 196640 | tf_op jit(solution)/shard_map/ppermute | solution.py:359
  86.6 12.4 %lower_inverse.2.inverse_ref = f32[256,256]{1,0:T(8,128)} custom-call(f32[384,128]{1,0:T(8,128)} %broadcast_select_fusion.2.lower_ref), custom_call_target="tpu_custom_call" | custom-call | tf_op jit(solution)/shard_map/lower_inverse/pallas_call | solution.py:122
  99.0 2.0 all-gather.8.cloned.1.call-done
  101.0 2.9 %top_pieces.1 = f32[8,128,128]{2,1,0:T(8,128)} custom-call(s32[8]{0:T(128)} %select_reduce_fusion.5.slot_ref, s32[8]{0:T(128)} %convert_element_type.9.live_ref, s32[2]{0:T(128)} %pad_add_fusion.1.row_ref, f32[8,512,128]{2,1,0:T(8,128)} %copy-done, f32[512,256]{1,0:T(8,128)} %bitcast.65, f32[256,256]{1,0:T(8,128)} %lower_inverse.2.inverse_ref, ...), custom_call_target="tpu_custom_call" | custom-call | tf_op jit(solution)/shard_map/top_pieces/pallas_call | solution.py:275
  104.0 18.9 %all-to-all-start.3 = ((f32[64,16,128]{2,1,0:T(8,128)}), f32[64,16,128]{2,1,0:T(8,128)S(1)}, u32[]{:S(2)}, u32[]{:S(2)}) async-start(f32[64,16,128]{2,1,0:T(8,128)} %bitcast.72), calls=%async_computation.3 | async-start | bytes 1048576 | tf_op jit(solution)/shard_map/all_to_all | solution.py:45
  124.0 12.7 %all-to-all-done.3 = f32[64,16,128]{2,1,0:T(8,128)S(1)} async-done(((f32[64,16,128]{2,1,0:T(8,128)}), f32[64,16,128]{2,1,0:T(8,128)S(1)}, u32[]{:S(2)}, u32[]{:S(2)}) %all-to-all-start.3) | async-done | bytes 524320 | tf_op jit(solution)/shard_map/all_to_all | solution.py:45
  137.6 6.4 %all-to-all-start.4 = ((f32[8,2,16,128]{3,2,1,0:T(8,128)}), f32[8,2,16,128]{3,2,1,0:T(8,128)S(1)}, u32[]{:S(2)}, u32[]{:S(2)}) async-start(f32[8,2,16,128]{3,2,1,0:T(8,128)} %broadcast_in_dim.110), calls=%async_computation.4 | async-start | bytes 262144 | tf_op jit(solution)/shard_map/all_to_all | solution.py:45
  144.0 2.5 fusion.13.factor_ref
  146.5 8.6 %schur_pieces.1 = f32[64,128,128]{2,1,0:T(8,128)} custom-call(s32[8]{0:T(128)} %select_reduce_fusion.5.slot_ref, s32[8]{0:T(128)} %convert_element_type.9.live_ref, s32[8]{0:T(128)} %fusion.16.piece_ref, s32[8]{0:T(128)} %get-tuple-element.36.valid_ref, f32[8,512,128]{2,1,0:T(8,128)} %copy-done, f32[512,256]{1,0:T(8,128)} %fusion.13.factor_ref, ...), custom_call_target="tpu_custom_call" | custom-call | tf_op jit(solution)/shard_map/schur_pieces/pallas_call | solution.py:241
  155.1 10.7 %all-to-all-start.5 = ((f32[64,128,128]{2,1,0:T(8,128)}), f32[64,128,128]{2,1,0:T(8,128)}, u32[]{:S(2)}, u32[]{:S(2)}) async-start(f32[64,128,128]{2,1,0:T(8,128)} %schur_pieces.1), calls=%async_computation.5 | async-start | bytes 8388608 | tf_op jit(solution)/shard_map/all_to_all | solution.py:45
  166.7 66.4 %all-gather.10.cloned.1.call-done = f32[2048,128]{1,0:T(8,128)} async-done(((f32[256,128]{1,0:T(8,128)}), f32[2048,128]{1,0:T(8,128)}) %all-gather.10.cloned.1.call-update) | async-done | bytes 1048592 | tf_op jit(solution)/shard_map/all_gather | solution.py:434
  236.9 2.8 collective-permute-done.7
  241.9 2.5 collective-permute-done.8
  248.5 12.4 %lower_inverse.3.inverse_ref = f32[256,256]{1,0:T(8,128)} custom-call(f32[384,128]{1,0:T(8,128)} %pad_maximum_fusion.2.lower_ref), custom_call_target="tpu_custom_call" | custom-call | tf_op jit(solution)/shard_map/lower_inverse/pallas_call | solution.py:122
  260.9 7.4 %parent_base.1.base_ref = f32[1024,128]{1,0:T(8,128)} custom-call(s32[2]{0:T(128)} %pad_add_fusion.where_ref, f32[256,256]{1,0:T(8,128)} %lower_inverse.3.inverse_ref, f32[8,256,128]{2,1,0:T(8,128)} %all-gather.6.cloned.1.call-done.tops_ref, f32[256,128]{1,0:T(8,128)} %bitcast_add_fusion.top_ref, f32[1024,128]{1,0:T(8,128)} %bitcast.75), custom_call_target="tpu_custom_call" | custom-call | tf_op jit(solution)/shard_map/parent_base/pallas_call | solution.py:164
  268.2 9.6 %all-to-all-done.5.blocks_ref = f32[64,128,128]{2,1,0:T(8,128)} async-done(((f32[64,128,128]{2,1,0:T(8,128)}), f32[64,128,128]{2,1,0:T(8,128)}, u32[]{:S(2)}, u32[]{:S(2)}) %all-to-all-start.5) | async-done | bytes 4194336 | tf_op jit(solution)/shard_map/all_to_all | solution.py:45
  277.8 4.2 %place_blocks.1 = f32[1024,128]{1,0:T(8,128)} custom-call(s32[64]{0:T(128)} %select_n.239.slot_ref, f32[1024,128]{1,0:T(8,128)} %parent_base.1.base_ref, f32[64,128,128]{2,1,0:T(8,128)} %all-to-all-done.5.blocks_ref), custom_call_target="tpu_custom_call" | custom-call | tf_op jit(solution)/shard_map/place_blocks/pallas_call | solution.py:314
  (92 shorter events, 30.8 us)
Async XLA Ops:
  8.1 8.8 %collective-permute-start = (f32[256,128]{1,0:T(8,128)S(1)}, f32[256,128]{1,0:T(8,128)S(1)}, u32[]{:S(2)}, u32[]{:S(2)}) collective-permute-start(f32[256,128]{1,0:T(8,128)S(1)} %slice_bitcast_fusion), channel_id=1, source_target_pairs={{0,32},{1,33},{2,34},{3,35},{4,36},{5,37},{6,38},{7,39},{64,96},{6... | collective-permute-start | bytes 393224 | tf_op jit(solution)/shard_map/ppermute | solution.py:359
  10.6 14.6 %all-to-all-start = ((f32[8,64,256]{2,1,0:T(8,128)}), f32[8,64,256]{2,1,0:T(8,128)S(1)}, u32[]{:S(2)}, u32[]{:S(2)}) async-start(f32[8,64,256]{2,1,0:T(8,128)} %bitcast.1), calls=%async_computation | async-start | bytes 1048576 | tf_op jit(solution)/shard_map/all_to_all | solution.py:45
  25.3 4.8 %collective-permute-start.1 = (f32[256,128]{1,0:T(8,128)S(1)}, f32[256,128]{1,0:T(8,128)S(1)}, u32[]{:S(2)}, u32[]{:S(2)}) collective-permute-start(f32[256,128]{1,0:T(8,128)S(1)} %broadcast_select_fusion.7), channel_id=1, source_target_pairs={{0,16},{32,48},{1,17},{33,49},{2,18},{34,50},{3,19},{35,51},{4,20}... | collective-permute-start | bytes 393224 | tf_op jit(solution)/shard_map/ppermute | solution.py:359
  26.7 10.1 %all-to-all-start.1 = ((f32[4,64,256]{2,1,0:T(8,128)}), f32[4,64,256]{2,1,0:T(8,128)S(1)}, u32[]{:S(2)}, u32[]{:S(2)}) async-start(f32[4,64,256]{2,1,0:T(8,128)} %broadcast_in_dim.98), calls=%async_computation.1 | async-start | bytes 524288 | tf_op jit(solution)/shard_map/all_to_all | solution.py:45
  36.7 10.3 %collective-permute-start.3 = (f32[256,128]{1,0:T(8,128)S(1)}, f32[256,128]{1,0:T(8,128)S(1)}, u32[]{:S(2)}, u32[]{:S(2)}) collective-permute-start(f32[256,128]{1,0:T(8,128)S(1)} %broadcast_select_fusion.6), channel_id=1, source_target_pairs={{0,8},{16,24},{32,40},{48,56},{1,9},{17,25},{33,41},{49,57},{2,10}... | collective-permute-start | bytes 393224 | tf_op jit(solution)/shard_map/ppermute | solution.py:359
  38.0 9.1 %collective-permute-start.2 = (f32[4,64,256]{2,1,0:T(8,128)S(1)}, f32[4,64,256]{2,1,0:T(8,128)S(1)}, u32[]{:S(2)}, u32[]{:S(2)}) collective-permute-start(f32[4,64,256]{2,1,0:T(8,128)S(1)} %all-to-all-done.1), channel_id=1, source_target_pairs={{0,1},{1,0},{2,3},{3,2},{4,5},{5,4},{6,7},{7,6},{8,9},{9,8},{10,11... | collective-permute-start | bytes 786440 | tf_op jit(solution)/shard_map/ppermute | solution.py:342
  47.2 53.9 %copy-start.1 = (f32[4,2,64,256]{3,2,1,0:T(8,128)}, f32[4,2,64,256]{3,2,1,0:T(8,128)S(1)}, u32[]{:S(2)}) copy-start(f32[4,2,64,256]{3,2,1,0:T(8,128)S(1)} %pad_maximum_fusion) | copy-start | bytes 1572868
  47.2 51.8 %all-to-all-start.2 = ((f32[8,512,128]{2,1,0:T(8,128)}), f32[8,512,128]{2,1,0:T(8,128)S(1)}, u32[]{:S(2)}, u32[]{:S(2)}) async-start(f32[8,512,128]{2,1,0:T(8,128)} %pick_columns.1), calls=%async_computation.2 | async-start | bytes 4194304 | tf_op jit(solution)/shard_map/all_to_all | solution.py:45
  50.8 50.2 %all-gather.8.cloned.1.call-start = ((), (), s32[]{:S(2)}) async-start(), calls=%async_computation.7 | async-start | bytes 1179648 | tf_op jit(solution)/shard_map/all_gather | solution.py:402
  52.2 2.6 collective-permute-start.4
  54.8 1.4 collective-permute-start.5
  56.3 29.6 %collective-permute-start.6 = (f32[384,128]{1,0:T(8,128)S(1)}, f32[384,128]{1,0:T(8,128)S(1)}, u32[]{:S(2)}, u32[]{:S(2)}) collective-permute-start(f32[384,128]{1,0:T(8,128)S(1)} %broadcast_select_fusion.1), channel_id=1, source_target_pairs={{0,8},{16,24},{32,40},{48,56},{1,9},{17,25},{33,41},{49,57},{2,10}... | collective-permute-start | bytes 589832 | tf_op jit(solution)/shard_map/ppermute | solution.py:359
  99.0 45.0 %copy-start.2 = (f32[256,256]{1,0:T(8,128)S(1)}, f32[256,256]{1,0:T(8,128)}, u32[]{:S(2)}) copy-start(f32[256,256]{1,0:T(8,128)} %lower_inverse.2.inverse_ref) | copy-start | bytes 786436
  99.0 2.0 copy-start
  104.0 32.7 %all-to-all-start.3 = ((f32[64,16,128]{2,1,0:T(8,128)}), f32[64,16,128]{2,1,0:T(8,128)S(1)}, u32[]{:S(2)}, u32[]{:S(2)}) async-start(f32[64,16,128]{2,1,0:T(8,128)} %bitcast.72), calls=%async_computation.3 | async-start | bytes 1048576 | tf_op jit(solution)/shard_map/all_to_all | solution.py:45
  137.6 17.5 %all-to-all-start.4 = ((f32[8,2,16,128]{3,2,1,0:T(8,128)}), f32[8,2,16,128]{3,2,1,0:T(8,128)S(1)}, u32[]{:S(2)}, u32[]{:S(2)}) async-start(f32[8,2,16,128]{3,2,1,0:T(8,128)} %broadcast_in_dim.110), calls=%async_computation.4 | async-start | bytes 262144 | tf_op jit(solution)/shard_map/all_to_all | solution.py:45
  155.1 122.7 %all-to-all-start.5 = ((f32[64,128,128]{2,1,0:T(8,128)}), f32[64,128,128]{2,1,0:T(8,128)}, u32[]{:S(2)}, u32[]{:S(2)}) async-start(f32[64,128,128]{2,1,0:T(8,128)} %schur_pieces.1), calls=%async_computation.5 | async-start | bytes 8388608 | tf_op jit(solution)/shard_map/all_to_all | solution.py:45
  165.9 67.2 %all-gather.10.cloned.1.call-start = ((), (), s32[]{:S(2)}) async-start(), calls=%async_computation.8 | async-start | bytes 1179648 | tf_op jit(solution)/shard_map/all_gather | solution.py:434
  166.6 94.2 %all-gather.6.cloned.1.call-start = ((), (), s32[]{:S(2)}) async-start(), calls=%async_computation.6 | async-start | bytes 1179648 | tf_op jit(solution)/shard_map/all_gather | solution.py:435
  235.6 4.1 %collective-permute-start.7 = (f32[256,128]{1,0:T(8,128)S(1)}, f32[256,128]{1,0:T(8,128)S(1)}, u32[]{:S(2)}, u32[]{:S(2)}) collective-permute-start(f32[256,128]{1,0:T(8,128)S(1)} %slice.59), channel_id=1, source_target_pairs={{0,4},{1,5},{8,12},{9,13},{16,20},{17,21},{24,28},{25,29},{32,36},... | collective-permute-start | bytes 393224 | tf_op jit(solution)/shard_map/ppermute | solution.py:359
  240.6 3.8 %collective-permute-start.8 = (f32[256,128]{1,0:T(8,128)S(1)}, f32[256,128]{1,0:T(8,128)S(1)}, u32[]{:S(2)}, u32[]{:S(2)}) collective-permute-start(f32[256,128]{1,0:T(8,128)S(1)} %broadcast_select_fusion.3), channel_id=1, source_target_pairs={{0,2},{4,6},{1,3},{5,7},{8,10},{12,14},{9,11},{13,15},{16,18},{20,... | collective-permute-start | bytes 393224 | tf_op jit(solution)/shard_map/ppermute | solution.py:359
  244.4 3.2 %collective-permute-start.9 = (f32[1,256,128]{2,1,0:T(8,128)S(1)}, f32[1,256,128]{2,1,0:T(8,128)S(1)}, u32[]{:S(2)}, u32[]{:S(2)}) collective-permute-start(f32[1,256,128]{2,1,0:T(8,128)S(1)} %select_bitcast_fusion.3), channel_id=1, source_target_pairs={{0,1},{1,0},{2,3},{3,2},{4,5},{5,4},{6,7},{7,6},{8,9},{9,8},{10,11... | collective-permute-start | bytes 393224 | tf_op jit(solution)/shard_map/ppermute | solution.py:342
Sparse Core Ops, SparseCore 0:
  53.7 47.2 all-gather.7
  168.8 64.2 all-gather.9
  235.2 24.6 all-gather.5
